TPU v7x, 32 devices: a whole 2x2x4 slice. The times are simulated.
32 devices in a mesh: dp: 8 (over z, y), proto: 4 (over x, core).
Axes of the slice: x: 2, y: 2, z: 4, core: 2. Of those that a mesh axis runs over, the one named last changes fastest.
Arguments:
- teacher_feat: bfloat16 [1024, 128], P('dp'), may hold values from -32 to 32
- student_feat: bfloat16 [1024, 128], P('dp'), may hold values from -32 to 32
- proto_weight: bfloat16 [128, 32768], P(None, 'proto'), may hold values from -0.5 to 0.5
Outputs:
- proto_grad: float32 [128, 32768], P('dp', 'proto')
- feature_grad: float32 [1024, 128], P('dp')
All inputs are finite; a program needn't handle non-finite values.
Results may differ from a plain program's by a relative error of at most 0.0028.
Values sent between devices are 32-bit elements; how exact they have to be, the bound alone decides.
No kernel may reach another device: no remote copies, remote signals or barrier semaphores. Data moves between devices by JAX's collectives and lax.ppermute only.
A program may use at most 64 MiB of HBM per device.

v0:
```python
import jax
import jax.numpy as jnp
from jax import lax
from jax.sharding import PartitionSpec as P

ITERS = 3


teacher_temp = 0.07
student_temp = 0.1


def combined_all(value, axis, combine):
    everything = jax.tree.map(lambda part: lax.all_gather(part, axis), value)
    leading = jax.tree.map(lambda part: part[0], everything)

    def step(k, so_far):
        return combine(so_far, jax.tree.map(lambda part: part[k], everything))

    return lax.fori_loop(1, lax.axis_size(axis), step, leading)


def divided_logits(feature_vector_count, cluster_center_matrix, logit_sharpness_divisor):
    return (
        jnp.dot(feature_vector_count, cluster_center_matrix, preferred_element_type=jnp.float32)
        / logit_sharpness_divisor
    )


def combine_stats(earlier, later):
    teacher_peak = jnp.maximum(earlier[0], later[0])
    student_peak = jnp.maximum(earlier[1], later[1])
    merged_total = earlier[2] * jnp.exp(earlier[1] - student_peak) + later[2] * jnp.exp(
        later[1] - student_peak
    )
    return (teacher_peak, student_peak, merged_total)


def shards(teacher_feat, student_feat, proto_weight):
    teacher_scores = divided_logits(teacher_feat, proto_weight, teacher_temp)
    student_scores = divided_logits(student_feat, proto_weight, student_temp)
    local_teacher = jnp.max(teacher_scores, axis=1)
    local_student = jnp.max(student_scores, axis=1)
    local_total = jnp.sum(jnp.exp(student_scores - local_student[:, None]), axis=1)
    teacher_peak, student_peak, student_total = combined_all(
        (local_teacher, local_student, local_total), "proto", combine_stats
    )
    stored = jnp.exp(teacher_scores - teacher_peak[:, None])

    def kernel():
        return stored

    row_scale = jnp.ones((teacher_feat.shape[0],), jnp.float32)
    col_scale = jnp.ones((proto_weight.shape[1],), jnp.float32)
    for sweep in range(ITERS):
        col_part = jnp.sum(kernel() * row_scale[:, None], axis=0)
        col_scale = 1.0 / lax.psum(col_part, "dp")
        row_part = jnp.sum(kernel() * col_scale[None, :], axis=1)
        row_scale = 1.0 / lax.psum(row_part, "proto")
    target = kernel() * row_scale[:, None] * col_scale[None, :]
    student_probs = jnp.exp(student_scores - student_peak[:, None]) / student_total[:, None]
    grad_scores = ((student_probs - target) / student_temp).astype(jnp.bfloat16)
    input_part = lax.dot_general(
        grad_scores, proto_weight, (((1,), (1,)), ((), ())), preferred_element_type=jnp.float32
    )
    feature_grad = lax.psum(input_part, "proto")
    proto_grad = lax.psum_scatter(
        lax.dot_general(
            student_feat, grad_scores, (((0,), (0,)), ((), ())), preferred_element_type=jnp.float32
        ),
        "dp",
        scatter_dimension=0,
        tiled=True,
    )
    return (proto_grad, feature_grad)


def solution(mesh):
    return jax.shard_map(
        shards,
        mesh=mesh,
        in_specs=(P("dp", None), P("dp", None), P(None, "proto")),
        out_specs=(P("dp", "proto"), P("dp", None)),
        check_vma=False,
    )
```

profile of v0, /device:TPU:0, one launch (start us, length us, event | category | flops | bytes accessed | tf_op | source)
XLA Modules:
  0.0 284.0 jit_solution(16471339425348787586)
XLA Ops:
  8.0 0.0 all-reduce.2.cloned.1.call-start
  8.1 1.5 copy-done
  9.6 3.4 %fusion.9 = (f32[128]{0:T(128)S(1)}, f32[128,8192]{1,0:T(8,128)}) fusion(bf16[128,128]{1,0:T(8,128)(2,1)} %param.5, bf16[128,8192]{1,0:T(8,128)(2,1)S(1)} %copy-done), kind=kOutput, calls=%fused_computation.31 | convolution fusion | flops 270532480 | bytes 6324736 | tf_op jit(solution)/shard_map/dot_general | solution.py:25
  13.0 6.0 %all-gather.3 = f32[4,1,128]{2,1,0:T(1,128)S(1)} all-gather(f32[1,1,128]{2,1,0:T(1,128)S(1)} %bitcast.46), channel_id=2, replica_groups=mesh['dp'=8,'proto'=4] {'proto'}, dimensions={0}, use_global_device_ids=true | all-gather | bytes 2560 | tf_op jit(solution)/shard_map/all_gather | solution.py:14
  19.0 0.8 fusion.10
  19.8 1.9 copy-done.1
  21.7 0.8 exponential_reduce_fusion
  22.5 5.4 %all-gather.5 = f32[4,1,128]{2,1,0:T(1,128)S(1)} all-gather(f32[1,1,128]{2,1,0:T(1,128)S(1)} %bitcast.47), channel_id=4, replica_groups=mesh['dp'=8,'proto'=4] {'proto'}, dimensions={0}, use_global_device_ids=true | all-gather | bytes 2560 | tf_op jit(solution)/shard_map/all_gather | solution.py:14
  27.9 5.0 %all-gather.4 = f32[4,1,128]{2,1,0:T(1,128)S(1)} all-gather(f32[1,1,128]{2,1,0:T(1,128)S(1)} %bitcast.45), channel_id=3, replica_groups=mesh['dp'=8,'proto'=4] {'proto'}, dimensions={0}, use_global_device_ids=true | all-gather | bytes 2560 | tf_op jit(solution)/shard_map/all_gather | solution.py:14
  32.9 0.1 while.19
  33.0 2.9 %fusion.7 = f32[8192]{0:T(1024)S(1)} fusion(f32[128,8192]{1,0:T(8,128)} %get-tuple-element.205, f32[128]{0:T(128)S(1)} %get-tuple-element.182), kind=kLoop, calls=%fused_computation.30 | loop fusion | flops 2088960 | bytes 4227584 | tf_op jit(solution)/shard_map/reduce_sum | solution.py:56
  35.9 37.6 %psum.49 = f32[8192]{0:T(1024)S(1)} all-reduce(f32[8192]{0:T(1024)S(1)} %fusion.7), channel_id=1, replica_groups=mesh['dp'=8,'proto'=4] {'dp'}, use_global_device_ids=true, to_apply=%region_6.0 | all-reduce | flops 8192 | bytes 65536 | tf_op jit(solution)/shard_map/psum | solution.py:57
  73.6 3.1 %multiply_reduce_fusion.4 = f32[128]{0:T(128)S(1)} fusion(f32[8192]{0:T(1024)S(1)} %broadcast_divide_fusion.2, f32[128,8192]{1,0:T(8,128)} %get-tuple-element.205, f32[128]{0:T(128)S(1)} %get-tuple-element.182), kind=kLoop, calls=%fused_computation.18 | loop fusion | flops 3145600 | bytes 4228096 | tf_op jit(solution)/shard_map/reduce_sum | solution.py:58
  76.6 5.7 %psum.50 = f32[128]{0:T(128)S(1)} all-reduce(f32[128]{0:T(128)S(1)} %multiply_reduce_fusion.4), channel_id=1, replica_groups=mesh['dp'=8,'proto'=4] {'proto'}, use_global_device_ids=true, to_apply=%region_8.0 | all-reduce | flops 128 | bytes 1024 | tf_op jit(solution)/shard_map/psum | solution.py:59
  82.3 3.0 %multiply_reduce_fusion.3 = f32[8192]{0:T(1024)S(1)} fusion(f32[128]{0:T(128)S(1)} %broadcast_divide_fusion.5, f32[128,8192]{1,0:T(8,128)} %get-tuple-element.205, f32[128]{0:T(128)S(1)} %get-tuple-element.182), kind=kLoop, calls=%fused_computation.17 | loop fusion | flops 3137536 | bytes 4228096 | tf_op jit(solution)/shard_map/reduce_sum | solution.py:56
  85.3 33.0 %psum.51 = f32[8192]{0:T(1024)S(1)} all-reduce(f32[8192]{0:T(1024)S(1)} %multiply_reduce_fusion.3), channel_id=1, replica_groups=mesh['dp'=8,'proto'=4] {'dp'}, use_global_device_ids=true, to_apply=%region_10.0 | all-reduce | flops 8192 | bytes 65536 | tf_op jit(solution)/shard_map/psum | solution.py:57
  118.3 3.1 %multiply_reduce_fusion.2 = f32[128]{0:T(128)S(1)} fusion(f32[8192]{0:T(1024)S(1)} %broadcast_divide_fusion.1, f32[128,8192]{1,0:T(8,128)} %get-tuple-element.205, f32[128]{0:T(128)S(1)} %get-tuple-element.182), kind=kLoop, calls=%fused_computation.16 | loop fusion | flops 3145600 | bytes 4228096 | tf_op jit(solution)/shard_map/reduce_sum | solution.py:58
  121.4 5.7 %psum.52 = f32[128]{0:T(128)S(1)} all-reduce(f32[128]{0:T(128)S(1)} %multiply_reduce_fusion.2), channel_id=1, replica_groups=mesh['dp'=8,'proto'=4] {'proto'}, use_global_device_ids=true, to_apply=%region_12.0 | all-reduce | flops 128 | bytes 1024 | tf_op jit(solution)/shard_map/psum | solution.py:59
  127.1 3.0 %multiply_reduce_fusion.1 = f32[8192]{0:T(1024)S(1)} fusion(f32[128]{0:T(128)S(1)} %broadcast_divide_fusion.4, f32[128,8192]{1,0:T(8,128)} %get-tuple-element.205, f32[128]{0:T(128)S(1)} %get-tuple-element.182), kind=kLoop, calls=%fused_computation.15 | loop fusion | flops 3137536 | bytes 4228096 | tf_op jit(solution)/shard_map/reduce_sum | solution.py:56
  130.1 33.0 %psum.53 = f32[8192]{0:T(1024)S(1)} all-reduce(f32[8192]{0:T(1024)S(1)} %multiply_reduce_fusion.1), channel_id=1, replica_groups=mesh['dp'=8,'proto'=4] {'dp'}, use_global_device_ids=true, to_apply=%region_14.0 | all-reduce | flops 8192 | bytes 65536 | tf_op jit(solution)/shard_map/psum | solution.py:57
  163.1 3.0 %multiply_reduce_fusion = f32[128]{0:T(128)S(1)} fusion(f32[8192]{0:T(1024)S(1)} %broadcast_divide_fusion, f32[128,8192]{1,0:T(8,128)} %get-tuple-element.205, f32[128]{0:T(128)S(1)} %get-tuple-element.182), kind=kLoop, calls=%fused_computation.14 | loop fusion | flops 3145600 | bytes 4228096 | tf_op jit(solution)/shard_map/reduce_sum | solution.py:58
  166.1 5.7 %psum.54 = f32[128]{0:T(128)S(1)} all-reduce(f32[128]{0:T(128)S(1)} %multiply_reduce_fusion), channel_id=1, replica_groups=mesh['dp'=8,'proto'=4] {'proto'}, use_global_device_ids=true, to_apply=%region_16.0 | all-reduce | flops 128 | bytes 1024 | tf_op jit(solution)/shard_map/psum | solution.py:59
  171.8 4.4 %multiply_convert_fusion = bf16[128,8192]{1,0:T(8,128)(2,1)S(1)} fusion(f32[128,8192]{1,0:T(8,128)} %copy-done.1, f32[128]{0:T(128)S(1)} %broadcast_divide_fusion.3, f32[8192]{0:T(1024)S(1)} %broadcast_divide_fusion, f32[128]{0:T(128)S(1)} %get-tuple-element.181, f32[128]{0:T(128)S(1)} %get-tuple-element.180, f32[128,8192]{1,0:T(8,128)} %get-tuple-element.205, ...), kind=kLoop, calls=%fused_computation.13 | loop fusion | flops 8388608 | bytes 10520576 | tf_op jit(solution)/shard_map/convert_element_type | solution.py:62
  176.2 1.3 copy-done.2
  177.5 1.6 fusion.11
  179.1 0.0 reduce-scatter.4.cloned.1.call-start
  179.2 4.3 %convolution_bitcast_fusion = f32[128,8192]{0,1:T(8,128)} fusion(bf16[128,8192]{1,0:T(8,128)(2,1)} %copy-done.2, bf16[128,128]{1,0:T(8,128)(2,1)S(1)} %copy-done.3), kind=kOutput, calls=%fused_computation.10 | convolution fusion | flops 268435456 | bytes 6324224 | tf_op jit(solution)/shard_map/dot_general | solution.py:68
  183.4 5.7 %copy.7 = f32[128,8192]{1,0:T(8,128)} copy(f32[128,8192]{0,1:T(8,128)} %convolution_bitcast_fusion) | data formatting | bytes 8388608
  189.1 0.0 reduce-scatter.4.cloned.1.call-update
  189.1 19.4 %all-reduce.2.cloned.1.call-done = f32[128,128]{1,0:T(8,128)} async-done(((f32[128,128]{1,0:T(8,128)}), f32[128,128]{1,0:T(8,128)}) %all-reduce.2.cloned.1.call-update) | async-done | bytes 65552 | tf_op jit(solution)/shard_map/psum | solution.py:66
  208.5 66.6 %reduce-scatter.4.cloned.1.call-done = f32[16,8192]{1,0:T(8,128)} async-done(((f32[128,8192]{1,0:T(8,128)}), f32[16,8192]{1,0:T(8,128)}) %reduce-scatter.4.cloned.1.call-update) | async-done | bytes 524304
  275.1 1.5 copy.22
  (18 shorter events, 0.2 us)
Async XLA Ops:
  8.0 1.6 copy-start
  8.0 11.0 %copy-start.3 = (bf16[128,128]{1,0:T(8,128)(2,1)S(1)}, bf16[128,128]{1,0:T(8,128)(2,1)}, u32[]{:S(2)}) copy-start(bf16[128,128]{1,0:T(8,128)(2,1)} %param.6) | copy-start | bytes 98308
  8.0 200.5 %all-reduce.2.cloned.1.call-start = ((), (), s32[]{:S(2)}) async-start(), calls=%async_computation.1 | async-start | bytes 131072 | tf_op jit(solution)/shard_map/psum | solution.py:66
  19.8 1.9 copy-start.1
  176.2 1.3 copy-start.2
  179.1 96.0 %reduce-scatter.4.cloned.1.call-start = ((), (), s32[]{:S(2)}) async-start(), calls=%async_computation.2 | async-start | bytes 4718592
Sparse Core Ops, SparseCore 0:
  179.2 29.2 all-reduce.1
Sparse Core Ops, SparseCore 1:
  189.2 85.9 reduce-scatter.3
where the time goes:
time: 285 us; the launch traced here: 284 us
  blocking collectives  137 us (48%)
  waiting for transfers between devices  86 us (30%)
  other arithmetic  23.3 us (8%)
  between operations  15.6 us (5%)
  local copies, waits for them, and re-layouts  11.9 us (4%)
  matrix products  10.1 us (4%)
    psum x3, blocking collectives, shards(): col_scale = 1.0 / lax.psum(col_part, 'dp')  104 us
    unnamed x3, waiting for transfers between devices  66.7 us
    psum x1, waiting for transfers between devices, shards(): feature_grad = lax.psum(input_part, 'proto')  19.4 us
    psum x3, blocking collectives, shards(): row_scale = 1.0 / lax.psum(row_part, 'proto')  17 us
    all_gather x3, blocking collectives, combined_all(): everything = jax.tree.map(lambda part: lax.all_gather(part, axis), value)  16.4 us
    unnamed x10, local copies, waits for them, and re-layouts  11.9 us
    reduce_sum x3, other arithmetic, shards(): row_part = jnp.sum(kernel() * col_scale[None, :], axis=1)  9.18 us
    reduce_sum x3, other arithmetic, shards(): col_part = jnp.sum(kernel() * row_scale[:, None], axis=0)  8.86 us
  transfers between devices with their start and end apart: 2, of which 2 were waited for; matrix products, arithmetic and copies ran while one was open for 3% of the time, Pallas kernels for 0%

commit v1 on v0

v1 whole, which is shorter than its diff:
```python
import math

import jax
import jax.numpy as jnp
from jax import lax
from jax.experimental import pallas as pl
from jax.experimental.pallas import tpu as pltpu
from jax.sharding import PartitionSpec as P

ITERS = 3

teacher_temp = 0.07
student_temp = 0.1

LOG2E = math.log2(math.e)
T_EXP = LOG2E / teacher_temp
S_EXP = LOG2E / student_temp

LANES = 128
SUB = 8
PARTS = 4
STAT_ROWS = 8
KERNEL_BYTES = 32 << 20


def combined_all(value, axis, combine):
    everything = jax.tree.map(lambda part: lax.all_gather(part, axis), value)
    leading = jax.tree.map(lambda part: part[0], everything)

    def step(k, so_far):
        return combine(so_far, jax.tree.map(lambda part: part[k], everything))

    return lax.fori_loop(1, lax.axis_size(axis), step, leading)


def divided_logits(features, prototypes, divisor):
    return jnp.dot(features, prototypes, preferred_element_type=jnp.float32) / divisor


def combine_stats(earlier, later):
    teacher_peak = jnp.maximum(earlier[0], later[0])
    student_peak = jnp.maximum(earlier[1], later[1])
    merged_total = earlier[2] * jnp.exp(earlier[1] - student_peak) + later[2] * jnp.exp(
        later[1] - student_peak
    )
    return (teacher_peak, student_peak, merged_total)


def split_crops(teacher_feat, student_feat, proto_weight):
    teacher_scores = divided_logits(teacher_feat, proto_weight, teacher_temp)
    student_scores = divided_logits(student_feat, proto_weight, student_temp)
    local_teacher = jnp.max(teacher_scores, axis=1)
    local_student = jnp.max(student_scores, axis=1)
    local_total = jnp.sum(jnp.exp(student_scores - local_student[:, None]), axis=1)
    teacher_peak, student_peak, student_total = combined_all(
        (local_teacher, local_student, local_total), "proto", combine_stats
    )
    kernel = jnp.exp(teacher_scores - teacher_peak[:, None])
    row_scale = jnp.ones((teacher_feat.shape[0],), jnp.float32)
    for sweep in range(ITERS):
        col_part = jnp.sum(kernel * row_scale[:, None], axis=0)
        col_scale = 1.0 / lax.psum(col_part, "dp")
        row_part = jnp.sum(kernel * col_scale[None, :], axis=1)
        row_scale = 1.0 / lax.psum(row_part, "proto")
    target = kernel * row_scale[:, None] * col_scale[None, :]
    student_probs = jnp.exp(student_scores - student_peak[:, None]) / student_total[:, None]
    grad_scores = ((student_probs - target) / student_temp).astype(jnp.bfloat16)
    input_part = lax.dot_general(
        grad_scores, proto_weight, (((1,), (1,)), ((), ())), preferred_element_type=jnp.float32
    )
    feature_grad = lax.psum(input_part, "proto")
    proto_grad = lax.psum_scatter(
        lax.dot_general(
            student_feat, grad_scores, (((0,), (0,)), ((), ())), preferred_element_type=jnp.float32
        ),
        "dp",
        scatter_dimension=0,
        tiled=True,
    )
    return (proto_grad, feature_grad)


def vmem():
    return pl.BlockSpec(memory_space=pltpu.VMEM)


def smem():
    return pl.BlockSpec(memory_space=pltpu.SMEM)


def swap(x, axis, bit):
    return lax.ppermute(x, axis, [(i, i ^ bit) for i in range(lax.axis_size(axis))])


def fold(parts, op):
    parts = list(parts)
    while len(parts) > 1:
        parts = [op(*parts[k : k + 2]) if k + 1 < len(parts) else parts[k] for k in range(0, len(parts), 2)]
    return parts[0]


def lane_tiles(x):
    return [x[:, k : k + LANES] for k in range(0, x.shape[1], LANES)]


def spread_rows(flat, out_ref):
    for j in range(flat.shape[0]):
        wide = jnp.broadcast_to(flat[j : j + 1, :], (LANES, LANES))
        out_ref[j * LANES : (j + 1) * LANES, :] = wide.T


def gather_rows(acc_ref):
    n = acc_ref.shape[0] // LANES
    rows = [
        jnp.sum(acc_ref[j * LANES : (j + 1) * LANES, :].T, axis=0, keepdims=True) for j in range(n)
    ]
    return jnp.concatenate(rows, axis=0)


def own_body(place_ref, t_ref, s_ref, w_ref, out_ref, scores_ref):
    rows = t_ref.shape[0]
    half = rows // 2
    width = scores_ref.shape[2]
    count = scores_ref.shape[0]
    t = t_ref[...]
    s = s_ref[...]

    def scores(j, so_far):
        w = w_ref[:, pl.ds(pl.multiple_of(j * width, width), width)]
        a = jnp.dot(t, w, preferred_element_type=jnp.float32)
        b = jnp.dot(s, w, preferred_element_type=jnp.float32)
        scores_ref[j] = b
        return (
            jnp.maximum(so_far[0], fold(lane_tiles(a), jnp.maximum)),
            jnp.maximum(so_far[1], fold(lane_tiles(b), jnp.maximum)),
        )

    low = jnp.full((rows, LANES), -jnp.inf, jnp.float32)
    t_max, s_max = lax.fori_loop(0, count, scores, (low, low))
    s_col = jnp.max(s_max, axis=1, keepdims=True)

    def total(j, so_far):
        e = jnp.exp2((scores_ref[j] - s_col) * S_EXP)
        return so_far + fold(lane_tiles(e), jnp.add)

    s_sum = lax.fori_loop(0, count, total, jnp.zeros((rows, LANES), jnp.float32))
    first = pl.multiple_of(place_ref[0] * half, half)
    out_ref[0:half, :] = t_ref[pl.ds(first, half), :].astype(jnp.float32)
    out_ref[half : 2 * half, :] = s_ref[pl.ds(first, half), :].astype(jnp.float32)
    stats = [
        jnp.max(t_max.T, axis=0, keepdims=True),
        jnp.max(s_max.T, axis=0, keepdims=True),
        jnp.sum(s_sum.T, axis=0, keepdims=True),
        jnp.zeros((STAT_ROWS - 3, LANES), jnp.float32),
    ]
    out_ref[2 * half :, :] = jnp.concatenate(stats, axis=0)


def exp_body(place_ref, mine_ref, other_ref, w_ref, *refs):
    k_refs = refs[:PARTS]
    s_ref, t_scr, m_scr = refs[PARTS:]
    blocks = mine_ref.shape[0]
    rows = LANES
    half = rows // 2
    core = place_ref[0]
    for j in range(blocks):
        a = pl.multiple_of(j * rows + core * half, half)
        b = pl.multiple_of(j * rows + (1 - core) * half, half)
        t_scr[pl.ds(a, half), :] = mine_ref[j, 0:half, :].astype(jnp.bfloat16)
        t_scr[pl.ds(b, half), :] = other_ref[j, 0:half, :].astype(jnp.bfloat16)
        s_ref[pl.ds(a, half), :] = mine_ref[j, half : 2 * half, :].astype(jnp.bfloat16)
        s_ref[pl.ds(b, half), :] = other_ref[j, half : 2 * half, :].astype(jnp.bfloat16)
        wide = jnp.broadcast_to(mine_ref[j, 2 * half : 2 * half + 1, :], (LANES, LANES))
        m_scr[j * rows : (j + 1) * rows, :] = wide.T
    t = t_scr[...]
    m = m_scr[:, 0:1]
    per, unused, width = k_refs[0].shape
    for p in range(PARTS):

        def block(j, unused, p=p):
            start = pl.multiple_of((p * per + j) * width, width)
            s = jnp.dot(t, w_ref[:, pl.ds(start, width)], preferred_element_type=jnp.float32)
            k_refs[p][j] = jnp.exp2((s - m) * T_EXP)
            return 0

        lax.fori_loop(0, per, block, 0)


def sweep_body(first, n_in, *refs):
    k_refs = refs[:PARTS]
    in_refs = refs[PARTS : PARTS + n_in]
    rest = refs[PARTS + n_in :]
    if first:
        out_refs, rest = rest[:PARTS], rest[PARTS:]
    else:
        out_refs = k_refs
    o_ref, c_ref, r_scr, acc_ref = rest
    if first:
        peak = fold([x[0] for x in in_refs], jnp.maximum)
        scale = jnp.exp2((in_refs[0][0] - peak) * T_EXP)
    else:
        scale = 1.0 / fold([x[...] for x in in_refs], jnp.add)
    spread_rows(scale, r_scr)
    acc_ref[...] = jnp.zeros_like(acc_ref)
    per, rows, width = k_refs[0].shape
    tiles = width // LANES
    unroll = 32
    steps = rows // SUB // unroll

    for p in range(PARTS):
        k_ref, out_ref = k_refs[p], out_refs[p]

        def block(j, unused, p=p, k_ref=k_ref, out_ref=out_ref):
            def down(i, sums):
                base = pl.multiple_of(i * (unroll * SUB), unroll * SUB)
                for u in range(unroll):
                    at = pl.ds(base + u * SUB, SUB)
                    rb = r_scr[at, :]
                    new = []
                    for q in range(tiles):
                        x = k_ref[j, at, q * LANES : (q + 1) * LANES] * rb
                        if first:
                            out_ref[j, at, q * LANES : (q + 1) * LANES] = x
                        new.append(sums[q] + x)
                    sums = tuple(new)
                return sums

            zero = jnp.zeros((SUB, LANES), jnp.float32)
            sums = lax.fori_loop(0, steps, down, (zero,) * tiles)
            cols = [1.0 / jnp.sum(x, axis=0, keepdims=True) for x in sums]
            for q in range(tiles):
                c_ref[p * per + j, :, q * LANES : (q + 1) * LANES] = cols[q]
            wide = [jnp.broadcast_to(x, (SUB, LANES)) for x in cols]

            def across(i, unused):
                base = pl.multiple_of(i * (unroll * SUB), unroll * SUB)
                for u in range(unroll):
                    at = pl.ds(base + u * SUB, SUB)
                    x = [out_ref[j, at, q * LANES : (q + 1) * LANES] * wide[q] for q in range(tiles)]
                    acc_ref[at, :] = acc_ref[at, :] + fold(x, jnp.add)
                return 0

            lax.fori_loop(0, steps, across, 0)
            return 0

        lax.fori_loop(0, per, block, 0)
    o_ref[...] = gather_rows(acc_ref)


def student_scale(stat_refs):
    peak = fold([x[1] for x in stat_refs], jnp.maximum)
    total = fold([x[2] * jnp.exp2((x[1] - peak) * S_EXP) for x in stat_refs], jnp.add)
    return peak, 1.0 / (total * student_temp)


def final_body(n_in, own_only, *refs):
    k_refs = refs[:PARTS]
    row_refs = refs[PARTS : PARTS + n_in]
    stat_refs = refs[PARTS + n_in : PARTS + 2 * n_in]
    rest = refs[PARTS + 2 * n_in :]
    if own_only:
        c_ref, s_ref, w_ref, out_ref, r_scr, m_scr, i_scr = rest
    else:
        c_ref, s_ref, w_ref, place_ref, out_ref, r_scr, m_scr, i_scr = rest
    rows = r_scr.shape[0]
    n = rows // LANES
    row_scale = 1.0 / fold([x[...] for x in row_refs], jnp.add)
    peak, inverse = student_scale(stat_refs)
    spread_rows((row_scale * (1.0 / student_temp))[:n], r_scr)
    spread_rows(peak[:n], m_scr)
    spread_rows(inverse[:n], i_scr)
    per, unused, width = k_refs[0].shape
    s = s_ref[0:rows, :]
    m = m_scr[:, 0:1]
    inv = i_scr[:, 0:1]
    r = r_scr[:, 0:1]
    if own_only:
        out_ref[...] = jnp.zeros_like(out_ref)
    else:
        shape = (out_ref.shape[0], s.shape[1])
        wanted = lax.broadcasted_iota(jnp.int32, shape, 0) + place_ref[1] * shape[0]
        pick = (lax.broadcasted_iota(jnp.int32, shape, 1) == wanted).astype(jnp.float32)
        picked = lax.dot_general(
            pick.astype(jnp.bfloat16), s, (((1,), (1,)), ((), ())), preferred_element_type=jnp.float32
        ).astype(jnp.bfloat16)
    for p in range(PARTS):

        def block(j, unused, p=p):
            start = pl.multiple_of((p * per + j) * width, width)
            w = w_ref[:, pl.ds(start, width)]
            scores = jnp.dot(s, w, preferred_element_type=jnp.float32)
            probs = jnp.exp2((scores - m) * S_EXP) * inv
            target = k_refs[p][j, 0:rows, :] * r * c_ref[p * per + j]
            grad = (probs - target).astype(jnp.bfloat16)
            if own_only:
                out_ref[...] += lax.dot_general(
                    grad, w, (((1,), (1,)), ((), ())), preferred_element_type=jnp.float32
                )
            else:
                out_ref[:, pl.ds(start, width)] = jnp.dot(
                    picked, grad, preferred_element_type=jnp.float32
                )
            return 0

        lax.fori_loop(0, per, block, 0)


def all_crops(teacher_feat, student_feat, proto_weight):
    own, depth = teacher_feat.shape
    n_dp = lax.axis_size("dp")
    n_proto = lax.axis_size("proto")
    rows = own * n_dp
    cols = proto_weight.shape[1]
    width = 1024
    per = cols // width // PARTS
    f32 = jnp.float32
    params = pltpu.CompilerParams(vmem_limit_bytes=16 << 20)
    place = jnp.stack([lax.axis_index("proto") % 2, lax.axis_index("dp")]).astype(jnp.int32)

    payload = pl.pallas_call(
        own_body,
        out_shape=jax.ShapeDtypeStruct((own + STAT_ROWS, depth), f32),
        in_specs=[smem(), vmem(), vmem(), vmem()],
        out_specs=vmem(),
        scratch_shapes=[pltpu.VMEM((cols // width, own, width), f32)],
        compiler_params=params,
        name="own_stats",
    )(place, teacher_feat, student_feat, proto_weight)

    mine = payload[None]
    bit = 1
    while bit < n_dp:
        mine = jnp.concatenate([mine, swap(mine, "dp", bit)], axis=0)
        bit *= 2
    other = swap(mine, "proto", 1)
    stats = jnp.swapaxes(mine[:, own : own + 3, :], 0, 1)

    def everyone(x):
        return [x] + [swap(x, "proto", k) for k in range(1, n_proto)]

    all_stats = everyone(stats)
    k_shape = pltpu.VMEM((per, rows, width), f32)
    *kernel, s_all = pl.pallas_call(
        exp_body,
        out_shape=(k_shape,) * PARTS + (jax.ShapeDtypeStruct((rows, depth), jnp.bfloat16),),
        in_specs=[smem(), vmem(), vmem(), vmem()],
        out_specs=(vmem(),) * (PARTS + 1),
        scratch_shapes=[pltpu.VMEM((rows, depth), jnp.bfloat16), pltpu.VMEM((rows, LANES), f32)],
        compiler_params=params,
        name="kernel_exp",
    )(place, mine, other, proto_weight)

    def sweep(kernel, ins, first):
        outs = (
            jax.ShapeDtypeStruct((rows // LANES, LANES), f32),
            jax.ShapeDtypeStruct((cols // width, 1, width), f32),
        )
        kept = (k_shape,) * PARTS if first else ()
        result = pl.pallas_call(
            lambda *refs: sweep_body(first, len(ins), *refs),
            out_shape=kept + outs,
            in_specs=[vmem()] * (PARTS + len(ins)),
            out_specs=(vmem(),) * (len(kept) + 2),
            scratch_shapes=[pltpu.VMEM((rows, LANES), f32), pltpu.VMEM((rows, LANES), f32)],
            input_output_aliases={k: k for k in range(len(kept))},
            compiler_params=params,
            name="sweep_first" if first else "sweep",
        )(*kernel, *ins)
        return (result[:PARTS] if first else kernel), result[-2], result[-1]

    ins = all_stats
    for it in range(ITERS):
        kernel, row_part, col_scale = sweep(kernel, ins, it == 0)
        ins = everyone(row_part)

    def final(own_only, extra, shape, crops, name):
        return pl.pallas_call(
            lambda *refs: final_body(len(ins), own_only, *refs),
            out_shape=jax.ShapeDtypeStruct(shape, f32),
            in_specs=[vmem()] * (PARTS + 2 * len(ins) + 3) + [smem()] * len(extra),
            out_specs=vmem(),
            scratch_shapes=[pltpu.VMEM((crops, LANES), f32)] * 3,
            compiler_params=params,
            name=name,
        )(*kernel, *ins, *all_stats, col_scale, s_all, proto_weight, *extra)

    part = final(True, (), (own, depth), own, "own_grad")
    parts = everyone(part)
    proto_grad = final(False, (place,), (depth // n_dp, cols), rows, "proto_grad")
    feature_grad = fold(parts, jnp.add)
    return (proto_grad, feature_grad)


def solution(mesh):
    n_dp = mesh.shape["dp"]
    n_proto = mesh.shape["proto"]

    def shards(teacher_feat, student_feat, proto_weight):
        own, depth = teacher_feat.shape
        cols = proto_weight.shape[1]
        fits = (
            own * n_dp * cols * 4 <= KERNEL_BYTES
            and own == LANES
            and depth == LANES
            and cols % (PARTS * 1024) == 0
            and n_dp & (n_dp - 1) == 0
            and n_proto & (n_proto - 1) == 0
            and 2 <= n_proto <= 8
            and depth % (n_dp * SUB) == 0
        )
        plan = all_crops if fits else split_crops
        return plan(teacher_feat, student_feat, proto_weight)

    return jax.shard_map(
        shards,
        mesh=mesh,
        in_specs=(P("dp", None), P("dp", None), P(None, "proto")),
        out_specs=(P("dp", "proto"), P("dp", None)),
        check_vma=False,
    )
```

time: 285 us -> 110 us (0.39)
  blocking collectives: 137 us -> 0 us
  waiting for transfers between devices: 86 us -> 22.9 us
  Pallas kernels: 0 us -> 61.1 us
  other arithmetic: 23.3 us -> 1.3 us
  starting transfers between devices: 0.08 us -> 18.4 us
  between operations: 15.6 us -> 0.77 us
  matrix products: 10.1 us -> 0 us
  local copies, waits for them, and re-layouts: 11.9 us -> 4.91 us
    psum x6 -> x0, blocking collectives: 121 us -> none  [the longest x3 104 us: shards(): col_scale = 1.0 / lax.psum(col_part, 'dp')]
    unnamed x3 -> x0, waiting for transfers between devices: 66.7 us -> none
    pallas_call x0 -> x7, Pallas kernels: none -> 61.1 us  [the longest x3 32.6 us: sweep(): pl.pallas_call(lambda *refs: sweep_body(first, len(ins), *refs), out_shap...]
    ppermute x0 -> x19, waiting for transfers between devices: none -> 22.9 us  [swap(): lax.ppermute(x, axis, [(i, i ^ bit) for i in range(lax.axis_size(axis))])]
    psum x1 -> x0, waiting for transfers between devices: 19.4 us -> none  [shards(): feature_grad = lax.psum(input_part, 'proto')]
    reduce_sum x7 -> x0, other arithmetic: 18.8 us -> none  [the longest x3 9.18 us: shards(): row_part = jnp.sum(kernel() * col_scale[None, :], axis=1)]
    ppermute x0 -> x19, starting transfers between devices: none -> 18.4 us  [swap(): lax.ppermute(x, axis, [(i, i ^ bit) for i in range(lax.axis_size(axis))])]
    all_gather x3 -> x0, blocking collectives: 16.4 us -> none  [combined_all(): everything = jax.tree.map(lambda part: lax.all_gather(part, axis), value)]
  transfers between devices with their start and end apart: 2 -> 19, of which waited for: 2 -> 9; matrix products, arithmetic and copies ran while one was open for 3% -> 0% of each run, Pallas kernels for 0% -> 20%
where the time goes in v1:
time: 110 us; the launch traced here: 109 us
  Pallas kernels  61.1 us (56%)
  waiting for transfers between devices  22.9 us (21%)
  starting transfers between devices  18.4 us (17%)
  local copies, waits for them, and re-layouts  4.91 us (4%)
  other arithmetic  1.3 us (1%)
    pallas_call x3, Pallas kernels, sweep(): pl.pallas_call(lambda *refs: sweep_body(first, len(ins), *refs), out_shap...  32.6 us
    ppermute x19, waiting for transfers between devices, swap(): lax.ppermute(x, axis, [(i, i ^ bit) for i in range(lax.axis_size(axis))])  22.9 us
    ppermute x19, starting transfers between devices, swap(): lax.ppermute(x, axis, [(i, i ^ bit) for i in range(lax.axis_size(axis))])  18.4 us
    pallas_call x2, Pallas kernels, final(): pl.pallas_call(lambda *refs: final_body(len(ins), own_only, *refs), out_s...  18 us
    pallas_call x1, Pallas kernels, all_crops(): pl.pallas_call(exp_body, out_shape=(k_shape,) * PARTS + (jax.ShapeDtypeSt...  6.77 us
    unnamed x8, local copies, waits for them, and re-layouts  4.69 us
    pallas_call x1, Pallas kernels, all_crops(): pl.pallas_call(own_body, out_shape=jax.ShapeDtypeStruct((own + STAT_ROWS,...  3.75 us
  transfers between devices with their start and end apart: 19, of which 9 were waited for; matrix products, arithmetic and copies ran while one was open for 0% of the time, Pallas kernels for 20%

profile of v1, /device:TPU:0, one launch (start us, length us, event | category | flops | bytes accessed | tf_op | source)
XLA Modules:
  0.0 109.3 jit_solution(221190436848215240)
XLA Ops:
  0.7 1.6 %copy-done = bf16[128,8192]{1,0:T(8,128)(2,1)S(1)} copy-done((bf16[128,8192]{1,0:T(8,128)(2,1)S(1)}, bf16[128,8192]{1,0:T(8,128)(2,1)}, u32[]{:S(2)}) %copy-start) | copy-done | bytes 2097176
  2.3 0.8 copy-done.2
  3.1 0.8 copy-done.3
  3.8 3.8 %own_stats.1 = f32[136,128]{1,0:T(8,128)S(1)} custom-call(s32[2]{0:T(128)S(1)} %pad_add_fusion.place_ref.refs_15_, bf16[128,128]{1,0:T(8,128)(2,1)S(1)} %copy-done.2, bf16[128,128]{1,0:T(8,128)(2,1)S(1)} %copy-done.3, bf16[128,8192]{1,0:T(8,128)(2,1)S(1)} %copy-done), custom_call_target="tpu_custom_call" | custom-call | tf_op jit(solution)/shard_map/own_stats/pallas_call | solution.py:320
  7.6 3.1 %collective-permute-start = (f32[1,136,128]{2,0,1:T(1,128)S(1)}, f32[1,136,128]{2,0,1:T(1,128)S(1)}, u32[]{:S(2)}, u32[]{:S(2)}) collective-permute-start(f32[1,136,128]{2,0,1:T(1,128)S(1)} %bitcast.5), channel_id=1, source_target_pairs={{0,4},{4,0},{8,12},{12,8},{16,20},{20,16},{24,28},{28,24},{1,5},{5... | collective-permute-start | bytes 208904 | tf_op jit(solution)/shard_map/ppermute | solution.py:92
  10.6 2.3 %collective-permute-done = f32[1,136,128]{2,0,1:T(1,128)S(1)} collective-permute-done((f32[1,136,128]{2,0,1:T(1,128)S(1)}, f32[1,136,128]{2,0,1:T(1,128)S(1)}, u32[]{:S(2)}, u32[]{:S(2)}) %collective-permute-start) | collective-permute-done | bytes 69664 | tf_op jit(solution)/shard_map/ppermute | solution.py:92
  13.1 2.1 %collective-permute-start.1 = (f32[2,136,128]{2,0,1:T(2,128)S(1)}, f32[2,136,128]{2,0,1:T(2,128)S(1)}, u32[]{:S(2)}, u32[]{:S(2)}) collective-permute-start(f32[2,136,128]{2,0,1:T(2,128)S(1)} %pad_maximum_fusion.2), channel_id=1, source_target_pairs={{0,8},{4,12},{8,0},{12,4},{16,24},{20,28},{24,16},{28,20},{1,9},{5... | collective-permute-start | bytes 417800 | tf_op jit(solution)/shard_map/ppermute | solution.py:92
  15.2 3.0 %collective-permute-done.1 = f32[2,136,128]{2,0,1:T(2,128)S(1)} collective-permute-done((f32[2,136,128]{2,0,1:T(2,128)S(1)}, f32[2,136,128]{2,0,1:T(2,128)S(1)}, u32[]{:S(2)}, u32[]{:S(2)}) %collective-permute-start.1) | collective-permute-done | bytes 139296 | tf_op jit(solution)/shard_map/ppermute | solution.py:92
  18.4 3.1 %collective-permute-start.2 = (f32[4,136,128]{2,0,1:T(4,128)S(1)}, f32[4,136,128]{2,0,1:T(4,128)S(1)}, u32[]{:S(2)}, u32[]{:S(2)}) collective-permute-start(f32[4,136,128]{2,0,1:T(4,128)S(1)} %pad_maximum_fusion.1), channel_id=1, source_target_pairs={{0,16},{4,20},{8,24},{12,28},{16,0},{20,4},{24,8},{28,12},{1,17},{... | collective-permute-start | bytes 835592 | tf_op jit(solution)/shard_map/ppermute | solution.py:92
  21.5 10.3 %collective-permute-done.2 = f32[4,136,128]{2,0,1:T(4,128)S(1)} collective-permute-done((f32[4,136,128]{2,0,1:T(4,128)S(1)}, f32[4,136,128]{2,0,1:T(4,128)S(1)}, u32[]{:S(2)}, u32[]{:S(2)}) %collective-permute-start.2) | collective-permute-done | bytes 278560 | tf_op jit(solution)/shard_map/ppermute | solution.py:92
  32.2 1.6 %collective-permute-start.6 = (f32[3,8,128]{2,1,0:T(8,128)S(1)}, f32[3,8,128]{2,1,0:T(8,128)S(1)}, u32[]{:S(2)}, u32[]{:S(2)}) collective-permute-start(f32[3,8,128]{2,1,0:T(8,128)S(1)} %slice_bitcast_fusion.refs_4_.refs_8_), channel_id=1, source_target_pairs={{0,3},{1,2},{2,1},{3,0},{4,7},{5,6},{6,5},{7,4},{8,11},{9,10},{10,... | collective-permute-start | bytes 36872 | tf_op jit(solution)/shard_map/ppermute | solution.py:92
  34.6 1.6 %copy-done.1 = bf16[128,8192]{1,0:T(8,128)(2,1)S(1)} copy-done((bf16[128,8192]{1,0:T(8,128)(2,1)S(1)}, bf16[128,8192]{1,0:T(8,128)(2,1)}, u32[]{:S(2)}) %copy-start.1) | copy-done | bytes 2097176
  36.2 6.8 %kernel_exp.1 = (f32[2,1024,1024]{2,1,0:T(8,128)S(1)}, f32[2,1024,1024]{2,1,0:T(8,128)S(1)}, f32[2,1024,1024]{2,1,0:T(8,128)S(1)}, f32[2,1024,1024]{2,1,0:T(8,128)S(1)}, bf16[1024,128]{1,0:T(8,128)(2,1)S(1)}) custom-call(s32[2]{0:T(128)S(1)} %pad_add_fusion.place_ref.refs_15_, f32[8,136,128]{2,1,0:T(8,128)S(1)} %copy.9.mine_ref, ...), custom_call_target="tpu_custom_call" | custom-call | tf_op jit(solution)/shard_map/kernel_exp/pallas_call | solution.py:343
  43.0 21.2 %sweep_first.1 = (f32[2,1024,1024]{2,1,0:T(8,128)S(1)}, f32[2,1024,1024]{2,1,0:T(8,128)S(1)}, f32[2,1024,1024]{2,1,0:T(8,128)S(1)}, f32[2,1024,1024]{2,1,0:T(8,1...) custom-call(f32[2,1024,1024]{2,1,0:T(8,128)S(1)} %get-tuple-element., ...), custom_call_target="tpu_custom_call", output_to_operand_aliasing={{0}: (0, {}), {1}: (1, {}), {2}: (2, {}), {3}: (3, {})} | custom-call | tf_op jit(solution)/shard_map/sweep_first/pallas_call | solution.py:359
  64.2 1.6 %collective-permute-start.9 = (f32[8,128]{1,0:T(8,128)S(1)}, f32[8,128]{1,0:T(8,128)S(1)}, u32[]{:S(2)}, u32[]{:S(2)}) collective-permute-start(f32[8,128]{1,0:T(8,128)S(1)} %get-tuple-element.23.refs_4_), channel_id=1, source_target_pairs={{0,3},{1,2},{2,1},{3,0},{4,7},{5,6},{6,5},{7,4},{8,11},{9,10},{10,... | collective-permute-start | bytes 12296 | tf_op jit(solution)/shard_map/ppermute | solution.py:92
  65.8 0.5 collective-permute-start.8
  66.3 0.9 collective-permute-done.9.refs_7_
  67.2 2.2 %collective-permute-done.8.refs_6_ = f32[8,128]{1,0:T(8,128)S(1)} collective-permute-done((f32[8,128]{1,0:T(8,128)S(1)}, f32[8,128]{1,0:T(8,128)S(1)}, u32[]{:S(2)}, u32[]{:S(2)}) %collective-permute-start.8) | collective-permute-done | bytes 4128 | tf_op jit(solution)/shard_map/ppermute | solution.py:92
  69.4 5.9 %sweep.2 = (f32[8,128]{1,0:T(8,128)S(1)}, f32[8,1,1024]{2,1,0:T(1,128)}) custom-call(f32[2,1024,1024]{2,1,0:T(8,128)S(1)} %get-tuple-element.19.refs_0_, f32[2,1024,1024]{2,1,0:T(8,128)S(1)} %get-tuple-element.20.refs_1_, f32[2,1024,1024]{2,1,0:T(8,128)S(1)} %get-tuple-element.21.refs_2_, f32[2,1024,1024]{2,1,0:T(8,128)S(1)} %get-tuple-element.22.refs_3_, ...), custom_call_target="tpu_custom_call" | custom-call | tf_op jit(solution)/shard_map/sweep/pallas_call | solution.py:359
  75.8 1.3 %collective-permute-start.10 = (f32[8,128]{1,0:T(8,128)S(1)}, f32[8,128]{1,0:T(8,128)S(1)}, u32[]{:S(2)}, u32[]{:S(2)}) collective-permute-start(f32[8,128]{1,0:T(8,128)S(1)} %get-tuple-element.24.refs_4_), channel_id=1, source_target_pairs={{0,1},{1,0},{2,3},{3,2},{4,5},{5,4},{6,7},{7,6},{8,9},{9,8},{10,11... | collective-permute-start | bytes 12296 | tf_op jit(solution)/shard_map/ppermute | solution.py:92
  77.2 1.2 %collective-permute-done.12.refs_7_ = f32[8,128]{1,0:T(8,128)S(1)} collective-permute-done((f32[8,128]{1,0:T(8,128)S(1)}, f32[8,128]{1,0:T(8,128)S(1)}, u32[]{:S(2)}, u32[]{:S(2)}) %collective-permute-start.12) | collective-permute-done | bytes 4128 | tf_op jit(solution)/shard_map/ppermute | solution.py:92
  78.3 0.6 collective-permute-done.11.refs_6_
  78.9 5.5 %sweep.3 = (f32[8,128]{1,0:T(8,128)S(1)}, f32[8,1,1024]{2,1,0:T(1,128)S(1)}) custom-call(f32[2,1024,1024]{2,1,0:T(8,128)S(1)} %get-tuple-element.19.refs_0_, f32[2,1024,1024]{2,1,0:T(8,128)S(1)} %get-tuple-element.20.refs_1_, f32[2,1024,1024]{2,1,0:T(8,128)S(1)} %get-tuple-element.21.refs_2_, f32[2,1024,1024]{2,1,0:T(8,128)S(1)} %get-tuple-element.22.refs_3_, ...), custom_call_target="tpu_custom_call" | custom-call | tf_op jit(solution)/shard_map/sweep/pallas_call | solution.py:359
  84.4 0.7 collective-permute-start.15
  85.1 0.6 collective-permute-start.14
  85.6 0.7 collective-permute-start.13
  86.3 1.2 %collective-permute-done.15.refs_7_ = f32[8,128]{1,0:T(8,128)S(1)} collective-permute-done((f32[8,128]{1,0:T(8,128)S(1)}, f32[8,128]{1,0:T(8,128)S(1)}, u32[]{:S(2)}, u32[]{:S(2)}) %collective-permute-start.15) | collective-permute-done | bytes 4128 | tf_op jit(solution)/shard_map/ppermute | solution.py:92
  87.5 1.2 %collective-permute-done.14.refs_6_ = f32[8,128]{1,0:T(8,128)S(1)} collective-permute-done((f32[8,128]{1,0:T(8,128)S(1)}, f32[8,128]{1,0:T(8,128)S(1)}, u32[]{:S(2)}, u32[]{:S(2)}) %collective-permute-start.14) | collective-permute-done | bytes 4128 | tf_op jit(solution)/shard_map/ppermute | solution.py:92
  88.7 3.3 %own_grad.1 = f32[128,128]{1,0:T(8,128)S(1)} custom-call(f32[2,1024,1024]{2,1,0:T(8,128)S(1)} %get-tuple-element.19.refs_0_, f32[2,1024,1024]{2,1,0:T(8,128)S(1)} %get-tuple-element.20.refs_1_, f32[2,1024,1024]{2,1,0:T(8,128)S(1)} %get-tuple-element.21.refs_2_, f32[2,1024,1024]{2,1,0:T(8,128)S(1)} %get-tuple-element.22.refs_3_, ...), custom_call_target="tpu_custom_call" | custom-call | tf_op jit(solution)/shard_map/own_grad/pallas_call | solution.py:377
  92.8 1.2 %collective-permute-start.16 = (f32[128,128]{1,0:T(8,128)S(1)}, f32[128,128]{1,0:T(8,128)S(1)}, u32[]{:S(2)}, u32[]{:S(2)}) collective-permute-start(f32[128,128]{1,0:T(8,128)S(1)} %own_grad.1), channel_id=1, source_target_pairs={{0,1},{1,0},{2,3},{3,2},{4,5},{5,4},{6,7},{7,6},{8,9},{9,8},{10,11... | collective-permute-start | bytes 196616 | tf_op jit(solution)/shard_map/ppermute | solution.py:92
  93.9 14.7 %proto_grad.1 = f32[16,8192]{1,0:T(8,128)} custom-call(f32[2,1024,1024]{2,1,0:T(8,128)S(1)} %get-tuple-element.19.refs_0_, f32[2,1024,1024]{2,1,0:T(8,128)S(1)} %get-tuple-element.20.refs_1_, f32[2,1024,1024]{2,1,0:T(8,128)S(1)} %get-tuple-element.21.refs_2_, f32[2,1024,1024]{2,1,0:T(8,128)S(1)} %get-tuple-element.22.refs_3_, ...), custom_call_target="tpu_custom_call" | custom-call | tf_op jit(solution)/shard_map/proto_grad/pallas_call | solution.py:377
  108.7 0.6 add_add_fusion
  (29 shorter events, 2.8 us)
Async XLA Ops:
  0.7 1.6 %copy-start = (bf16[128,8192]{1,0:T(8,128)(2,1)S(1)}, bf16[128,8192]{1,0:T(8,128)(2,1)}, u32[]{:S(2)}) copy-start(bf16[128,8192]{1,0:T(8,128)(2,1)} %refs_14_.3) | copy-start | bytes 6291460
  2.3 0.8 copy-start.2
  3.1 0.8 copy-start.3
  7.6 5.3 %collective-permute-start = (f32[1,136,128]{2,0,1:T(1,128)S(1)}, f32[1,136,128]{2,0,1:T(1,128)S(1)}, u32[]{:S(2)}, u32[]{:S(2)}) collective-permute-start(f32[1,136,128]{2,0,1:T(1,128)S(1)} %bitcast.5), channel_id=1, source_target_pairs={{0,4},{4,0},{8,12},{12,8},{16,20},{20,16},{24,28},{28,24},{1,5},{5... | collective-permute-start | bytes 208904 | tf_op jit(solution)/shard_map/ppermute | solution.py:92
  13.1 5.2 %collective-permute-start.1 = (f32[2,136,128]{2,0,1:T(2,128)S(1)}, f32[2,136,128]{2,0,1:T(2,128)S(1)}, u32[]{:S(2)}, u32[]{:S(2)}) collective-permute-start(f32[2,136,128]{2,0,1:T(2,128)S(1)} %pad_maximum_fusion.2), channel_id=1, source_target_pairs={{0,8},{4,12},{8,0},{12,4},{16,24},{20,28},{24,16},{28,20},{1,9},{5... | collective-permute-start | bytes 417800 | tf_op jit(solution)/shard_map/ppermute | solution.py:92
  18.4 13.4 %collective-permute-start.2 = (f32[4,136,128]{2,0,1:T(4,128)S(1)}, f32[4,136,128]{2,0,1:T(4,128)S(1)}, u32[]{:S(2)}, u32[]{:S(2)}) collective-permute-start(f32[4,136,128]{2,0,1:T(4,128)S(1)} %pad_maximum_fusion.1), channel_id=1, source_target_pairs={{0,16},{4,20},{8,24},{12,28},{16,0},{20,4},{24,8},{28,12},{1,17},{... | collective-permute-start | bytes 835592 | tf_op jit(solution)/shard_map/ppermute | solution.py:92
  32.1 2.3 %collective-permute-start.3 = (f32[8,136,128]{2,0,1:T(8,128)S(1)}, f32[8,136,128]{2,0,1:T(8,128)S(1)}, u32[]{:S(2)}, u32[]{:S(2)}) collective-permute-start(f32[8,136,128]{2,0,1:T(8,128)S(1)} %pad_maximum_fusion), channel_id=1, source_target_pairs={{0,1},{1,0},{2,3},{3,2},{4,5},{5,4},{6,7},{7,6},{8,9},{9,8},{10,11... | collective-permute-start | bytes 1671176 | tf_op jit(solution)/shard_map/ppermute | solution.py:92
  32.2 10.7 %collective-permute-start.6 = (f32[3,8,128]{2,1,0:T(8,128)S(1)}, f32[3,8,128]{2,1,0:T(8,128)S(1)}, u32[]{:S(2)}, u32[]{:S(2)}) collective-permute-start(f32[3,8,128]{2,1,0:T(8,128)S(1)} %slice_bitcast_fusion.refs_4_.refs_8_), channel_id=1, source_target_pairs={{0,3},{1,2},{2,1},{3,0},{4,7},{5,6},{6,5},{7,4},{8,11},{9,10},{10,... | collective-permute-start | bytes 36872 | tf_op jit(solution)/shard_map/ppermute | solution.py:92
  33.8 9.1 %collective-permute-start.5 = (f32[3,8,128]{2,1,0:T(8,128)S(1)}, f32[3,8,128]{2,1,0:T(8,128)S(1)}, u32[]{:S(2)}, u32[]{:S(2)}) collective-permute-start(f32[3,8,128]{2,1,0:T(8,128)S(1)} %slice_bitcast_fusion.refs_4_.refs_8_), channel_id=1, source_target_pairs={{0,2},{1,3},{2,0},{3,1},{4,6},{5,7},{6,4},{7,5},{8,10},{9,11},{10,... | collective-permute-start | bytes 36872 | tf_op jit(solution)/shard_map/ppermute | solution.py:92
  34.3 8.6 %collective-permute-start.4 = (f32[3,8,128]{2,1,0:T(8,128)S(1)}, f32[3,8,128]{2,1,0:T(8,128)S(1)}, u32[]{:S(2)}, u32[]{:S(2)}) collective-permute-start(f32[3,8,128]{2,1,0:T(8,128)S(1)} %slice_bitcast_fusion.refs_4_.refs_8_), channel_id=1, source_target_pairs={{0,1},{1,0},{2,3},{3,2},{4,5},{5,4},{6,7},{7,6},{8,9},{9,8},{10,11... | collective-permute-start | bytes 36872 | tf_op jit(solution)/shard_map/ppermute | solution.py:92
  34.6 1.6 %copy-start.1 = (bf16[128,8192]{1,0:T(8,128)(2,1)S(1)}, bf16[128,8192]{1,0:T(8,128)(2,1)}, u32[]{:S(2)}) copy-start(bf16[128,8192]{1,0:T(8,128)(2,1)} %refs_14_.3) | copy-start | bytes 6291460
  64.2 3.0 %collective-permute-start.9 = (f32[8,128]{1,0:T(8,128)S(1)}, f32[8,128]{1,0:T(8,128)S(1)}, u32[]{:S(2)}, u32[]{:S(2)}) collective-permute-start(f32[8,128]{1,0:T(8,128)S(1)} %get-tuple-element.23.refs_4_), channel_id=1, source_target_pairs={{0,3},{1,2},{2,1},{3,0},{4,7},{5,6},{6,5},{7,4},{8,11},{9,10},{10,... | collective-permute-start | bytes 12296 | tf_op jit(solution)/shard_map/ppermute | solution.py:92
  65.8 3.6 %collective-permute-start.8 = (f32[8,128]{1,0:T(8,128)S(1)}, f32[8,128]{1,0:T(8,128)S(1)}, u32[]{:S(2)}, u32[]{:S(2)}) collective-permute-start(f32[8,128]{1,0:T(8,128)S(1)} %get-tuple-element.23.refs_4_), channel_id=1, source_target_pairs={{0,2},{1,3},{2,0},{3,1},{4,6},{5,7},{6,4},{7,5},{8,10},{9,11},{10,... | collective-permute-start | bytes 12296 | tf_op jit(solution)/shard_map/ppermute | solution.py:92
  66.3 3.1 %collective-permute-start.7 = (f32[8,128]{1,0:T(8,128)S(1)}, f32[8,128]{1,0:T(8,128)S(1)}, u32[]{:S(2)}, u32[]{:S(2)}) collective-permute-start(f32[8,128]{1,0:T(8,128)S(1)} %get-tuple-element.23.refs_4_), channel_id=1, source_target_pairs={{0,1},{1,0},{2,3},{3,2},{4,5},{5,4},{6,7},{7,6},{8,9},{9,8},{10,11... | collective-permute-start | bytes 12296 | tf_op jit(solution)/shard_map/ppermute | solution.py:92
  75.3 3.0 %collective-permute-start.12 = (f32[8,128]{1,0:T(8,128)S(1)}, f32[8,128]{1,0:T(8,128)S(1)}, u32[]{:S(2)}, u32[]{:S(2)}) collective-permute-start(f32[8,128]{1,0:T(8,128)S(1)} %get-tuple-element.24.refs_4_), channel_id=1, source_target_pairs={{0,3},{1,2},{2,1},{3,0},{4,7},{5,6},{6,5},{7,4},{8,11},{9,10},{10,... | collective-permute-start | bytes 12296 | tf_op jit(solution)/shard_map/ppermute | solution.py:92
  75.3 3.6 %collective-permute-start.11 = (f32[8,128]{1,0:T(8,128)S(1)}, f32[8,128]{1,0:T(8,128)S(1)}, u32[]{:S(2)}, u32[]{:S(2)}) collective-permute-start(f32[8,128]{1,0:T(8,128)S(1)} %get-tuple-element.24.refs_4_), channel_id=1, source_target_pairs={{0,2},{1,3},{2,0},{3,1},{4,6},{5,7},{6,4},{7,5},{8,10},{9,11},{10,... | collective-permute-start | bytes 12296 | tf_op jit(solution)/shard_map/ppermute | solution.py:92
  75.8 3.1 %collective-permute-start.10 = (f32[8,128]{1,0:T(8,128)S(1)}, f32[8,128]{1,0:T(8,128)S(1)}, u32[]{:S(2)}, u32[]{:S(2)}) collective-permute-start(f32[8,128]{1,0:T(8,128)S(1)} %get-tuple-element.24.refs_4_), channel_id=1, source_target_pairs={{0,1},{1,0},{2,3},{3,2},{4,5},{5,4},{6,7},{7,6},{8,9},{9,8},{10,11... | collective-permute-start | bytes 12296 | tf_op jit(solution)/shard_map/ppermute | solution.py:92
  84.4 3.1 %collective-permute-start.15 = (f32[8,128]{1,0:T(8,128)S(1)}, f32[8,128]{1,0:T(8,128)S(1)}, u32[]{:S(2)}, u32[]{:S(2)}) collective-permute-start(f32[8,128]{1,0:T(8,128)S(1)} %get-tuple-element.25.refs_4_), channel_id=1, source_target_pairs={{0,3},{1,2},{2,1},{3,0},{4,7},{5,6},{6,5},{7,4},{8,11},{9,10},{10,... | collective-permute-start | bytes 12296 | tf_op jit(solution)/shard_map/ppermute | solution.py:92
  85.1 3.6 %collective-permute-start.14 = (f32[8,128]{1,0:T(8,128)S(1)}, f32[8,128]{1,0:T(8,128)S(1)}, u32[]{:S(2)}, u32[]{:S(2)}) collective-permute-start(f32[8,128]{1,0:T(8,128)S(1)} %get-tuple-element.25.refs_4_), channel_id=1, source_target_pairs={{0,2},{1,3},{2,0},{3,1},{4,6},{5,7},{6,4},{7,5},{8,10},{9,11},{10,... | collective-permute-start | bytes 12296 | tf_op jit(solution)/shard_map/ppermute | solution.py:92
  85.6 3.0 %collective-permute-start.13 = (f32[8,128]{1,0:T(8,128)S(1)}, f32[8,128]{1,0:T(8,128)S(1)}, u32[]{:S(2)}, u32[]{:S(2)}) collective-permute-start(f32[8,128]{1,0:T(8,128)S(1)} %get-tuple-element.25.refs_4_), channel_id=1, source_target_pairs={{0,1},{1,0},{2,3},{3,2},{4,5},{5,4},{6,7},{7,6},{8,9},{9,8},{10,11... | collective-permute-start | bytes 12296 | tf_op jit(solution)/shard_map/ppermute | solution.py:92
  92.0 16.7 %collective-permute-start.18 = (f32[128,128]{1,0:T(8,128)S(1)}, f32[128,128]{1,0:T(8,128)S(1)}, u32[]{:S(2)}, u32[]{:S(2)}) collective-permute-start(f32[128,128]{1,0:T(8,128)S(1)} %own_grad.1), channel_id=1, source_target_pairs={{0,3},{1,2},{2,1},{3,0},{4,7},{5,6},{6,5},{7,4},{8,11},{9,10},{10,... | collective-permute-start | bytes 196616 | tf_op jit(solution)/shard_map/ppermute | solution.py:92
  92.4 16.3 %collective-permute-start.17 = (f32[128,128]{1,0:T(8,128)S(1)}, f32[128,128]{1,0:T(8,128)S(1)}, u32[]{:S(2)}, u32[]{:S(2)}) collective-permute-start(f32[128,128]{1,0:T(8,128)S(1)} %own_grad.1), channel_id=1, source_target_pairs={{0,2},{1,3},{2,0},{3,1},{4,6},{5,7},{6,4},{7,5},{8,10},{9,11},{10,... | collective-permute-start | bytes 196616 | tf_op jit(solution)/shard_map/ppermute | solution.py:92
  92.8 15.9 %collective-permute-start.16 = (f32[128,128]{1,0:T(8,128)S(1)}, f32[128,128]{1,0:T(8,128)S(1)}, u32[]{:S(2)}, u32[]{:S(2)}) collective-permute-start(f32[128,128]{1,0:T(8,128)S(1)} %own_grad.1), channel_id=1, source_target_pairs={{0,1},{1,0},{2,3},{3,2},{4,5},{5,4},{6,7},{7,6},{8,9},{9,8},{10,11... | collective-permute-start | bytes 196616 | tf_op jit(solution)/shard_map/ppermute | solution.py:92

commit v2 on v1

v2 whole, which is shorter than its diff:
```python
import math

import jax
import jax.numpy as jnp
from jax import lax
from jax.experimental import pallas as pl
from jax.experimental.pallas import tpu as pltpu
from jax.sharding import PartitionSpec as P

ITERS = 3

teacher_temp = 0.07
student_temp = 0.1

LOG2E = math.log2(math.e)
T_EXP = LOG2E / teacher_temp
S_EXP = LOG2E / student_temp

LANES = 128
SUB = 8
PARTS = 4
STAT_ROWS = 8
KERNEL_BYTES = 32 << 20


def combined_all(value, axis, combine):
    everything = jax.tree.map(lambda part: lax.all_gather(part, axis), value)
    leading = jax.tree.map(lambda part: part[0], everything)

    def step(k, so_far):
        return combine(so_far, jax.tree.map(lambda part: part[k], everything))

    return lax.fori_loop(1, lax.axis_size(axis), step, leading)


def divided_logits(features, prototypes, divisor):
    return jnp.dot(features, prototypes, preferred_element_type=jnp.float32) / divisor


def combine_stats(earlier, later):
    teacher_peak = jnp.maximum(earlier[0], later[0])
    student_peak = jnp.maximum(earlier[1], later[1])
    merged_total = earlier[2] * jnp.exp(earlier[1] - student_peak) + later[2] * jnp.exp(
        later[1] - student_peak
    )
    return (teacher_peak, student_peak, merged_total)


def split_crops(teacher_feat, student_feat, proto_weight):
    teacher_scores = divided_logits(teacher_feat, proto_weight, teacher_temp)
    student_scores = divided_logits(student_feat, proto_weight, student_temp)
    local_teacher = jnp.max(teacher_scores, axis=1)
    local_student = jnp.max(student_scores, axis=1)
    local_total = jnp.sum(jnp.exp(student_scores - local_student[:, None]), axis=1)
    teacher_peak, student_peak, student_total = combined_all(
        (local_teacher, local_student, local_total), "proto", combine_stats
    )
    kernel = jnp.exp(teacher_scores - teacher_peak[:, None])
    row_scale = jnp.ones((teacher_feat.shape[0],), jnp.float32)
    for sweep in range(ITERS):
        col_part = jnp.sum(kernel * row_scale[:, None], axis=0)
        col_scale = 1.0 / lax.psum(col_part, "dp")
        row_part = jnp.sum(kernel * col_scale[None, :], axis=1)
        row_scale = 1.0 / lax.psum(row_part, "proto")
    target = kernel * row_scale[:, None] * col_scale[None, :]
    student_probs = jnp.exp(student_scores - student_peak[:, None]) / student_total[:, None]
    grad_scores = ((student_probs - target) / student_temp).astype(jnp.bfloat16)
    input_part = lax.dot_general(
        grad_scores, proto_weight, (((1,), (1,)), ((), ())), preferred_element_type=jnp.float32
    )
    feature_grad = lax.psum(input_part, "proto")
    proto_grad = lax.psum_scatter(
        lax.dot_general(
            student_feat, grad_scores, (((0,), (0,)), ((), ())), preferred_element_type=jnp.float32
        ),
        "dp",
        scatter_dimension=0,
        tiled=True,
    )
    return (proto_grad, feature_grad)


def vmem():
    return pl.BlockSpec(memory_space=pltpu.VMEM)


def smem():
    return pl.BlockSpec(memory_space=pltpu.SMEM)


def swap(x, axis, bit):
    return lax.ppermute(x, axis, [(i, i ^ bit) for i in range(lax.axis_size(axis))])


def fold(parts, op):
    parts = list(parts)
    while len(parts) > 1:
        parts = [op(*parts[k : k + 2]) if k + 1 < len(parts) else parts[k] for k in range(0, len(parts), 2)]
    return parts[0]


def lane_tiles(x):
    return [x[:, k : k + LANES] for k in range(0, x.shape[1], LANES)]


def spread_rows(flat, out_ref):
    for j in range(flat.shape[0]):
        wide = jnp.broadcast_to(flat[j : j + 1, :], (LANES, LANES))
        out_ref[j * LANES : (j + 1) * LANES, :] = wide.T


def gather_rows(acc_ref):
    n = acc_ref.shape[0] // LANES
    rows = [
        jnp.sum(acc_ref[j * LANES : (j + 1) * LANES, :].T, axis=0, keepdims=True) for j in range(n)
    ]
    return jnp.concatenate(rows, axis=0)


def row_max(acc):
    return [
        jnp.max(acc[k : k + LANES, :].T, axis=0, keepdims=True) for k in range(0, acc.shape[0], LANES)
    ]


def own_body(place_ref, s_ref, w_hbm, out_ref, w_ref, scores_ref, sems):
    rows = s_ref.shape[0]
    half = rows // 2
    count, unused, width = scores_ref.shape
    copies = []
    for j in range(count):
        at = pl.ds(j * width, width)
        copies.append(pltpu.make_async_copy(w_hbm.at[:, at], w_ref.at[:, at], sems.at[j]))
        copies[-1].start()
    s = s_ref[...]
    s_max = None
    for j in range(count):
        copies[j].wait()
        b = jnp.dot(s, w_ref[:, j * width : (j + 1) * width], preferred_element_type=jnp.float32)
        scores_ref[j] = b
        top = fold(lane_tiles(b), jnp.maximum)
        s_max = top if s_max is None else jnp.maximum(s_max, top)
    s_col = jnp.broadcast_to(jnp.max(s_max, axis=1, keepdims=True), (rows, LANES))

    def total(j, so_far):
        e = [jnp.exp2((x - s_col) * S_EXP) for x in lane_tiles(scores_ref[j])]
        return so_far + fold(e, jnp.add)

    s_sum = lax.fori_loop(0, count, total, jnp.zeros((rows, LANES), jnp.float32))
    first = pl.multiple_of(place_ref[0] * half, half)
    out_ref[0:half, :] = s_ref[pl.ds(first, half), :].astype(jnp.float32)
    stats = [
        jnp.max(s_max.T, axis=0, keepdims=True),
        jnp.sum(s_sum.T, axis=0, keepdims=True),
        jnp.zeros((STAT_ROWS - 2, LANES), jnp.float32),
    ]
    out_ref[half:, :] = jnp.concatenate(stats, axis=0)


def join_halves(core, mine, other, out_ref, first):
    half = LANES // 2
    for j in range(mine.shape[0]):
        base = (first + j) * LANES
        a = pl.multiple_of(base + core * half, half)
        b = pl.multiple_of(base + (1 - core) * half, half)
        out_ref[pl.ds(a, half), :] = mine[j, 0:half, :].astype(jnp.bfloat16)
        out_ref[pl.ds(b, half), :] = other[j, 0:half, :].astype(jnp.bfloat16)


def scores_body(place_ref, mine_ref, other_ref, w_ref, *refs):
    k_refs = refs[:PARTS]
    max_ref, t_scr, acc_ref = refs[PARTS:]
    join_halves(place_ref[0], mine_ref, other_ref, t_scr, 0)
    t = t_scr[...]
    per, unused, width = k_refs[0].shape
    acc_ref[...] = jnp.full(acc_ref.shape, -jnp.inf, jnp.float32)
    for p in range(PARTS):

        def block(j, unused, p=p):
            start = pl.multiple_of((p * per + j) * width, width)
            s = jnp.dot(t, w_ref[:, pl.ds(start, width)], preferred_element_type=jnp.float32) * T_EXP
            k_refs[p][j] = s
            acc_ref[...] = jnp.maximum(acc_ref[...], fold(lane_tiles(s), jnp.maximum))
            return 0

        lax.fori_loop(0, per, block, 0)
    max_ref[...] = jnp.concatenate(row_max(acc_ref), axis=0)


def sweep_body(first, n_in, n_extra, *refs):
    k_refs, refs = refs[:PARTS], refs[PARTS:]
    in_refs, refs = refs[:n_in], refs[n_in:]
    extra_refs, refs = refs[:n_extra], refs[n_extra:]
    if first:
        k_refs, refs = refs[:PARTS], refs[PARTS:]
    o_ref, c_ref, r_scr, acc_ref = refs
    per, rows, width = k_refs[0].shape
    n = rows // LANES
    if first:
        spread_rows(fold([x[...] for x in in_refs], jnp.maximum), r_scr)
    else:
        spread_rows(1.0 / fold([x[0:n, :] for x in in_refs], jnp.add), r_scr)
    acc_ref[...] = jnp.zeros_like(acc_ref)
    tiles = width // LANES
    unroll = 32
    steps = rows // SUB // unroll

    for p in range(PARTS):
        k_ref = k_refs[p]

        def block(j, unused, p=p, k_ref=k_ref):
            def down(i, sums):
                base = pl.multiple_of(i * (unroll * SUB), unroll * SUB)
                for u in range(unroll):
                    at = pl.ds(base + u * SUB, SUB)
                    rb = r_scr[at, :]
                    new = []
                    for q in range(tiles):
                        x = k_ref[j, at, q * LANES : (q + 1) * LANES]
                        if first:
                            x = jnp.exp2(x - rb)
                            k_ref[j, at, q * LANES : (q + 1) * LANES] = x
                        else:
                            x = x * rb
                        new.append(sums[q] + x)
                    sums = tuple(new)
                return sums

            zero = jnp.zeros((SUB, LANES), jnp.float32)
            sums = lax.fori_loop(0, steps, down, (zero,) * tiles)
            cols = [1.0 / jnp.sum(x, axis=0, keepdims=True) for x in sums]
            for q in range(tiles):
                c_ref[p * per + j, :, q * LANES : (q + 1) * LANES] = cols[q]
            wide = [jnp.broadcast_to(x, (SUB, LANES)) for x in cols]

            def across(i, unused):
                base = pl.multiple_of(i * (unroll * SUB), unroll * SUB)
                for u in range(unroll):
                    at = pl.ds(base + u * SUB, SUB)
                    x = [k_ref[j, at, q * LANES : (q + 1) * LANES] * wide[q] for q in range(tiles)]
                    acc_ref[at, :] = acc_ref[at, :] + fold(x, jnp.add)
                return 0

            lax.fori_loop(0, steps, across, 0)
            return 0

        lax.fori_loop(0, per, block, 0)
    o_ref[0:n, :] = gather_rows(acc_ref)
    if n_extra:
        half = LANES // 2
        for k in range(2):
            rows_k = [x[j, half + k : half + k + 1, :] for x in extra_refs for j in range(x.shape[0])]
            o_ref[(k + 1) * n : (k + 2) * n, :] = jnp.concatenate(rows_k, axis=0)


def grad_tiles(k_ref, j, first, last, c_row, s_scr, g_scr, r_scr, b_scr, rows):
    tiles = (last - first) // LANES
    step = 2 * SUB
    c = [jnp.broadcast_to(c_row[:, q * LANES : (q + 1) * LANES], (step, LANES)) for q in range(tiles)]
    for i in range(0, rows, step):
        at = slice(i, i + step)
        rb, bb = r_scr[at, :], b_scr[at, :]
        for q in range(tiles):
            lanes = slice(q * LANES, (q + 1) * LANES)
            probs = jnp.exp2(s_scr[at, lanes] * S_EXP - bb)
            k = k_ref[j, at, first + q * LANES : first + (q + 1) * LANES]
            g_scr[at, lanes] = (probs - k * rb * c[q]).astype(jnp.bfloat16)


def final_body(n_in, own_only, *refs):
    k_refs, refs = refs[:PARTS], refs[PARTS:]
    row_refs, refs = refs[:n_in], refs[n_in:]
    stat_refs, refs = refs[:n_in], refs[n_in:]
    near_ref, near_other_ref, far_ref, far_other_ref, c_ref, w_ref, place_ref, out_ref = refs[:8]
    f_scr, r_scr, b_scr, *pairs = refs[8:]
    rows = r_scr.shape[0]
    used = rows // LANES
    n = stat_refs[0].shape[0] // 3
    row_scale = 1.0 / fold([x[...] for x in row_refs], jnp.add)
    peak = fold([x[n : 2 * n, :] for x in stat_refs], jnp.maximum)
    total = fold(
        [x[2 * n :, :] * jnp.exp2((x[n : 2 * n, :] - peak) * S_EXP) for x in stat_refs], jnp.add
    )
    shift = peak * S_EXP + jnp.log(total * student_temp) * LOG2E
    spread_rows((row_scale * (1.0 / student_temp))[:used], r_scr)
    spread_rows(shift[:used], b_scr)
    core = place_ref[0]
    if own_only:
        join_halves(core, near_ref.at[0:1], near_other_ref.at[0:1], f_scr, 0)
        out_ref[...] = jnp.zeros_like(out_ref)
    else:
        join_halves(core, near_ref, near_other_ref, f_scr, 0)
        join_halves(core, far_ref, far_other_ref, f_scr, near_ref.shape[0])
    s = f_scr[...]
    if not own_only:
        shape = (out_ref.shape[0], s.shape[1])
        wanted = lax.broadcasted_iota(jnp.int32, shape, 0) + place_ref[1] * shape[0]
        pick = (lax.broadcasted_iota(jnp.int32, shape, 1) == wanted).astype(jnp.float32)
        picked = lax.dot_general(
            pick.astype(jnp.bfloat16), s, (((1,), (1,)), ((), ())), preferred_element_type=jnp.float32
        ).astype(jnp.bfloat16)
    per, unused, width = k_refs[0].shape
    tile = pairs[0].shape[1]
    for p in range(PARTS):

        def block(j, unused, p=p):
            start = pl.multiple_of((p * per + j) * width, width)
            for q in range(width // tile):
                s_scr, g_scr = pairs[2 * (q % (len(pairs) // 2)) :][:2]
                at = pl.ds(start + q * tile, tile)
                w = w_ref[:, at]
                s_scr[...] = jnp.dot(s, w, preferred_element_type=jnp.float32)
                c_row = c_ref[p * per + j, :, q * tile : (q + 1) * tile]
                grad_tiles(
                    k_refs[p], j, q * tile, (q + 1) * tile, c_row, s_scr, g_scr, r_scr, b_scr, rows
                )
                if own_only:
                    out_ref[...] += lax.dot_general(
                        g_scr[...], w, (((1,), (1,)), ((), ())), preferred_element_type=jnp.float32
                    )
                else:
                    out_ref[:, at] = jnp.dot(picked, g_scr[...], preferred_element_type=jnp.float32)
            return 0

        lax.fori_loop(0, per, block, 0)


def all_crops(teacher_feat, student_feat, proto_weight):
    own, depth = teacher_feat.shape
    n_dp = lax.axis_size("dp")
    n_proto = lax.axis_size("proto")
    rows = own * n_dp
    n = rows // LANES
    cols = proto_weight.shape[1]
    width = 1024
    per = cols // width // PARTS
    half = own // 2
    f32 = jnp.float32
    params = pltpu.CompilerParams(vmem_limit_bytes=16 << 20)
    place = jnp.stack([lax.axis_index("proto") % 2, lax.axis_index("dp")]).astype(jnp.int32)

    def everyone(x):
        return [x] + [swap(x, "proto", k) for k in range(1, n_proto)]

    def spread(x, bits):
        for bit in bits:
            x = jnp.concatenate([x, swap(x, "dp", bit)], axis=0)
        return x

    bits = [1 << k for k in range(n_dp.bit_length() - 1)][::-1]
    teacher_half = lax.dynamic_slice_in_dim(teacher_feat, place[0] * half, half, 0).astype(f32)
    mine = spread(teacher_half[None], bits)
    other = swap(mine, "proto", 1)

    chunk = 1024
    student_part, weight = pl.pallas_call(
        own_body,
        out_shape=(
            jax.ShapeDtypeStruct((half + STAT_ROWS, depth), f32),
            pltpu.VMEM(proto_weight.shape, proto_weight.dtype),
        ),
        in_specs=[smem(), vmem(), pl.BlockSpec(memory_space=pl.ANY)],
        out_specs=(vmem(), vmem()),
        scratch_shapes=[
            pltpu.VMEM((cols // chunk, own, chunk), f32),
            pltpu.SemaphoreType.DMA((cols // chunk,)),
        ],
        compiler_params=params,
        name="own_stats",
    )(place, student_feat, proto_weight)
    near = spread(student_part[None], bits[:-1])

    k_shape = pltpu.VMEM((per, rows, width), f32)
    flat = jax.ShapeDtypeStruct((n, LANES), f32)
    *kernel, local_peak = pl.pallas_call(
        scores_body,
        out_shape=(k_shape,) * PARTS + (flat,),
        in_specs=[smem(), vmem(), vmem(), vmem()],
        out_specs=(vmem(),) * (PARTS + 1),
        scratch_shapes=[pltpu.VMEM((rows, depth), jnp.bfloat16), pltpu.VMEM((rows, LANES), f32)],
        compiler_params=params,
        name="scores",
    )(place, mine, other, weight)

    def sweep(kernel, ins, extra, first):
        outs = (
            jax.ShapeDtypeStruct((3 * n if extra else n, LANES), f32),
            jax.ShapeDtypeStruct((cols // width, 1, width), f32),
        )
        kept = (k_shape,) * PARTS if first else ()
        result = pl.pallas_call(
            lambda *refs: sweep_body(first, len(ins), len(extra), *refs),
            out_shape=kept + outs,
            in_specs=[vmem()] * (PARTS + len(ins) + len(extra)),
            out_specs=(vmem(),) * (len(kept) + 2),
            scratch_shapes=[pltpu.VMEM((rows, LANES), f32), pltpu.VMEM((rows, LANES), f32)],
            input_output_aliases={k: k for k in range(len(kept))},
            compiler_params=params,
            name="sweep_first" if first else "sweep",
        )(*kernel, *ins, *extra)
        return (result[:PARTS] if first else kernel), result[-2], result[-1]

    ins = everyone(local_peak)
    far = swap(near, "dp", bits[-1])
    near_other = swap(near, "proto", 1)
    far_other = swap(far, "proto", 1)
    stats = None
    for it in range(ITERS):
        extra = (near, far) if it == ITERS - 2 else ()
        kernel, row_part, col_scale = sweep(kernel, ins, extra, it == 0)
        ins = everyone(row_part)
        if extra:
            stats = ins

    def final(own_only, shape, crops, tile, name):
        scratch = [pltpu.VMEM((crops, depth), jnp.bfloat16)] + [pltpu.VMEM((crops, LANES), f32)] * 2
        for unused in range(4):
            scratch += [pltpu.VMEM((crops, tile), f32), pltpu.VMEM((crops, tile), jnp.bfloat16)]
        return pl.pallas_call(
            lambda *refs: final_body(len(ins), own_only, *refs),
            out_shape=jax.ShapeDtypeStruct(shape, f32),
            in_specs=[vmem()] * (PARTS + 2 * len(ins) + 6) + [smem()],
            out_specs=vmem(),
            scratch_shapes=scratch,
            compiler_params=params,
            name=name,
        )(*kernel, *ins, *stats, near, near_other, far, far_other, col_scale, weight, place)

    parts = everyone(final(True, (own, depth), own, 256, "own_grad"))
    proto_grad = final(False, (depth // n_dp, cols), rows, 256, "proto_grad")
    feature_grad = fold(parts, jnp.add)
    return (proto_grad, feature_grad)


def solution(mesh):
    n_dp = mesh.shape["dp"]
    n_proto = mesh.shape["proto"]

    def shards(teacher_feat, student_feat, proto_weight):
        own, depth = teacher_feat.shape
        cols = proto_weight.shape[1]
        fits = (
            own * n_dp * cols * 4 <= KERNEL_BYTES
            and own == LANES
            and depth == LANES
            and cols % (PARTS * 1024) == 0
            and n_dp & (n_dp - 1) == 0
            and n_proto & (n_proto - 1) == 0
            and 2 <= n_proto <= 8
            and depth % (n_dp * SUB) == 0
        )
        plan = all_crops if fits else split_crops
        return plan(teacher_feat, student_feat, proto_weight)

    return jax.shard_map(
        shards,
        mesh=mesh,
        in_specs=(P("dp", None), P("dp", None), P(None, "proto")),
        out_specs=(P("dp", "proto"), P("dp", None)),
        check_vma=False,
    )
```

time: 110 us -> 104 us (0.945)
  waiting for transfers between devices: 22.9 us -> 16.6 us
  starting transfers between devices: 18.4 us -> 21.4 us
  local copies, waits for them, and re-layouts: 4.91 us -> 2.35 us
    ppermute x19 -> x24, waiting for transfers between devices: 22.9 us -> 16.6 us  [swap(): lax.ppermute(x, axis, [(i, i ^ bit) for i in range(lax.axis_size(axis))])]
    pallas_call x5, Pallas kernels: 43.1 us -> 37.1 us  [the longest x3 27.2 us: sweep(): pl.pallas_call(lambda *refs: sweep_body(first, len(ins), len(extra), *ref...]
    pallas_call x2, Pallas kernels: 18 us -> 23.7 us  [final(): pl.pallas_call(lambda *refs: final_body(len(ins), own_only, *refs), out_s...]
    ppermute x19 -> x24, starting transfers between devices: 18.4 us -> 21.4 us  [swap(): lax.ppermute(x, axis, [(i, i ^ bit) for i in range(lax.axis_size(axis))])]
    unnamed x8 -> x4, local copies, waits for them, and re-layouts: 4.69 us -> 2.35 us
  transfers between devices with their start and end apart: 19 -> 24, of which waited for: 9 -> 11; matrix products, arithmetic and copies ran while one was open for 0% -> 0% of each run, Pallas kernels for 20% -> 55%
where the time goes in v2:
time: 104 us; the launch traced here: 103 us
  Pallas kernels  60.7 us (58%)
  starting transfers between devices  21.4 us (21%)
  waiting for transfers between devices  16.6 us (16%)
  local copies, waits for them, and re-layouts  2.35 us (2%)
  other arithmetic  1.5 us (1%)
    pallas_call x3, Pallas kernels, sweep(): pl.pallas_call(lambda *refs: sweep_body(first, len(ins), len(extra), *ref...  27.2 us
    pallas_call x2, Pallas kernels, final(): pl.pallas_call(lambda *refs: final_body(len(ins), own_only, *refs), out_s...  23.7 us
    ppermute x24, starting transfers between devices, swap(): lax.ppermute(x, axis, [(i, i ^ bit) for i in range(lax.axis_size(axis))])  21.4 us
    ppermute x24, waiting for transfers between devices, swap(): lax.ppermute(x, axis, [(i, i ^ bit) for i in range(lax.axis_size(axis))])  16.6 us
    pallas_call x1, Pallas kernels, all_crops(): pl.pallas_call(scores_body, out_shape=(k_shape,) * PARTS + (flat,), in_sp...  6.43 us
    pallas_call x1, Pallas kernels, all_crops(): pl.pallas_call(own_body, out_shape=(jax.ShapeDtypeStruct((half + STAT_ROW...  3.38 us
    unnamed x4, local copies, waits for them, and re-layouts  2.35 us
  transfers between devices with their start and end apart: 24, of which 11 were waited for; matrix products, arithmetic and copies ran while one was open for 0% of the time, Pallas kernels for 55%

profile of v2, /device:TPU:0, one launch (start us, length us, event | category | flops | bytes accessed | tf_op | source)
XLA Modules:
  0.0 103.3 jit_solution(9275526366305475463)
XLA Ops:
  0.6 0.7 bitcast_convert_fusion
  1.4 4.1 %collective-permute-start = (f32[1,64,128]{2,1,0:T(8,128)S(1)}, f32[1,64,128]{2,1,0:T(8,128)S(1)}, u32[]{:S(2)}, u32[]{:S(2)}) collective-permute-start(f32[1,64,128]{2,1,0:T(8,128)S(1)} %bitcast_convert_fusion), channel_id=1, source_target_pairs={{0,16},{4,20},{8,24},{12,28},{16,0},{20,4},{24,8},{28,12},{1,17},{... | collective-permute-start | bytes 98312 | tf_op jit(solution)/shard_map/ppermute | solution.py:92
  5.5 1.6 %copy-done = bf16[128,8192]{1,0:T(8,128)(2,1)S(1)} copy-done((bf16[128,8192]{1,0:T(8,128)(2,1)S(1)}, bf16[128,8192]{1,0:T(8,128)(2,1)}, u32[]{:S(2)}) %copy-start) | copy-done | bytes 2097176
  7.1 0.8 copy-done.1
  7.9 3.4 %own_stats.1 = (f32[72,128]{1,0:T(8,128)S(1)}, bf16[128,8192]{1,0:T(8,128)(2,1)S(1)}) custom-call(s32[2]{0:T(128)S(1)} %pad_add_fusion.place_ref.refs_18_, bf16[128,128]{1,0:T(8,128)(2,1)S(1)} %copy-done.1, bf16[128,8192]{1,0:T(8,128)(2,1)S(1)} %copy-done), custom_call_target="tpu_custom_call" | custom-call | tf_op jit(solution)/shard_map/own_stats/pallas_call | solution.py:356
  11.4 1.9 %collective-permute-start.1 = (f32[2,64,128]{2,1,0:T(8,128)S(1)}, f32[2,64,128]{2,1,0:T(8,128)S(1)}, u32[]{:S(2)}, u32[]{:S(2)}) collective-permute-start(f32[2,64,128]{2,1,0:T(8,128)S(1)} %pad_maximum_fusion.4), channel_id=1, source_target_pairs={{0,8},{4,12},{8,0},{12,4},{16,24},{20,28},{24,16},{28,20},{1,9},{5... | collective-permute-start | bytes 196616 | tf_op jit(solution)/shard_map/ppermute | solution.py:92
  13.3 2.9 %collective-permute-done.10 = f32[1,72,128]{2,1,0:T(8,128)S(1)} collective-permute-done((f32[1,72,128]{2,1,0:T(8,128)S(1)}, f32[1,72,128]{2,1,0:T(8,128)S(1)}, u32[]{:S(2)}, u32[]{:S(2)}) %collective-permute-start.10) | collective-permute-done | bytes 36896 | tf_op jit(solution)/shard_map/ppermute | solution.py:92
  16.2 1.7 %collective-permute-start.11 = (f32[2,72,128]{2,1,0:T(8,128)S(1)}, f32[2,72,128]{2,1,0:T(8,128)S(1)}, u32[]{:S(2)}, u32[]{:S(2)}) collective-permute-start(f32[2,72,128]{2,1,0:T(8,128)S(1)} %pad_maximum_fusion.3), channel_id=1, source_target_pairs={{0,8},{4,12},{8,0},{12,4},{16,24},{20,28},{24,16},{28,20},{1,9},{5... | collective-permute-start | bytes 221192 | tf_op jit(solution)/shard_map/ppermute | solution.py:92
  17.9 1.5 %collective-permute-start.2 = (f32[4,64,128]{2,1,0:T(8,128)S(1)}, f32[4,64,128]{2,1,0:T(8,128)S(1)}, u32[]{:S(2)}, u32[]{:S(2)}) collective-permute-start(f32[4,64,128]{2,1,0:T(8,128)S(1)} %pad_maximum_fusion.2), channel_id=1, source_target_pairs={{0,4},{4,0},{8,12},{12,8},{16,20},{20,16},{24,28},{28,24},{1,5},{5... | collective-permute-start | bytes 393224 | tf_op jit(solution)/shard_map/ppermute | solution.py:92
  19.5 1.1 %collective-permute-done.11 = f32[2,72,128]{2,1,0:T(8,128)S(1)} collective-permute-done((f32[2,72,128]{2,1,0:T(8,128)S(1)}, f32[2,72,128]{2,1,0:T(8,128)S(1)}, u32[]{:S(2)}, u32[]{:S(2)}) %collective-permute-start.11) | collective-permute-done | bytes 73760 | tf_op jit(solution)/shard_map/ppermute | solution.py:92
  20.6 1.7 %collective-permute-start.12 = (f32[4,72,128]{2,1,0:T(8,128)S(1)}, f32[4,72,128]{2,1,0:T(8,128)S(1)}, u32[]{:S(2)}, u32[]{:S(2)}) collective-permute-start(f32[4,72,128]{2,1,0:T(8,128)S(1)} %pad_maximum_fusion.1.refs_8_.refs_12_), channel_id=1, source_target_pairs={{0,4},{4,0},{8,12},{12,8},{16,20},{20,16},{24,28},{28,24},{1,5},{5... | collective-permute-start | bytes 442376 | tf_op jit(solution)/shard_map/ppermute | solution.py:92
  22.2 1.2 %collective-permute-done.2 = f32[4,64,128]{2,1,0:T(8,128)S(1)} collective-permute-done((f32[4,64,128]{2,1,0:T(8,128)S(1)}, f32[4,64,128]{2,1,0:T(8,128)S(1)}, u32[]{:S(2)}, u32[]{:S(2)}) %collective-permute-start.2) | collective-permute-done | bytes 131104 | tf_op jit(solution)/shard_map/ppermute | solution.py:92
  24.1 1.7 %collective-permute-done.12.refs_9_.refs_14_ = f32[4,72,128]{2,1,0:T(8,128)S(1)} collective-permute-done((f32[4,72,128]{2,1,0:T(8,128)S(1)}, f32[4,72,128]{2,1,0:T(8,128)S(1)}, u32[]{:S(2)}, u32[]{:S(2)}) %collective-permute-start.12) | collective-permute-done | bytes 147488 | tf_op jit(solution)/shard_map/ppermute | solution.py:92
  25.8 6.4 %scores.1 = (f32[2,1024,1024]{2,1,0:T(8,128)S(1)}, f32[2,1024,1024]{2,1,0:T(8,128)S(1)}, f32[2,1024,1024]{2,1,0:T(8,128)S(1)}, f32[2,1024,1024]{2,1,0:T(8,128)S(1)}, f32[8,128]{1,0:T(8,128)S(1)}) custom-call(s32[2]{0:T(128)S(1)} %pad_add_fusion.place_ref.refs_18_, f32[8,64,128]{2,1,0:T(8,128)S(1)} %pad_maximum_fusion.mine_ref, ...), custom_call_target="tpu_custom_call" | custom-call | tf_op jit(solution)/shard_map/scores/pallas_call | solution.py:375
  32.8 1.6 %collective-permute-start.5 = (f32[8,128]{1,0:T(8,128)S(1)}, f32[8,128]{1,0:T(8,128)S(1)}, u32[]{:S(2)}, u32[]{:S(2)}) collective-permute-start(f32[8,128]{1,0:T(8,128)S(1)} %get-tuple-element.22.refs_4_), channel_id=1, source_target_pairs={{0,2},{1,3},{2,0},{3,1},{4,6},{5,7},{6,4},{7,5},{8,10},{9,11},{10,... | collective-permute-start | bytes 12296 | tf_op jit(solution)/shard_map/ppermute | solution.py:92
  34.4 2.0 %collective-permute-done.5.refs_6_ = f32[8,128]{1,0:T(8,128)S(1)} collective-permute-done((f32[8,128]{1,0:T(8,128)S(1)}, f32[8,128]{1,0:T(8,128)S(1)}, u32[]{:S(2)}, u32[]{:S(2)}) %collective-permute-start.5) | collective-permute-done | bytes 4128 | tf_op jit(solution)/shard_map/ppermute | solution.py:92
  36.4 1.0 %collective-permute-done.6.refs_7_ = f32[8,128]{1,0:T(8,128)S(1)} collective-permute-done((f32[8,128]{1,0:T(8,128)S(1)}, f32[8,128]{1,0:T(8,128)S(1)}, u32[]{:S(2)}, u32[]{:S(2)}) %collective-permute-start.6) | collective-permute-done | bytes 4128 | tf_op jit(solution)/shard_map/ppermute | solution.py:92
  37.4 15.9 %sweep_first.1 = (f32[2,1024,1024]{2,1,0:T(8,128)S(1)}, f32[2,1024,1024]{2,1,0:T(8,128)S(1)}, f32[2,1024,1024]{2,1,0:T(8,128)S(1)}, f32[2,1024,1024]{2,1,0:T(8,1...) custom-call(f32[2,1024,1024]{2,1,0:T(8,128)S(1)} %get-tuple-element., ...), custom_call_target="tpu_custom_call", output_to_operand_aliasing={{0}: (0, {}), {1}: (1, {}), {2}: (2, {}), {3}: (3, {})} | custom-call | tf_op jit(solution)/shard_map/sweep_first/pallas_call | solution.py:391
  54.0 1.2 %collective-permute-start.9 = (f32[8,128]{1,0:T(8,128)S(1)}, f32[8,128]{1,0:T(8,128)S(1)}, u32[]{:S(2)}, u32[]{:S(2)}) collective-permute-start(f32[8,128]{1,0:T(8,128)S(1)} %get-tuple-element.27.refs_4_), channel_id=1, source_target_pairs={{0,3},{1,2},{2,1},{3,0},{4,7},{5,6},{6,5},{7,4},{8,11},{9,10},{10,... | collective-permute-start | bytes 12296 | tf_op jit(solution)/shard_map/ppermute | solution.py:92
  55.2 1.9 %collective-permute-done.8.refs_6_ = f32[8,128]{1,0:T(8,128)S(1)} collective-permute-done((f32[8,128]{1,0:T(8,128)S(1)}, f32[8,128]{1,0:T(8,128)S(1)}, u32[]{:S(2)}, u32[]{:S(2)}) %collective-permute-start.8) | collective-permute-done | bytes 4128 | tf_op jit(solution)/shard_map/ppermute | solution.py:92
  57.0 5.9 %sweep.2 = (f32[24,128]{1,0:T(8,128)S(1)}, f32[8,1,1024]{2,1,0:T(1,128)}) custom-call(f32[2,1024,1024]{2,1,0:T(8,128)S(1)} %get-tuple-element.23.refs_0_, f32[2,1024,1024]{2,1,0:T(8,128)S(1)} %get-tuple-element.24.refs_1_, f32[2,1024,1024]{2,1,0:T(8,128)S(1)} %get-tuple-element.25.refs_2_, f32[2,1024,1024]{2,1,0:T(8,128)S(1)} %get-tuple-element.26.refs_3_, ...), custom_call_target="tpu_custom_call" | custom-call | tf_op jit(solution)/shard_map/sweep/pallas_call | solution.py:391
  63.0 1.4 %collective-permute-start.14 = (f32[24,128]{1,0:T(8,128)S(1)}, f32[24,128]{1,0:T(8,128)S(1)}, u32[]{:S(2)}, u32[]{:S(2)}) collective-permute-start(f32[24,128]{1,0:T(8,128)S(1)} %get-tuple-element.29.refs_4_.refs_8_), channel_id=1, source_target_pairs={{0,2},{1,3},{2,0},{3,1},{4,6},{5,7},{6,4},{7,5},{8,10},{9,11},{10,... | collective-permute-start | bytes 36872 | tf_op jit(solution)/shard_map/ppermute | solution.py:92
  64.8 1.9 %collective-permute-done.14.refs_6_.refs_10_ = f32[24,128]{1,0:T(8,128)S(1)} collective-permute-done((f32[24,128]{1,0:T(8,128)S(1)}, f32[24,128]{1,0:T(8,128)S(1)}, u32[]{:S(2)}, u32[]{:S(2)}) %collective-permute-start.14) | collective-permute-done | bytes 12320 | tf_op jit(solution)/shard_map/ppermute | solution.py:92
  66.7 0.9 collective-permute-done.15.refs_7_.refs_11_
  67.6 5.5 %sweep.3 = (f32[8,128]{1,0:T(8,128)S(1)}, f32[8,1,1024]{2,1,0:T(1,128)S(1)}) custom-call(f32[2,1024,1024]{2,1,0:T(8,128)S(1)} %get-tuple-element.23.refs_0_, f32[2,1024,1024]{2,1,0:T(8,128)S(1)} %get-tuple-element.24.refs_1_, f32[2,1024,1024]{2,1,0:T(8,128)S(1)} %get-tuple-element.25.refs_2_, f32[2,1024,1024]{2,1,0:T(8,128)S(1)} %get-tuple-element.26.refs_3_, ...), custom_call_target="tpu_custom_call" | custom-call | tf_op jit(solution)/shard_map/sweep/pallas_call | solution.py:391
  73.3 0.7 collective-permute-start.17
  74.0 1.0 %collective-permute-start.18 = (f32[8,128]{1,0:T(8,128)S(1)}, f32[8,128]{1,0:T(8,128)S(1)}, u32[]{:S(2)}, u32[]{:S(2)}) collective-permute-start(f32[8,128]{1,0:T(8,128)S(1)} %get-tuple-element.30.refs_4_), channel_id=1, source_target_pairs={{0,3},{1,2},{2,1},{3,0},{4,7},{5,6},{6,5},{7,4},{8,11},{9,10},{10,... | collective-permute-start | bytes 12296 | tf_op jit(solution)/shard_map/ppermute | solution.py:92
  75.0 1.8 %collective-permute-done.17.refs_6_ = f32[8,128]{1,0:T(8,128)S(1)} collective-permute-done((f32[8,128]{1,0:T(8,128)S(1)}, f32[8,128]{1,0:T(8,128)S(1)}, u32[]{:S(2)}, u32[]{:S(2)}) %collective-permute-start.17) | collective-permute-done | bytes 4128 | tf_op jit(solution)/shard_map/ppermute | solution.py:92
  77.0 4.3 %own_grad.1 = f32[128,128]{1,0:T(8,128)S(1)} custom-call(f32[2,1024,1024]{2,1,0:T(8,128)S(1)} %get-tuple-element.23.refs_0_, f32[2,1024,1024]{2,1,0:T(8,128)S(1)} %get-tuple-element.24.refs_1_, f32[2,1024,1024]{2,1,0:T(8,128)S(1)} %get-tuple-element.25.refs_2_, f32[2,1024,1024]{2,1,0:T(8,128)S(1)} %get-tuple-element.26.refs_3_, ...), custom_call_target="tpu_custom_call" | custom-call | tf_op jit(solution)/shard_map/own_grad/pallas_call | solution.py:419
  81.5 1.3 %collective-permute-start.22 = (f32[128,128]{1,0:T(8,128)S(1)}, f32[128,128]{1,0:T(8,128)S(1)}, u32[]{:S(2)}, u32[]{:S(2)}) collective-permute-start(f32[128,128]{1,0:T(8,128)S(1)} %own_grad.1), channel_id=1, source_target_pairs={{0,2},{1,3},{2,0},{3,1},{4,6},{5,7},{6,4},{7,5},{8,10},{9,11},{10,... | collective-permute-start | bytes 196616 | tf_op jit(solution)/shard_map/ppermute | solution.py:92
  83.2 19.4 %proto_grad.1 = f32[16,8192]{1,0:T(8,128)} custom-call(f32[2,1024,1024]{2,1,0:T(8,128)S(1)} %get-tuple-element.23.refs_0_, f32[2,1024,1024]{2,1,0:T(8,128)S(1)} %get-tuple-element.24.refs_1_, f32[2,1024,1024]{2,1,0:T(8,128)S(1)} %get-tuple-element.25.refs_2_, f32[2,1024,1024]{2,1,0:T(8,128)S(1)} %get-tuple-element.26.refs_3_, ...), custom_call_target="tpu_custom_call" | custom-call | tf_op jit(solution)/shard_map/proto_grad/pallas_call | solution.py:419
  102.6 0.6 add_add_fusion
  (35 shorter events, 3.4 us)
Async XLA Ops:
  1.4 10.0 %collective-permute-start = (f32[1,64,128]{2,1,0:T(8,128)S(1)}, f32[1,64,128]{2,1,0:T(8,128)S(1)}, u32[]{:S(2)}, u32[]{:S(2)}) collective-permute-start(f32[1,64,128]{2,1,0:T(8,128)S(1)} %bitcast_convert_fusion), channel_id=1, source_target_pairs={{0,16},{4,20},{8,24},{12,28},{16,0},{20,4},{24,8},{28,12},{1,17},{... | collective-permute-start | bytes 98312 | tf_op jit(solution)/shard_map/ppermute | solution.py:92
  5.5 1.6 %copy-start = (bf16[128,8192]{1,0:T(8,128)(2,1)S(1)}, bf16[128,8192]{1,0:T(8,128)(2,1)}, u32[]{:S(2)}) copy-start(bf16[128,8192]{1,0:T(8,128)(2,1)} %w_hbm.1) | copy-start | bytes 6291460
  7.1 0.8 copy-start.1
  11.3 4.9 %collective-permute-start.10 = (f32[1,72,128]{2,1,0:T(8,128)S(1)}, f32[1,72,128]{2,1,0:T(8,128)S(1)}, u32[]{:S(2)}, u32[]{:S(2)}) collective-permute-start(f32[1,72,128]{2,1,0:T(8,128)S(1)} %bitcast.6), channel_id=1, source_target_pairs={{0,16},{4,20},{8,24},{12,28},{16,0},{20,4},{24,8},{28,12},{1,17},{... | collective-permute-start | bytes 110600 | tf_op jit(solution)/shard_map/ppermute | solution.py:92
  11.4 6.6 %collective-permute-start.1 = (f32[2,64,128]{2,1,0:T(8,128)S(1)}, f32[2,64,128]{2,1,0:T(8,128)S(1)}, u32[]{:S(2)}, u32[]{:S(2)}) collective-permute-start(f32[2,64,128]{2,1,0:T(8,128)S(1)} %pad_maximum_fusion.4), channel_id=1, source_target_pairs={{0,8},{4,12},{8,0},{12,4},{16,24},{20,28},{24,16},{28,20},{1,9},{5... | collective-permute-start | bytes 196616 | tf_op jit(solution)/shard_map/ppermute | solution.py:92
  16.2 4.4 %collective-permute-start.11 = (f32[2,72,128]{2,1,0:T(8,128)S(1)}, f32[2,72,128]{2,1,0:T(8,128)S(1)}, u32[]{:S(2)}, u32[]{:S(2)}) collective-permute-start(f32[2,72,128]{2,1,0:T(8,128)S(1)} %pad_maximum_fusion.3), channel_id=1, source_target_pairs={{0,8},{4,12},{8,0},{12,4},{16,24},{20,28},{24,16},{28,20},{1,9},{5... | collective-permute-start | bytes 221192 | tf_op jit(solution)/shard_map/ppermute | solution.py:92
  17.9 5.5 %collective-permute-start.2 = (f32[4,64,128]{2,1,0:T(8,128)S(1)}, f32[4,64,128]{2,1,0:T(8,128)S(1)}, u32[]{:S(2)}, u32[]{:S(2)}) collective-permute-start(f32[4,64,128]{2,1,0:T(8,128)S(1)} %pad_maximum_fusion.2), channel_id=1, source_target_pairs={{0,4},{4,0},{8,12},{12,8},{16,20},{20,16},{24,28},{28,24},{1,5},{5... | collective-permute-start | bytes 393224 | tf_op jit(solution)/shard_map/ppermute | solution.py:92
  20.6 5.2 %collective-permute-start.12 = (f32[4,72,128]{2,1,0:T(8,128)S(1)}, f32[4,72,128]{2,1,0:T(8,128)S(1)}, u32[]{:S(2)}, u32[]{:S(2)}) collective-permute-start(f32[4,72,128]{2,1,0:T(8,128)S(1)} %pad_maximum_fusion.1.refs_8_.refs_12_), channel_id=1, source_target_pairs={{0,4},{4,0},{8,12},{12,8},{16,20},{20,16},{24,28},{28,24},{1,5},{5... | collective-permute-start | bytes 442376 | tf_op jit(solution)/shard_map/ppermute | solution.py:92
  23.5 2.3 %collective-permute-start.3 = (f32[8,64,128]{2,1,0:T(8,128)S(1)}, f32[8,64,128]{2,1,0:T(8,128)S(1)}, u32[]{:S(2)}, u32[]{:S(2)}) collective-permute-start(f32[8,64,128]{2,1,0:T(8,128)S(1)} %pad_maximum_fusion.mine_ref), channel_id=1, source_target_pairs={{0,1},{1,0},{2,3},{3,2},{4,5},{5,4},{6,7},{7,6},{8,9},{9,8},{10,11... | collective-permute-start | bytes 786440 | tf_op jit(solution)/shard_map/ppermute | solution.py:92
  23.6 51.5 %collective-permute-start.19 = (f32[4,72,128]{2,1,0:T(8,128)S(1)}, f32[4,72,128]{2,1,0:T(8,128)S(1)}, u32[]{:S(2)}, u32[]{:S(2)}) collective-permute-start(f32[4,72,128]{2,1,0:T(8,128)S(1)} %pad_maximum_fusion.1.refs_8_.refs_12_), channel_id=1, source_target_pairs={{0,1},{1,0},{2,3},{3,2},{4,5},{5,4},{6,7},{7,6},{8,9},{9,8},{10,11... | collective-permute-start | bytes 442376 | tf_op jit(solution)/shard_map/ppermute | solution.py:92
  25.8 49.3 %collective-permute-start.20 = (f32[4,72,128]{2,1,0:T(8,128)S(1)}, f32[4,72,128]{2,1,0:T(8,128)S(1)}, u32[]{:S(2)}, u32[]{:S(2)}) collective-permute-start(f32[4,72,128]{2,1,0:T(8,128)S(1)} %collective-permute-done.12.refs_9_.refs_14_), channel_id=1, source_target_pairs={{0,1},{1,0},{2,3},{3,2},{4,5},{5,4},{6,7},{7,6},{8,9},{9,8},{10,11... | collective-permute-start | bytes 442376 | tf_op jit(solution)/shard_map/ppermute | solution.py:92
  32.2 2.2 %collective-permute-start.4 = (f32[8,128]{1,0:T(8,128)S(1)}, f32[8,128]{1,0:T(8,128)S(1)}, u32[]{:S(2)}, u32[]{:S(2)}) collective-permute-start(f32[8,128]{1,0:T(8,128)S(1)} %get-tuple-element.22.refs_4_), channel_id=1, source_target_pairs={{0,1},{1,0},{2,3},{3,2},{4,5},{5,4},{6,7},{7,6},{8,9},{9,8},{10,11... | collective-permute-start | bytes 12296 | tf_op jit(solution)/shard_map/ppermute | solution.py:92
  32.8 3.6 %collective-permute-start.5 = (f32[8,128]{1,0:T(8,128)S(1)}, f32[8,128]{1,0:T(8,128)S(1)}, u32[]{:S(2)}, u32[]{:S(2)}) collective-permute-start(f32[8,128]{1,0:T(8,128)S(1)} %get-tuple-element.22.refs_4_), channel_id=1, source_target_pairs={{0,2},{1,3},{2,0},{3,1},{4,6},{5,7},{6,4},{7,5},{8,10},{9,11},{10,... | collective-permute-start | bytes 12296 | tf_op jit(solution)/shard_map/ppermute | solution.py:92
  34.4 3.1 %collective-permute-start.6 = (f32[8,128]{1,0:T(8,128)S(1)}, f32[8,128]{1,0:T(8,128)S(1)}, u32[]{:S(2)}, u32[]{:S(2)}) collective-permute-start(f32[8,128]{1,0:T(8,128)S(1)} %get-tuple-element.22.refs_4_), channel_id=1, source_target_pairs={{0,3},{1,2},{2,1},{3,0},{4,7},{5,6},{6,5},{7,4},{8,11},{9,10},{10,... | collective-permute-start | bytes 12296 | tf_op jit(solution)/shard_map/ppermute | solution.py:92
  53.3 1.9 %collective-permute-start.7 = (f32[8,128]{1,0:T(8,128)S(1)}, f32[8,128]{1,0:T(8,128)S(1)}, u32[]{:S(2)}, u32[]{:S(2)}) collective-permute-start(f32[8,128]{1,0:T(8,128)S(1)} %get-tuple-element.27.refs_4_), channel_id=1, source_target_pairs={{0,1},{1,0},{2,3},{3,2},{4,5},{5,4},{6,7},{7,6},{8,9},{9,8},{10,11... | collective-permute-start | bytes 12296 | tf_op jit(solution)/shard_map/ppermute | solution.py:92
  53.4 3.6 %collective-permute-start.8 = (f32[8,128]{1,0:T(8,128)S(1)}, f32[8,128]{1,0:T(8,128)S(1)}, u32[]{:S(2)}, u32[]{:S(2)}) collective-permute-start(f32[8,128]{1,0:T(8,128)S(1)} %get-tuple-element.27.refs_4_), channel_id=1, source_target_pairs={{0,2},{1,3},{2,0},{3,1},{4,6},{5,7},{6,4},{7,5},{8,10},{9,11},{10,... | collective-permute-start | bytes 12296 | tf_op jit(solution)/shard_map/ppermute | solution.py:92
  54.0 3.1 %collective-permute-start.9 = (f32[8,128]{1,0:T(8,128)S(1)}, f32[8,128]{1,0:T(8,128)S(1)}, u32[]{:S(2)}, u32[]{:S(2)}) collective-permute-start(f32[8,128]{1,0:T(8,128)S(1)} %get-tuple-element.27.refs_4_), channel_id=1, source_target_pairs={{0,3},{1,2},{2,1},{3,0},{4,7},{5,6},{6,5},{7,4},{8,11},{9,10},{10,... | collective-permute-start | bytes 12296 | tf_op jit(solution)/shard_map/ppermute | solution.py:92
  62.9 1.9 %collective-permute-start.13 = (f32[24,128]{1,0:T(8,128)S(1)}, f32[24,128]{1,0:T(8,128)S(1)}, u32[]{:S(2)}, u32[]{:S(2)}) collective-permute-start(f32[24,128]{1,0:T(8,128)S(1)} %get-tuple-element.29.refs_4_.refs_8_), channel_id=1, source_target_pairs={{0,1},{1,0},{2,3},{3,2},{4,5},{5,4},{6,7},{7,6},{8,9},{9,8},{10,11... | collective-permute-start | bytes 36872 | tf_op jit(solution)/shard_map/ppermute | solution.py:92
  63.0 3.7 %collective-permute-start.14 = (f32[24,128]{1,0:T(8,128)S(1)}, f32[24,128]{1,0:T(8,128)S(1)}, u32[]{:S(2)}, u32[]{:S(2)}) collective-permute-start(f32[24,128]{1,0:T(8,128)S(1)} %get-tuple-element.29.refs_4_.refs_8_), channel_id=1, source_target_pairs={{0,2},{1,3},{2,0},{3,1},{4,6},{5,7},{6,4},{7,5},{8,10},{9,11},{10,... | collective-permute-start | bytes 36872 | tf_op jit(solution)/shard_map/ppermute | solution.py:92
  64.5 3.1 %collective-permute-start.15 = (f32[24,128]{1,0:T(8,128)S(1)}, f32[24,128]{1,0:T(8,128)S(1)}, u32[]{:S(2)}, u32[]{:S(2)}) collective-permute-start(f32[24,128]{1,0:T(8,128)S(1)} %get-tuple-element.29.refs_4_.refs_8_), channel_id=1, source_target_pairs={{0,3},{1,2},{2,1},{3,0},{4,7},{5,6},{6,5},{7,4},{8,11},{9,10},{10,... | collective-permute-start | bytes 36872 | tf_op jit(solution)/shard_map/ppermute | solution.py:92
  73.1 1.9 %collective-permute-start.16 = (f32[8,128]{1,0:T(8,128)S(1)}, f32[8,128]{1,0:T(8,128)S(1)}, u32[]{:S(2)}, u32[]{:S(2)}) collective-permute-start(f32[8,128]{1,0:T(8,128)S(1)} %get-tuple-element.30.refs_4_), channel_id=1, source_target_pairs={{0,1},{1,0},{2,3},{3,2},{4,5},{5,4},{6,7},{7,6},{8,9},{9,8},{10,11... | collective-permute-start | bytes 12296 | tf_op jit(solution)/shard_map/ppermute | solution.py:92
  73.3 3.6 %collective-permute-start.17 = (f32[8,128]{1,0:T(8,128)S(1)}, f32[8,128]{1,0:T(8,128)S(1)}, u32[]{:S(2)}, u32[]{:S(2)}) collective-permute-start(f32[8,128]{1,0:T(8,128)S(1)} %get-tuple-element.30.refs_4_), channel_id=1, source_target_pairs={{0,2},{1,3},{2,0},{3,1},{4,6},{5,7},{6,4},{7,5},{8,10},{9,11},{10,... | collective-permute-start | bytes 12296 | tf_op jit(solution)/shard_map/ppermute | solution.py:92
  74.0 3.0 %collective-permute-start.18 = (f32[8,128]{1,0:T(8,128)S(1)}, f32[8,128]{1,0:T(8,128)S(1)}, u32[]{:S(2)}, u32[]{:S(2)}) collective-permute-start(f32[8,128]{1,0:T(8,128)S(1)} %get-tuple-element.30.refs_4_), channel_id=1, source_target_pairs={{0,3},{1,2},{2,1},{3,0},{4,7},{5,6},{6,5},{7,4},{8,11},{9,10},{10,... | collective-permute-start | bytes 12296 | tf_op jit(solution)/shard_map/ppermute | solution.py:92
  81.3 21.3 %collective-permute-start.21 = (f32[128,128]{1,0:T(8,128)S(1)}, f32[128,128]{1,0:T(8,128)S(1)}, u32[]{:S(2)}, u32[]{:S(2)}) collective-permute-start(f32[128,128]{1,0:T(8,128)S(1)} %own_grad.1), channel_id=1, source_target_pairs={{0,1},{1,0},{2,3},{3,2},{4,5},{5,4},{6,7},{7,6},{8,9},{9,8},{10,11... | collective-permute-start | bytes 196616 | tf_op jit(solution)/shard_map/ppermute | solution.py:92
  81.5 21.2 %collective-permute-start.22 = (f32[128,128]{1,0:T(8,128)S(1)}, f32[128,128]{1,0:T(8,128)S(1)}, u32[]{:S(2)}, u32[]{:S(2)}) collective-permute-start(f32[128,128]{1,0:T(8,128)S(1)} %own_grad.1), channel_id=1, source_target_pairs={{0,2},{1,3},{2,0},{3,1},{4,6},{5,7},{6,4},{7,5},{8,10},{9,11},{10,... | collective-permute-start | bytes 196616 | tf_op jit(solution)/shard_map/ppermute | solution.py:92
  82.8 19.9 %collective-permute-start.23 = (f32[128,128]{1,0:T(8,128)S(1)}, f32[128,128]{1,0:T(8,128)S(1)}, u32[]{:S(2)}, u32[]{:S(2)}) collective-permute-start(f32[128,128]{1,0:T(8,128)S(1)} %own_grad.1), channel_id=1, source_target_pairs={{0,3},{1,2},{2,1},{3,0},{4,7},{5,6},{6,5},{7,4},{8,11},{9,10},{10,... | collective-permute-start | bytes 196616 | tf_op jit(solution)/shard_map/ppermute | solution.py:92

commit v3 on v0

v3 whole, which is shorter than its diff:
```python
import math

import jax
import jax.numpy as jnp
from jax import lax
from jax.experimental import pallas as pl
from jax.experimental.pallas import tpu as pltpu
from jax.sharding import PartitionSpec as P

ITERS = 3

teacher_temp = 0.07
student_temp = 0.1

LOG2E = math.log2(math.e)
T_EXP = LOG2E / teacher_temp
S_EXP = LOG2E / student_temp

LANES = 128
SUB = 8
PARTS = 4
STAT_ROWS = 8
KERNEL_BYTES = 32 << 20


def combined_all(value, axis, combine):
    everything = jax.tree.map(lambda part: lax.all_gather(part, axis), value)
    leading = jax.tree.map(lambda part: part[0], everything)

    def step(k, so_far):
        return combine(so_far, jax.tree.map(lambda part: part[k], everything))

    return lax.fori_loop(1, lax.axis_size(axis), step, leading)


def divided_logits(features, prototypes, divisor):
    return jnp.dot(features, prototypes, preferred_element_type=jnp.float32) / divisor


def combine_stats(earlier, later):
    teacher_peak = jnp.maximum(earlier[0], later[0])
    student_peak = jnp.maximum(earlier[1], later[1])
    merged_total = earlier[2] * jnp.exp(earlier[1] - student_peak) + later[2] * jnp.exp(
        later[1] - student_peak
    )
    return (teacher_peak, student_peak, merged_total)


def split_crops(teacher_feat, student_feat, proto_weight):
    teacher_scores = divided_logits(teacher_feat, proto_weight, teacher_temp)
    student_scores = divided_logits(student_feat, proto_weight, student_temp)
    local_teacher = jnp.max(teacher_scores, axis=1)
    local_student = jnp.max(student_scores, axis=1)
    local_total = jnp.sum(jnp.exp(student_scores - local_student[:, None]), axis=1)
    teacher_peak, student_peak, student_total = combined_all(
        (local_teacher, local_student, local_total), "proto", combine_stats
    )
    kernel = jnp.exp(teacher_scores - teacher_peak[:, None])
    row_scale = jnp.ones((teacher_feat.shape[0],), jnp.float32)
    for sweep in range(ITERS):
        col_part = jnp.sum(kernel * row_scale[:, None], axis=0)
        col_scale = 1.0 / lax.psum(col_part, "dp")
        row_part = jnp.sum(kernel * col_scale[None, :], axis=1)
        row_scale = 1.0 / lax.psum(row_part, "proto")
    target = kernel * row_scale[:, None] * col_scale[None, :]
    student_probs = jnp.exp(student_scores - student_peak[:, None]) / student_total[:, None]
    grad_scores = ((student_probs - target) / student_temp).astype(jnp.bfloat16)
    input_part = lax.dot_general(
        grad_scores, proto_weight, (((1,), (1,)), ((), ())), preferred_element_type=jnp.float32
    )
    feature_grad = lax.psum(input_part, "proto")
    proto_grad = lax.psum_scatter(
        lax.dot_general(
            student_feat, grad_scores, (((0,), (0,)), ((), ())), preferred_element_type=jnp.float32
        ),
        "dp",
        scatter_dimension=0,
        tiled=True,
    )
    return (proto_grad, feature_grad)


def vmem():
    return pl.BlockSpec(memory_space=pltpu.VMEM)


def smem():
    return pl.BlockSpec(memory_space=pltpu.SMEM)


def swap(x, axis, bit):
    return lax.ppermute(x, axis, [(i, i ^ bit) for i in range(lax.axis_size(axis))])


def fold(parts, op):
    parts = list(parts)
    while len(parts) > 1:
        parts = [op(*parts[k : k + 2]) if k + 1 < len(parts) else parts[k] for k in range(0, len(parts), 2)]
    return parts[0]


NT = (((1,), (1,)), ((), ()))
TN = (((0,), (0,)), ((), ()))


def fold_rows(x, op):
    return fold([x[k : k + SUB, :] for k in range(0, x.shape[0], SUB)], op)


def lane_rows(flat):
    return [jnp.broadcast_to(flat[q : q + 1, :], (SUB, LANES)) for q in range(flat.shape[0])]


def own_body(place_ref, s_ref, w_ref, out_ref, wt_ref, scores_ref):
    rows = s_ref.shape[0]
    half = rows // 2
    count, width, unused = scores_ref.shape
    s = s_ref[...]
    top = None
    for j in range(count):
        wt = w_ref[:, j * width : (j + 1) * width].astype(jnp.float32).T.astype(jnp.bfloat16)
        wt_ref[j * width : (j + 1) * width, :] = wt
        scores = lax.dot_general(wt, s, NT, preferred_element_type=jnp.float32)
        scores_ref[j] = scores
        new = fold_rows(scores, jnp.maximum)
        top = new if top is None else jnp.maximum(top, new)
    peak = jnp.max(top, axis=0, keepdims=True)

    def total(j, so_far):
        return so_far + fold_rows(jnp.exp2((scores_ref[j] - peak) * S_EXP), jnp.add)

    sums = lax.fori_loop(0, count, total, jnp.zeros((SUB, rows), jnp.float32))
    first = pl.multiple_of(place_ref[0] * half, half)
    out_ref[0:half, :] = s_ref[pl.ds(first, half), :].astype(jnp.float32)
    stats = [
        peak,
        jnp.sum(sums, axis=0, keepdims=True),
        jnp.zeros((STAT_ROWS - 2, LANES), jnp.float32),
    ]
    out_ref[half:, :] = jnp.concatenate(stats, axis=0)


def join_halves(core, mine, other, out_ref, first):
    half = LANES // 2
    for j in range(mine.shape[0]):
        base = (first + j) * LANES
        a = pl.multiple_of(base + core * half, half)
        b = pl.multiple_of(base + (1 - core) * half, half)
        out_ref[pl.ds(a, half), :] = mine[j, 0:half, :].astype(jnp.bfloat16)
        out_ref[pl.ds(b, half), :] = other[j, 0:half, :].astype(jnp.bfloat16)


def scores_body(place_ref, mine_ref, other_ref, wt_ref, *refs):
    k_refs = refs[:PARTS]
    max_ref, t_scr, acc_ref = refs[PARTS:]
    join_halves(place_ref[0], mine_ref, other_ref, t_scr, 0)
    t = t_scr[...]
    per = k_refs[0].shape[0]
    chunk = min(per, 1024)
    acc_ref[...] = jnp.full(acc_ref.shape, -jnp.inf, jnp.float32)
    for p in range(PARTS):

        def block(j, unused, p=p):
            at = pl.ds(pl.multiple_of(j * chunk, chunk), chunk)
            w = wt_ref[pl.ds(pl.multiple_of(p * per + j * chunk, chunk), chunk), :]
            s = lax.dot_general(w, t, NT, preferred_element_type=jnp.float32) * T_EXP
            k_refs[p][at, :] = s
            acc_ref[...] = jnp.maximum(acc_ref[...], fold_rows(s, jnp.maximum))
            return 0

        lax.fori_loop(0, per // chunk, block, 0)
    n = max_ref.shape[0]
    tops = [jnp.max(acc_ref[:, q * LANES : (q + 1) * LANES], axis=0, keepdims=True) for q in range(n)]
    max_ref[...] = jnp.concatenate(tops, axis=0)


def sweep_body(first, last, n_in, n_extra, *refs):
    k_refs, refs = refs[:PARTS], refs[PARTS:]
    in_refs, refs = refs[:n_in], refs[n_in:]
    extra_refs, refs = refs[:n_extra], refs[n_extra:]
    if first or last:
        k_refs, refs = refs[:PARTS], refs[PARTS:]
    o_ref = refs[0]
    per, rows = k_refs[0].shape
    n = rows // LANES
    if first:
        scale = fold([x[...] for x in in_refs], jnp.maximum)
    else:
        scale = 1.0 / fold([x[0:n, :] for x in in_refs], jnp.add)
    wide = lane_rows(scale)
    unroll = 16
    group = 2 if last else 4
    chunk = unroll * SUB
    tiles = [slice(q * LANES, (q + 1) * LANES) for q in range(n)]

    def phases(p_down, i_down, p_across, i_across, inverse, acc):
        acc = list(acc)
        new = []

        def load(g):
            out = []
            for u in range(g, g + group):
                at = pl.ds(pl.multiple_of(i_down * chunk, chunk) + u * SUB, SUB)
                x = [k_refs[p_down][at, tiles[q]] for q in range(n)]
                out.append((at, [x[q] - wide[q] if first else x[q] * wide[q] for q in range(n)]))
            return out

        ahead = load(0) if p_down is not None else None
        for g in range(0, unroll, group):
            if p_down is not None:
                now = ahead
                if g + group < unroll and (first or last):
                    ahead = load(g + group)
            if p_across is not None:
                done = []
                for u in range(g, g + group):
                    at = pl.ds(pl.multiple_of(i_across * chunk, chunk) + u * SUB, SUB)
                    for q in range(n):
                        x = k_refs[p_across][at, tiles[q]] * inverse[u]
                        acc[q] = acc[q] + x
                        done.append((at, tiles[q], x))
                if last:
                    for at, lanes, x in done:
                        k_refs[p_across][at, lanes] = x
            if p_down is not None:
                for at, x in now:
                    if first:
                        x = [jnp.exp2(v) for v in x]
                        for q in range(n):
                            k_refs[p_down][at, tiles[q]] = x[q]
                    c = 1.0 / jnp.sum(fold(x, jnp.add), axis=1, keepdims=True)
                    c = jnp.broadcast_to(c, (SUB, LANES))
                    new.append(c)
                if g + group < unroll and not (first or last):
                    ahead = load(g + group)
        return tuple(new), tuple(acc)

    acc = (jnp.zeros((SUB, LANES), jnp.float32),) * n
    inverse = None
    steps = per // chunk
    for p in range(PARTS):
        before = None if p == 0 else p - 1
        inverse, acc = phases(p, 0, before, steps - 1, inverse, acc)

        def step(i, carry, p=p):
            return phases(p, i + 1, p, i, *carry)

        inverse, acc = lax.fori_loop(0, steps - 1, step, (inverse, acc))
    unused, acc = phases(None, 0, PARTS - 1, steps - 1, inverse, acc)
    o_ref[0:n, :] = jnp.concatenate([jnp.sum(x, axis=0, keepdims=True) for x in acc], axis=0)
    if n_extra:
        half = LANES // 2
        for k in range(2):
            rows_k = [x[j, half + k : half + k + 1, :] for x in extra_refs for j in range(x.shape[0])]
            o_ref[(k + 1) * n : (k + 2) * n, :] = jnp.concatenate(rows_k, axis=0)


def final_scales(row_refs, stat_refs):
    n = row_refs[0].shape[0]
    row_scale = 1.0 / fold([x[...] for x in row_refs], jnp.add)
    peak = fold([x[n : 2 * n, :] for x in stat_refs], jnp.maximum)
    total = fold(
        [x[2 * n :, :] * jnp.exp2((x[n : 2 * n, :] - peak) * S_EXP) for x in stat_refs], jnp.add
    )
    shift = peak * S_EXP + jnp.log(total * student_temp) * LOG2E
    return row_scale * (1.0 / student_temp), shift


def grad_rows(k_ref, first, s_scr, g_scr, scale, shift):
    step = 2 * SUB
    scale = [jnp.concatenate([x, x], axis=0) for x in scale]
    shift = [jnp.concatenate([x, x], axis=0) for x in shift]
    for i in range(0, s_scr.shape[0], step):
        for q in range(len(scale)):
            lanes = slice(q * LANES, (q + 1) * LANES)
            probs = jnp.exp2(s_scr[i : i + step, lanes] * S_EXP - shift[q])
            target = k_ref[pl.ds(first + i, step), lanes] * scale[q]
            g_scr[i : i + step, lanes] = (probs - target).astype(jnp.bfloat16)


def own_grad_body(n_in, *refs):
    k_refs, refs = refs[:PARTS], refs[PARTS:]
    row_refs, refs = refs[:n_in], refs[n_in:]
    stat_refs, refs = refs[:n_in], refs[n_in:]
    near_ref, other_ref, wt_ref, place_ref, out_ref, f_scr, *pairs = refs
    scale, shift = final_scales(row_refs, stat_refs)
    scale, shift = lane_rows(scale[0:1]), lane_rows(shift[0:1])
    join_halves(place_ref[0], near_ref.at[0:1], other_ref.at[0:1], f_scr, 0)
    s = f_scr[...]
    per = k_refs[0].shape[0]
    half = len(pairs) // 2
    chunk = pairs[0].shape[0]
    total = jnp.zeros(out_ref.shape, jnp.float32)
    for p in range(PARTS):
        for k in range(per // chunk):
            s_scr, g_scr = pairs[2 * (k % half)], pairs[2 * (k % half) + 1]
            start = p * per + k * chunk
            w = wt_ref[start : start + chunk, :]
            s_scr[...] = lax.dot_general(w, s, NT, preferred_element_type=jnp.float32)
            grad_rows(k_refs[p], k * chunk, s_scr, g_scr, scale, shift)
            total = total + lax.dot_general(g_scr[...], w, TN, preferred_element_type=jnp.float32)
    out_ref[...] = total


def proto_grad_body(n_in, *refs):
    k_refs, refs = refs[:PARTS], refs[PARTS:]
    row_refs, refs = refs[:n_in], refs[n_in:]
    stat_refs, refs = refs[:n_in], refs[n_in:]
    near_ref, near_other_ref, far_ref, far_other_ref, wt_ref, place_ref, out_ref = refs[:7]
    f_scr, s_even, g_even, s_odd, g_odd = refs[7:]
    scale, shift = (lane_rows(x) for x in final_scales(row_refs, stat_refs))
    core = place_ref[0]
    join_halves(core, near_ref, near_other_ref, f_scr, 0)
    join_halves(core, far_ref, far_other_ref, f_scr, near_ref.shape[0])
    s = f_scr[...]
    owned = out_ref.shape[0]
    depth = s.shape[1]
    column = lax.broadcasted_iota(jnp.int32, (depth, LANES), 1)
    wanted = column + place_ref[1] * owned
    pick = (lax.broadcasted_iota(jnp.int32, (depth, LANES), 0) == wanted) & (column < owned)
    pick = pick.astype(jnp.float32).astype(jnp.bfloat16)
    picked = jnp.dot(s, pick, preferred_element_type=jnp.float32).astype(jnp.bfloat16)
    per = k_refs[0].shape[0]
    chunk = s_even.shape[0]
    final_chunk = wt_ref.shape[0] // chunk - 1

    def scores(k, s_scr):
        at = pl.ds(pl.multiple_of(jnp.minimum(k, final_chunk) * chunk, chunk), chunk)
        s_scr[...] = lax.dot_general(wt_ref[at, :], s, NT, preferred_element_type=jnp.float32)

    def finish(k, g_scr):
        at = pl.ds(pl.multiple_of(jnp.maximum(k, 0) * chunk, chunk), chunk)
        part = jnp.dot(g_scr[...], picked, preferred_element_type=jnp.float32)
        out_ref[:, at] = part.T[0:owned, :]

    g_odd[...] = jnp.zeros_like(g_odd)
    scores(0, s_even)
    pairs = per // chunk // 2
    for p in range(PARTS):

        def step(i, unused, p=p):
            k = 2 * (p * pairs + i)
            here = pl.multiple_of(2 * i * chunk, 2 * chunk)
            scores(k + 1, s_odd)
            finish(k - 1, g_odd)
            grad_rows(k_refs[p], here, s_even, g_even, scale, shift)
            scores(k + 2, s_even)
            finish(k, g_even)
            grad_rows(k_refs[p], here + chunk, s_odd, g_odd, scale, shift)
            return 0

        lax.fori_loop(0, pairs, step, 0)
    finish(final_chunk, g_odd)


def all_crops(teacher_feat, student_feat, proto_weight):
    own, depth = teacher_feat.shape
    n_dp = lax.axis_size("dp")
    n_proto = lax.axis_size("proto")
    rows = own * n_dp
    n = rows // LANES
    cols = proto_weight.shape[1]
    per = cols // PARTS
    half = own // 2
    f32 = jnp.float32
    bf16 = jnp.bfloat16

    def grant(mib):
        return pltpu.CompilerParams(vmem_limit_bytes=mib << 20)

    place = jnp.stack([lax.axis_index("proto") % 2, lax.axis_index("dp")]).astype(jnp.int32)

    def everyone(x):
        return [x] + [swap(x, "proto", k) for k in range(1, n_proto)]

    def spread(x, bits):
        for bit in bits:
            x = jnp.concatenate([x, swap(x, "dp", bit)], axis=0)
        return x

    bits = [1 << k for k in range(n_dp.bit_length() - 1)][::-1]
    teacher_half = lax.dynamic_slice_in_dim(teacher_feat, place[0] * half, half, 0).astype(f32)
    mine = spread(teacher_half[None], bits)
    other = swap(mine, "proto", 1)

    chunk = 1024
    student_part, weight_t = pl.pallas_call(
        own_body,
        out_shape=(
            jax.ShapeDtypeStruct((half + STAT_ROWS, depth), f32),
            pltpu.VMEM((cols, depth), bf16),
        ),
        in_specs=[smem(), vmem(), vmem()],
        out_specs=(vmem(),) * 2,
        scratch_shapes=[pltpu.VMEM((cols // chunk, chunk, own), f32)],
        compiler_params=grant(16),
        name="own_stats",
    )(place, student_feat, proto_weight)
    near = spread(student_part[None], bits[:-1])

    k_shape = pltpu.VMEM((per, rows), f32)
    flat = jax.ShapeDtypeStruct((n, LANES), f32)
    *kernel, local_peak = pl.pallas_call(
        scores_body,
        out_shape=(k_shape,) * PARTS + (flat,),
        in_specs=[smem(), vmem(), vmem(), vmem()],
        out_specs=(vmem(),) * (PARTS + 1),
        scratch_shapes=[pltpu.VMEM((rows, depth), bf16), pltpu.VMEM((SUB, rows), f32)],
        compiler_params=grant(16),
        name="scores",
    )(place, mine, other, weight_t)

    def sweep(kernel, ins, extra, it):
        first, last = it == 0, it == ITERS - 1
        kept = (k_shape,) * PARTS if first or last else ()
        outs = (jax.ShapeDtypeStruct((3 * n if extra else n, LANES), f32),)
        result = pl.pallas_call(
            lambda *refs: sweep_body(first, last, len(ins), len(extra), *refs),
            out_shape=kept + outs,
            in_specs=[vmem()] * (PARTS + len(ins) + len(extra)),
            out_specs=(vmem(),) * (len(kept) + len(outs)),
            input_output_aliases={k: k for k in range(len(kept))},
            compiler_params=grant(16),
            name="sweep_first" if first else "sweep_last" if last else "sweep",
        )(*kernel, *ins, *extra)
        return (result[:PARTS] if kept else kernel), result[-1]

    ins = everyone(local_peak)
    far = swap(near, "dp", bits[-1])
    near_other = swap(near, "proto", 1)
    far_other = swap(far, "proto", 1)
    stats = None
    for it in range(ITERS):
        extra = (near, far) if it == ITERS - 2 else ()
        kernel, row_part = sweep(kernel, ins, extra, it)
        ins = everyone(row_part)
        if extra:
            stats = ins

    def final(body, operands, shape, scratch, mib, name):
        return pl.pallas_call(
            lambda *refs: body(len(ins), *refs),
            out_shape=jax.ShapeDtypeStruct(shape, f32),
            in_specs=[vmem()] * (PARTS + 2 * len(ins) + len(operands)) + [smem()],
            out_specs=vmem(),
            scratch_shapes=scratch,
            compiler_params=grant(16),
            name=name,
        )(*kernel, *ins, *stats, *operands, place)

    pair = [pltpu.VMEM((1024, LANES), f32), pltpu.VMEM((1024, LANES), bf16)]
    own_part = final(
        own_grad_body,
        (near, near_other, weight_t),
        (own, depth),
        [pltpu.VMEM((own, depth), bf16)] + pair * 2,
        4,
        "own_grad",
    )
    parts = everyone(own_part)
    pair = [pltpu.VMEM((512, rows), f32), pltpu.VMEM((512, rows), bf16)]
    proto_grad = final(
        proto_grad_body,
        (near, near_other, far, far_other, weight_t),
        (depth // n_dp, cols),
        [pltpu.VMEM((rows, depth), bf16)] + pair * 2,
        10,
        "proto_grad",
    )
    feature_grad = fold(parts, jnp.add)
    return (proto_grad, feature_grad)


def solution(mesh):
    n_dp = mesh.shape["dp"]
    n_proto = mesh.shape["proto"]

    def shards(teacher_feat, student_feat, proto_weight):
        own, depth = teacher_feat.shape
        cols = proto_weight.shape[1]
        fits = (
            own * n_dp * cols * 4 <= KERNEL_BYTES
            and own == LANES
            and depth == LANES
            and cols % (PARTS * 1024) == 0
            and n_dp & (n_dp - 1) == 0
            and n_proto & (n_proto - 1) == 0
            and 2 <= n_proto <= 8
            and depth % (n_dp * SUB) == 0
        )
        plan = all_crops if fits else split_crops
        return plan(teacher_feat, student_feat, proto_weight)

    return jax.shard_map(
        shards,
        mesh=mesh,
        in_specs=(P("dp", None), P("dp", None), P(None, "proto")),
        out_specs=(P("dp", "proto"), P("dp", None)),
        check_vma=False,
    )
```

time: 285 us -> 108 us (0.38)
  blocking collectives: 137 us -> 0 us
  waiting for transfers between devices: 86 us -> 20.2 us
  Pallas kernels: 0 us -> 60.8 us
  starting transfers between devices: 0.08 us -> 22.1 us
  other arithmetic: 23.3 us -> 1.5 us
  between operations: 15.6 us -> 0.74 us
  matrix products: 10.1 us -> 0 us
  local copies, waits for them, and re-layouts: 11.9 us -> 2.35 us
    psum x6 -> x0, blocking collectives: 121 us -> none  [the longest x3 104 us: shards(): col_scale = 1.0 / lax.psum(col_part, 'dp')]
    unnamed x3 -> x0, waiting for transfers between devices: 66.7 us -> none
    pallas_call x0 -> x7, Pallas kernels: none -> 60.8 us  [the longest x3 35.4 us: sweep(): pl.pallas_call(lambda *refs: sweep_body(first, last, len(ins), len(extra)...]
    ppermute x0 -> x24, starting transfers between devices: none -> 22.1 us  [swap(): lax.ppermute(x, axis, [(i, i ^ bit) for i in range(lax.axis_size(axis))])]
    ppermute x0 -> x24, waiting for transfers between devices: none -> 20.2 us  [swap(): lax.ppermute(x, axis, [(i, i ^ bit) for i in range(lax.axis_size(axis))])]
    psum x1 -> x0, waiting for transfers between devices: 19.4 us -> none  [shards(): feature_grad = lax.psum(input_part, 'proto')]
    reduce_sum x7 -> x0, other arithmetic: 18.8 us -> none  [the longest x3 9.18 us: shards(): row_part = jnp.sum(kernel() * col_scale[None, :], axis=1)]
    all_gather x3 -> x0, blocking collectives: 16.4 us -> none  [combined_all(): everything = jax.tree.map(lambda part: lax.all_gather(part, axis), value)]
  transfers between devices with their start and end apart: 2 -> 24, of which waited for: 2 -> 12; matrix products, arithmetic and copies ran while one was open for 3% -> 0% of each run, Pallas kernels for 0% -> 56%
where the time goes in v3:
time: 108 us
  Pallas kernels  60.8 us (56%)
  starting transfers between devices  22.1 us (20%)
  waiting for transfers between devices  20.2 us (19%)
  local copies, waits for them, and re-layouts  2.35 us (2%)
  other arithmetic  1.5 us (1%)
    pallas_call x3, Pallas kernels, sweep(): pl.pallas_call(lambda *refs: sweep_body(first, last, len(ins), len(extra)...  35.4 us
    ppermute x24, starting transfers between devices, swap(): lax.ppermute(x, axis, [(i, i ^ bit) for i in range(lax.axis_size(axis))])  22.1 us
    ppermute x24, waiting for transfers between devices, swap(): lax.ppermute(x, axis, [(i, i ^ bit) for i in range(lax.axis_size(axis))])  20.2 us
    pallas_call x2, Pallas kernels, final(): pl.pallas_call(lambda *refs: body(len(ins), *refs), out_shape=jax.ShapeDt...  17 us
    pallas_call x1, Pallas kernels, all_crops(): pl.pallas_call(scores_body, out_shape=(k_shape,) * PARTS + (flat,), in_sp...  6.29 us
    unnamed x4, local copies, waits for them, and re-layouts  2.35 us
    pallas_call x1, Pallas kernels, all_crops(): pl.pallas_call(own_body, out_shape=(jax.ShapeDtypeStruct((half + STAT_ROW...  2.16 us
  transfers between devices with their start and end apart: 24, of which 12 were waited for; matrix products, arithmetic and copies ran while one was open for 0% of the time, Pallas kernels for 56%

profile of v3, /device:TPU:0, one launch (start us, length us, event | category | flops | bytes accessed | tf_op | source)
XLA Modules:
  0.0 107.7 jit_solution(15790389779722530802)
XLA Ops:
  0.6 0.7 bitcast_convert_fusion
  1.4 4.1 %collective-permute-start = (f32[1,64,128]{2,1,0:T(8,128)S(1)}, f32[1,64,128]{2,1,0:T(8,128)S(1)}, u32[]{:S(2)}, u32[]{:S(2)}) collective-permute-start(f32[1,64,128]{2,1,0:T(8,128)S(1)} %bitcast_convert_fusion), channel_id=1, source_target_pairs={{0,16},{4,20},{8,24},{12,28},{16,0},{20,4},{24,8},{28,12},{1,17},{... | collective-permute-start | bytes 98312 | tf_op jit(solution)/shard_map/ppermute | solution.py:92
  5.4 2.2 %collective-permute-done = f32[1,64,128]{2,1,0:T(8,128)S(1)} collective-permute-done((f32[1,64,128]{2,1,0:T(8,128)S(1)}, f32[1,64,128]{2,1,0:T(8,128)S(1)}, u32[]{:S(2)}, u32[]{:S(2)}) %collective-permute-start) | collective-permute-done | bytes 32800 | tf_op jit(solution)/shard_map/ppermute | solution.py:92
  7.7 1.6 %collective-permute-start.1 = (f32[2,64,128]{2,1,0:T(8,128)S(1)}, f32[2,64,128]{2,1,0:T(8,128)S(1)}, u32[]{:S(2)}, u32[]{:S(2)}) collective-permute-start(f32[2,64,128]{2,1,0:T(8,128)S(1)} %pad_maximum_fusion.4), channel_id=1, source_target_pairs={{0,8},{4,12},{8,0},{12,4},{16,24},{20,28},{24,16},{28,20},{1,9},{5... | collective-permute-start | bytes 196616 | tf_op jit(solution)/shard_map/ppermute | solution.py:92
  9.3 1.6 %copy-done = bf16[128,8192]{1,0:T(8,128)(2,1)S(1)} copy-done((bf16[128,8192]{1,0:T(8,128)(2,1)S(1)}, bf16[128,8192]{1,0:T(8,128)(2,1)}, u32[]{:S(2)}) %copy-start) | copy-done | bytes 2097176
  10.9 0.8 copy-done.1
  11.7 2.2 %own_stats.1 = (f32[72,128]{1,0:T(8,128)S(1)}, bf16[8192,128]{1,0:T(8,128)(2,1)S(1)}) custom-call(s32[2]{0:T(128)S(1)} %pad_add_fusion.place_ref.refs_17_.refs_15_, bf16[128,128]{1,0:T(8,128)(2,1)S(1)} %copy-done.1, bf16[128,8192]{1,0:T(8,128)(2,1)S(1)} %copy-done), custom_call_target="tpu_custom_call" | custom-call | tf_op jit(solution)/shard_map/own_stats/pallas_call | solution.py:387
  13.8 2.9 %collective-permute-start.10 = (f32[1,72,128]{2,1,0:T(8,128)S(1)}, f32[1,72,128]{2,1,0:T(8,128)S(1)}, u32[]{:S(2)}, u32[]{:S(2)}) collective-permute-start(f32[1,72,128]{2,1,0:T(8,128)S(1)} %bitcast.6), channel_id=1, source_target_pairs={{0,16},{4,20},{8,24},{12,28},{16,0},{20,4},{24,8},{28,12},{1,17},{... | collective-permute-start | bytes 110600 | tf_op jit(solution)/shard_map/ppermute | solution.py:92
  16.7 1.6 %collective-permute-start.2 = (f32[4,64,128]{2,1,0:T(8,128)S(1)}, f32[4,64,128]{2,1,0:T(8,128)S(1)}, u32[]{:S(2)}, u32[]{:S(2)}) collective-permute-start(f32[4,64,128]{2,1,0:T(8,128)S(1)} %pad_maximum_fusion.2), channel_id=1, source_target_pairs={{0,4},{4,0},{8,12},{12,8},{16,20},{20,16},{24,28},{28,24},{1,5},{5... | collective-permute-start | bytes 393224 | tf_op jit(solution)/shard_map/ppermute | solution.py:92
  18.3 0.7 collective-permute-done.10
  19.3 2.5 %collective-permute-done.2 = f32[4,64,128]{2,1,0:T(8,128)S(1)} collective-permute-done((f32[4,64,128]{2,1,0:T(8,128)S(1)}, f32[4,64,128]{2,1,0:T(8,128)S(1)}, u32[]{:S(2)}, u32[]{:S(2)}) %collective-permute-start.2) | collective-permute-done | bytes 131104 | tf_op jit(solution)/shard_map/ppermute | solution.py:92
  21.9 1.6 %collective-permute-done.11 = f32[2,72,128]{2,1,0:T(8,128)S(1)} collective-permute-done((f32[2,72,128]{2,1,0:T(8,128)S(1)}, f32[2,72,128]{2,1,0:T(8,128)S(1)}, u32[]{:S(2)}, u32[]{:S(2)}) %collective-permute-start.11) | collective-permute-done | bytes 73760 | tf_op jit(solution)/shard_map/ppermute | solution.py:92
  23.4 1.8 %collective-permute-start.12 = (f32[4,72,128]{2,1,0:T(8,128)S(1)}, f32[4,72,128]{2,1,0:T(8,128)S(1)}, u32[]{:S(2)}, u32[]{:S(2)}) collective-permute-start(f32[4,72,128]{2,1,0:T(8,128)S(1)} %pad_maximum_fusion.1.refs_8_.refs_12_), channel_id=1, source_target_pairs={{0,4},{4,0},{8,12},{12,8},{16,20},{20,16},{24,28},{28,24},{1,5},{5... | collective-permute-start | bytes 442376 | tf_op jit(solution)/shard_map/ppermute | solution.py:92
  25.2 3.4 %collective-permute-done.12.refs_9_.refs_14_ = f32[4,72,128]{2,1,0:T(8,128)S(1)} collective-permute-done((f32[4,72,128]{2,1,0:T(8,128)S(1)}, f32[4,72,128]{2,1,0:T(8,128)S(1)}, u32[]{:S(2)}, u32[]{:S(2)}) %collective-permute-start.12) | collective-permute-done | bytes 147488 | tf_op jit(solution)/shard_map/ppermute | solution.py:92
  28.7 6.3 %scores.1 = (f32[2048,1024]{1,0:T(8,128)S(1)}, f32[2048,1024]{1,0:T(8,128)S(1)}, f32[2048,1024]{1,0:T(8,128)S(1)}, f32[2048,1024]{1,0:T(8,128)S(1)}, f32[8,128]{1,0:T(8,128)S(1)}) custom-call(s32[2]{0:T(128)S(1)} %pad_add_fusion.place_ref.refs_17_.refs_15_, f32[8,64,128]{2,1,0:T(8,128)S(1)} %pad_maximum_fusion.mine_ref, ...), custom_call_target="tpu_custom_call" | custom-call | tf_op jit(solution)/shard_map/scores/pallas_call | solution.py:403
  35.5 1.7 %collective-permute-start.5 = (f32[8,128]{1,0:T(8,128)S(1)}, f32[8,128]{1,0:T(8,128)S(1)}, u32[]{:S(2)}, u32[]{:S(2)}) collective-permute-start(f32[8,128]{1,0:T(8,128)S(1)} %get-tuple-element.24.refs_4_), channel_id=1, source_target_pairs={{0,2},{1,3},{2,0},{3,1},{4,6},{5,7},{6,4},{7,5},{8,10},{9,11},{10,... | collective-permute-start | bytes 12296 | tf_op jit(solution)/shard_map/ppermute | solution.py:92
  37.3 1.9 %collective-permute-done.5.refs_6_ = f32[8,128]{1,0:T(8,128)S(1)} collective-permute-done((f32[8,128]{1,0:T(8,128)S(1)}, f32[8,128]{1,0:T(8,128)S(1)}, u32[]{:S(2)}, u32[]{:S(2)}) %collective-permute-start.5) | collective-permute-done | bytes 4128 | tf_op jit(solution)/shard_map/ppermute | solution.py:92
  39.1 1.2 %collective-permute-done.6.refs_7_ = f32[8,128]{1,0:T(8,128)S(1)} collective-permute-done((f32[8,128]{1,0:T(8,128)S(1)}, f32[8,128]{1,0:T(8,128)S(1)}, u32[]{:S(2)}, u32[]{:S(2)}) %collective-permute-start.6) | collective-permute-done | bytes 4128 | tf_op jit(solution)/shard_map/ppermute | solution.py:92
  40.3 14.6 %sweep_first.1 = (f32[2048,1024]{1,0:T(8,128)S(1)}, f32[2048,1024]{1,0:T(8,128)S(1)}, f32[2048,1024]{1,0:T(8,128)S(1)}, f32[2048,1024]{1,0:T(8,128)S(1)}, f32[8,128]{1,0:T(8,128)S(1)}) custom-call(f32[2048,1024]{1,0:T(8,128)S(1)} %get-tuple-element.20.refs_0_, ...), custom_call_target="tpu_custom_call", output_to_operand_aliasing={{0}: (0, {}), {1}: (1, {}), {2}: (2, {}), {3}: (3, {})} | custom-call | tf_op jit(solution)/shard_map/sweep_first/pallas_call | solution.py:417
  55.6 1.2 %collective-permute-start.9 = (f32[8,128]{1,0:T(8,128)S(1)}, f32[8,128]{1,0:T(8,128)S(1)}, u32[]{:S(2)}, u32[]{:S(2)}) collective-permute-start(f32[8,128]{1,0:T(8,128)S(1)} %get-tuple-element.29.refs_4_), channel_id=1, source_target_pairs={{0,3},{1,2},{2,1},{3,0},{4,7},{5,6},{6,5},{7,4},{8,11},{9,10},{10,... | collective-permute-start | bytes 12296 | tf_op jit(solution)/shard_map/ppermute | solution.py:92
  56.8 1.9 %collective-permute-done.8.refs_6_ = f32[8,128]{1,0:T(8,128)S(1)} collective-permute-done((f32[8,128]{1,0:T(8,128)S(1)}, f32[8,128]{1,0:T(8,128)S(1)}, u32[]{:S(2)}, u32[]{:S(2)}) %collective-permute-start.8) | collective-permute-done | bytes 4128 | tf_op jit(solution)/shard_map/ppermute | solution.py:92
  58.7 9.6 %sweep.1.refs_4_.refs_8_ = f32[24,128]{1,0:T(8,128)S(1)} custom-call(f32[2048,1024]{1,0:T(8,128)S(1)} %get-tuple-element.25.refs_0_, f32[2048,1024]{1,0:T(8,128)S(1)} %get-tuple-element.26.refs_1_, f32[2048,1024]{1,0:T(8,128)S(1)} %get-tuple-element.27.refs_2_, f32[2048,1024]{1,0:T(8,128)S(1)} %get-tuple-element.28.refs_3_, ...), custom_call_target="tpu_custom_call" | custom-call | tf_op jit(solution)/shard_map/sweep/pallas_call | solution.py:417
  68.4 1.4 %collective-permute-start.14 = (f32[24,128]{1,0:T(8,128)S(1)}, f32[24,128]{1,0:T(8,128)S(1)}, u32[]{:S(2)}, u32[]{:S(2)}) collective-permute-start(f32[24,128]{1,0:T(8,128)S(1)} %sweep.1.refs_4_.refs_8_), channel_id=1, source_target_pairs={{0,2},{1,3},{2,0},{3,1},{4,6},{5,7},{6,4},{7,5},{8,10},{9,11},{10,... | collective-permute-start | bytes 36872 | tf_op jit(solution)/shard_map/ppermute | solution.py:92
  70.2 1.9 %collective-permute-done.14.refs_6_.refs_10_ = f32[24,128]{1,0:T(8,128)S(1)} collective-permute-done((f32[24,128]{1,0:T(8,128)S(1)}, f32[24,128]{1,0:T(8,128)S(1)}, u32[]{:S(2)}, u32[]{:S(2)}) %collective-permute-start.14) | collective-permute-done | bytes 12320 | tf_op jit(solution)/shard_map/ppermute | solution.py:92
  72.1 0.9 collective-permute-done.15.refs_7_.refs_11_
  73.0 11.2 %sweep_last.1 = (f32[2048,1024]{1,0:T(8,128)S(1)}, f32[2048,1024]{1,0:T(8,128)S(1)}, f32[2048,1024]{1,0:T(8,128)S(1)}, f32[2048,1024]{1,0:T(8,128)S(1)}, f32[8,128]{1,0:T(8,128)S(1)}) custom-call(f32[2048,1024]{1,0:T(8,128)S(1)} %get-tuple-element.25.refs_0_, ...), custom_call_target="tpu_custom_call", output_to_operand_aliasing={{0}: (0, {}), {1}: (1, {}), {2}: (2, {}), {3}: (3, {})} | custom-call | tf_op jit(solution)/shard_map/sweep_last/pallas_call | solution.py:417
  84.4 0.7 collective-permute-start.17
  85.1 1.0 collective-permute-start.18
  86.2 1.9 %collective-permute-done.17.refs_6_ = f32[8,128]{1,0:T(8,128)S(1)} collective-permute-done((f32[8,128]{1,0:T(8,128)S(1)}, f32[8,128]{1,0:T(8,128)S(1)}, u32[]{:S(2)}, u32[]{:S(2)}) %collective-permute-start.17) | collective-permute-done | bytes 4128 | tf_op jit(solution)/shard_map/ppermute | solution.py:92
  88.1 2.5 %own_grad.1 = f32[128,128]{1,0:T(8,128)S(1)} custom-call(f32[2048,1024]{1,0:T(8,128)S(1)} %get-tuple-element.31.refs_0_, f32[2048,1024]{1,0:T(8,128)S(1)} %get-tuple-element.32.refs_1_, f32[2048,1024]{1,0:T(8,128)S(1)} %get-tuple-element.33.refs_2_, f32[2048,1024]{1,0:T(8,128)S(1)} %get-tuple-element.34.refs_3_, f32[8,128]{1,0:T(8,128)S(1)} %get-tuple-element.35.refs_4_, ...), custom_call_target="tpu_custom_call" | custom-call | tf_op jit(solution)/shard_map/own_grad/pallas_call | solution.py:441
  90.8 1.3 %collective-permute-start.22 = (f32[128,128]{1,0:T(8,128)S(1)}, f32[128,128]{1,0:T(8,128)S(1)}, u32[]{:S(2)}, u32[]{:S(2)}) collective-permute-start(f32[128,128]{1,0:T(8,128)S(1)} %own_grad.1), channel_id=1, source_target_pairs={{0,2},{1,3},{2,0},{3,1},{4,6},{5,7},{6,4},{7,5},{8,10},{9,11},{10,... | collective-permute-start | bytes 196616 | tf_op jit(solution)/shard_map/ppermute | solution.py:92
  92.6 14.5 %proto_grad.1 = f32[16,8192]{1,0:T(8,128)} custom-call(f32[2048,1024]{1,0:T(8,128)S(1)} %get-tuple-element.31.refs_0_, f32[2048,1024]{1,0:T(8,128)S(1)} %get-tuple-element.32.refs_1_, f32[2048,1024]{1,0:T(8,128)S(1)} %get-tuple-element.33.refs_2_, f32[2048,1024]{1,0:T(8,128)S(1)} %get-tuple-element.34.refs_3_, f32[8,128]{1,0:T(8,128)S(1)} %get-tuple-element.35.refs_4_, ...), custom_call_target="tpu_custom_call" | custom-call | tf_op jit(solution)/shard_map/proto_grad/pallas_call | solution.py:441
  (35 shorter events, 3.8 us)
Async XLA Ops:
  1.4 6.3 %collective-permute-start = (f32[1,64,128]{2,1,0:T(8,128)S(1)}, f32[1,64,128]{2,1,0:T(8,128)S(1)}, u32[]{:S(2)}, u32[]{:S(2)}) collective-permute-start(f32[1,64,128]{2,1,0:T(8,128)S(1)} %bitcast_convert_fusion), channel_id=1, source_target_pairs={{0,16},{4,20},{8,24},{12,28},{16,0},{20,4},{24,8},{28,12},{1,17},{... | collective-permute-start | bytes 98312 | tf_op jit(solution)/shard_map/ppermute | solution.py:92
  7.7 9.0 %collective-permute-start.1 = (f32[2,64,128]{2,1,0:T(8,128)S(1)}, f32[2,64,128]{2,1,0:T(8,128)S(1)}, u32[]{:S(2)}, u32[]{:S(2)}) collective-permute-start(f32[2,64,128]{2,1,0:T(8,128)S(1)} %pad_maximum_fusion.4), channel_id=1, source_target_pairs={{0,8},{4,12},{8,0},{12,4},{16,24},{20,28},{24,16},{28,20},{1,9},{5... | collective-permute-start | bytes 196616 | tf_op jit(solution)/shard_map/ppermute | solution.py:92
  9.3 1.6 %copy-start = (bf16[128,8192]{1,0:T(8,128)(2,1)S(1)}, bf16[128,8192]{1,0:T(8,128)(2,1)}, u32[]{:S(2)}) copy-start(bf16[128,8192]{1,0:T(8,128)(2,1)} %w_ref.1) | copy-start | bytes 6291460
  10.9 0.8 copy-start.1
  13.8 5.2 %collective-permute-start.10 = (f32[1,72,128]{2,1,0:T(8,128)S(1)}, f32[1,72,128]{2,1,0:T(8,128)S(1)}, u32[]{:S(2)}, u32[]{:S(2)}) collective-permute-start(f32[1,72,128]{2,1,0:T(8,128)S(1)} %bitcast.6), channel_id=1, source_target_pairs={{0,16},{4,20},{8,24},{12,28},{16,0},{20,4},{24,8},{28,12},{1,17},{... | collective-permute-start | bytes 110600 | tf_op jit(solution)/shard_map/ppermute | solution.py:92
  16.7 5.0 %collective-permute-start.2 = (f32[4,64,128]{2,1,0:T(8,128)S(1)}, f32[4,64,128]{2,1,0:T(8,128)S(1)}, u32[]{:S(2)}, u32[]{:S(2)}) collective-permute-start(f32[4,64,128]{2,1,0:T(8,128)S(1)} %pad_maximum_fusion.2), channel_id=1, source_target_pairs={{0,4},{4,0},{8,12},{12,8},{16,20},{20,16},{24,28},{28,24},{1,5},{5... | collective-permute-start | bytes 393224 | tf_op jit(solution)/shard_map/ppermute | solution.py:92
  19.1 4.4 %collective-permute-start.11 = (f32[2,72,128]{2,1,0:T(8,128)S(1)}, f32[2,72,128]{2,1,0:T(8,128)S(1)}, u32[]{:S(2)}, u32[]{:S(2)}) collective-permute-start(f32[2,72,128]{2,1,0:T(8,128)S(1)} %pad_maximum_fusion.3), channel_id=1, source_target_pairs={{0,8},{4,12},{8,0},{12,4},{16,24},{20,28},{24,16},{28,20},{1,9},{5... | collective-permute-start | bytes 221192 | tf_op jit(solution)/shard_map/ppermute | solution.py:92
  21.8 6.9 %collective-permute-start.3 = (f32[8,64,128]{2,1,0:T(8,128)S(1)}, f32[8,64,128]{2,1,0:T(8,128)S(1)}, u32[]{:S(2)}, u32[]{:S(2)}) collective-permute-start(f32[8,64,128]{2,1,0:T(8,128)S(1)} %pad_maximum_fusion.mine_ref), channel_id=1, source_target_pairs={{0,1},{1,0},{2,3},{3,2},{4,5},{5,4},{6,7},{7,6},{8,9},{9,8},{10,11... | collective-permute-start | bytes 786440 | tf_op jit(solution)/shard_map/ppermute | solution.py:92
  23.4 5.2 %collective-permute-start.12 = (f32[4,72,128]{2,1,0:T(8,128)S(1)}, f32[4,72,128]{2,1,0:T(8,128)S(1)}, u32[]{:S(2)}, u32[]{:S(2)}) collective-permute-start(f32[4,72,128]{2,1,0:T(8,128)S(1)} %pad_maximum_fusion.1.refs_8_.refs_12_), channel_id=1, source_target_pairs={{0,4},{4,0},{8,12},{12,8},{16,20},{20,16},{24,28},{28,24},{1,5},{5... | collective-permute-start | bytes 442376 | tf_op jit(solution)/shard_map/ppermute | solution.py:92
  25.2 60.9 %collective-permute-start.19 = (f32[4,72,128]{2,1,0:T(8,128)S(1)}, f32[4,72,128]{2,1,0:T(8,128)S(1)}, u32[]{:S(2)}, u32[]{:S(2)}) collective-permute-start(f32[4,72,128]{2,1,0:T(8,128)S(1)} %pad_maximum_fusion.1.refs_8_.refs_12_), channel_id=1, source_target_pairs={{0,1},{1,0},{2,3},{3,2},{4,5},{5,4},{6,7},{7,6},{8,9},{9,8},{10,11... | collective-permute-start | bytes 442376 | tf_op jit(solution)/shard_map/ppermute | solution.py:92
  28.7 63.9 %collective-permute-start.20 = (f32[4,72,128]{2,1,0:T(8,128)S(1)}, f32[4,72,128]{2,1,0:T(8,128)S(1)}, u32[]{:S(2)}, u32[]{:S(2)}) collective-permute-start(f32[4,72,128]{2,1,0:T(8,128)S(1)} %collective-permute-done.12.refs_9_.refs_14_), channel_id=1, source_target_pairs={{0,1},{1,0},{2,3},{3,2},{4,5},{5,4},{6,7},{7,6},{8,9},{9,8},{10,11... | collective-permute-start | bytes 442376 | tf_op jit(solution)/shard_map/ppermute | solution.py:92
  35.0 2.3 %collective-permute-start.4 = (f32[8,128]{1,0:T(8,128)S(1)}, f32[8,128]{1,0:T(8,128)S(1)}, u32[]{:S(2)}, u32[]{:S(2)}) collective-permute-start(f32[8,128]{1,0:T(8,128)S(1)} %get-tuple-element.24.refs_4_), channel_id=1, source_target_pairs={{0,1},{1,0},{2,3},{3,2},{4,5},{5,4},{6,7},{7,6},{8,9},{9,8},{10,11... | collective-permute-start | bytes 12296 | tf_op jit(solution)/shard_map/ppermute | solution.py:92
  35.5 3.6 %collective-permute-start.5 = (f32[8,128]{1,0:T(8,128)S(1)}, f32[8,128]{1,0:T(8,128)S(1)}, u32[]{:S(2)}, u32[]{:S(2)}) collective-permute-start(f32[8,128]{1,0:T(8,128)S(1)} %get-tuple-element.24.refs_4_), channel_id=1, source_target_pairs={{0,2},{1,3},{2,0},{3,1},{4,6},{5,7},{6,4},{7,5},{8,10},{9,11},{10,... | collective-permute-start | bytes 12296 | tf_op jit(solution)/shard_map/ppermute | solution.py:92
  37.3 3.1 %collective-permute-start.6 = (f32[8,128]{1,0:T(8,128)S(1)}, f32[8,128]{1,0:T(8,128)S(1)}, u32[]{:S(2)}, u32[]{:S(2)}) collective-permute-start(f32[8,128]{1,0:T(8,128)S(1)} %get-tuple-element.24.refs_4_), channel_id=1, source_target_pairs={{0,3},{1,2},{2,1},{3,0},{4,7},{5,6},{6,5},{7,4},{8,11},{9,10},{10,... | collective-permute-start | bytes 12296 | tf_op jit(solution)/shard_map/ppermute | solution.py:92
  54.9 1.9 %collective-permute-start.7 = (f32[8,128]{1,0:T(8,128)S(1)}, f32[8,128]{1,0:T(8,128)S(1)}, u32[]{:S(2)}, u32[]{:S(2)}) collective-permute-start(f32[8,128]{1,0:T(8,128)S(1)} %get-tuple-element.29.refs_4_), channel_id=1, source_target_pairs={{0,1},{1,0},{2,3},{3,2},{4,5},{5,4},{6,7},{7,6},{8,9},{9,8},{10,11... | collective-permute-start | bytes 12296 | tf_op jit(solution)/shard_map/ppermute | solution.py:92
  55.0 3.6 %collective-permute-start.8 = (f32[8,128]{1,0:T(8,128)S(1)}, f32[8,128]{1,0:T(8,128)S(1)}, u32[]{:S(2)}, u32[]{:S(2)}) collective-permute-start(f32[8,128]{1,0:T(8,128)S(1)} %get-tuple-element.29.refs_4_), channel_id=1, source_target_pairs={{0,2},{1,3},{2,0},{3,1},{4,6},{5,7},{6,4},{7,5},{8,10},{9,11},{10,... | collective-permute-start | bytes 12296 | tf_op jit(solution)/shard_map/ppermute | solution.py:92
  55.6 3.1 %collective-permute-start.9 = (f32[8,128]{1,0:T(8,128)S(1)}, f32[8,128]{1,0:T(8,128)S(1)}, u32[]{:S(2)}, u32[]{:S(2)}) collective-permute-start(f32[8,128]{1,0:T(8,128)S(1)} %get-tuple-element.29.refs_4_), channel_id=1, source_target_pairs={{0,3},{1,2},{2,1},{3,0},{4,7},{5,6},{6,5},{7,4},{8,11},{9,10},{10,... | collective-permute-start | bytes 12296 | tf_op jit(solution)/shard_map/ppermute | solution.py:92
  68.3 1.9 %collective-permute-start.13 = (f32[24,128]{1,0:T(8,128)S(1)}, f32[24,128]{1,0:T(8,128)S(1)}, u32[]{:S(2)}, u32[]{:S(2)}) collective-permute-start(f32[24,128]{1,0:T(8,128)S(1)} %sweep.1.refs_4_.refs_8_), channel_id=1, source_target_pairs={{0,1},{1,0},{2,3},{3,2},{4,5},{5,4},{6,7},{7,6},{8,9},{9,8},{10,11... | collective-permute-start | bytes 36872 | tf_op jit(solution)/shard_map/ppermute | solution.py:92
  68.4 3.7 %collective-permute-start.14 = (f32[24,128]{1,0:T(8,128)S(1)}, f32[24,128]{1,0:T(8,128)S(1)}, u32[]{:S(2)}, u32[]{:S(2)}) collective-permute-start(f32[24,128]{1,0:T(8,128)S(1)} %sweep.1.refs_4_.refs_8_), channel_id=1, source_target_pairs={{0,2},{1,3},{2,0},{3,1},{4,6},{5,7},{6,4},{7,5},{8,10},{9,11},{10,... | collective-permute-start | bytes 36872 | tf_op jit(solution)/shard_map/ppermute | solution.py:92
  69.9 3.1 %collective-permute-start.15 = (f32[24,128]{1,0:T(8,128)S(1)}, f32[24,128]{1,0:T(8,128)S(1)}, u32[]{:S(2)}, u32[]{:S(2)}) collective-permute-start(f32[24,128]{1,0:T(8,128)S(1)} %sweep.1.refs_4_.refs_8_), channel_id=1, source_target_pairs={{0,3},{1,2},{2,1},{3,0},{4,7},{5,6},{6,5},{7,4},{8,11},{9,10},{10,... | collective-permute-start | bytes 36872 | tf_op jit(solution)/shard_map/ppermute | solution.py:92
  84.2 1.9 %collective-permute-start.16 = (f32[8,128]{1,0:T(8,128)S(1)}, f32[8,128]{1,0:T(8,128)S(1)}, u32[]{:S(2)}, u32[]{:S(2)}) collective-permute-start(f32[8,128]{1,0:T(8,128)S(1)} %get-tuple-element.35.refs_4_), channel_id=1, source_target_pairs={{0,1},{1,0},{2,3},{3,2},{4,5},{5,4},{6,7},{7,6},{8,9},{9,8},{10,11... | collective-permute-start | bytes 12296 | tf_op jit(solution)/shard_map/ppermute | solution.py:92
  84.4 3.6 %collective-permute-start.17 = (f32[8,128]{1,0:T(8,128)S(1)}, f32[8,128]{1,0:T(8,128)S(1)}, u32[]{:S(2)}, u32[]{:S(2)}) collective-permute-start(f32[8,128]{1,0:T(8,128)S(1)} %get-tuple-element.35.refs_4_), channel_id=1, source_target_pairs={{0,2},{1,3},{2,0},{3,1},{4,6},{5,7},{6,4},{7,5},{8,10},{9,11},{10,... | collective-permute-start | bytes 12296 | tf_op jit(solution)/shard_map/ppermute | solution.py:92
  85.1 3.0 %collective-permute-start.18 = (f32[8,128]{1,0:T(8,128)S(1)}, f32[8,128]{1,0:T(8,128)S(1)}, u32[]{:S(2)}, u32[]{:S(2)}) collective-permute-start(f32[8,128]{1,0:T(8,128)S(1)} %get-tuple-element.35.refs_4_), channel_id=1, source_target_pairs={{0,3},{1,2},{2,1},{3,0},{4,7},{5,6},{6,5},{7,4},{8,11},{9,10},{10,... | collective-permute-start | bytes 12296 | tf_op jit(solution)/shard_map/ppermute | solution.py:92
  90.7 16.4 %collective-permute-start.21 = (f32[128,128]{1,0:T(8,128)S(1)}, f32[128,128]{1,0:T(8,128)S(1)}, u32[]{:S(2)}, u32[]{:S(2)}) collective-permute-start(f32[128,128]{1,0:T(8,128)S(1)} %own_grad.1), channel_id=1, source_target_pairs={{0,1},{1,0},{2,3},{3,2},{4,5},{5,4},{6,7},{7,6},{8,9},{9,8},{10,11... | collective-permute-start | bytes 196616 | tf_op jit(solution)/shard_map/ppermute | solution.py:92
  90.8 16.2 %collective-permute-start.22 = (f32[128,128]{1,0:T(8,128)S(1)}, f32[128,128]{1,0:T(8,128)S(1)}, u32[]{:S(2)}, u32[]{:S(2)}) collective-permute-start(f32[128,128]{1,0:T(8,128)S(1)} %own_grad.1), channel_id=1, source_target_pairs={{0,2},{1,3},{2,0},{3,1},{4,6},{5,7},{6,4},{7,5},{8,10},{9,11},{10,... | collective-permute-start | bytes 196616 | tf_op jit(solution)/shard_map/ppermute | solution.py:92
  92.2 14.9 %collective-permute-start.23 = (f32[128,128]{1,0:T(8,128)S(1)}, f32[128,128]{1,0:T(8,128)S(1)}, u32[]{:S(2)}, u32[]{:S(2)}) collective-permute-start(f32[128,128]{1,0:T(8,128)S(1)} %own_grad.1), channel_id=1, source_target_pairs={{0,3},{1,2},{2,1},{3,0},{4,7},{5,6},{6,5},{7,4},{8,11},{9,10},{10,... | collective-permute-start | bytes 196616 | tf_op jit(solution)/shard_map/ppermute | solution.py:92

commit v4 on v3

--- a/solution.py
+++ b/solution.py
@@ -180,7 +180,7 @@
     extra_refs, refs = refs[:n_extra], refs[n_extra:]
     if first or last:
         k_refs, refs = refs[:PARTS], refs[PARTS:]
-    o_ref = refs[0]
+    o_ref, y_scr = refs
     per, rows = k_refs[0].shape
     n = rows // LANES
     if first:
@@ -188,65 +188,75 @@
     else:
         scale = 1.0 / fold([x[0:n, :] for x in in_refs], jnp.add)
     wide = lane_rows(scale)
-    unroll = 16
-    group = 2 if last else 4
+    unroll = 32
     chunk = unroll * SUB
     tiles = [slice(q * LANES, (q + 1) * LANES) for q in range(n)]
 
-    def phases(p_down, i_down, p_across, i_across, inverse, acc):
-        acc = list(acc)
-        new = []
-
-        def load(g):
-            out = []
-            for u in range(g, g + group):
-                at = pl.ds(pl.multiple_of(i_down * chunk, chunk) + u * SUB, SUB)
-                x = [k_refs[p_down][at, tiles[q]] for q in range(n)]
-                out.append((at, [x[q] - wide[q] if first else x[q] * wide[q] for q in range(n)]))
-            return out
-
-        ahead = load(0) if p_down is not None else None
+    def rows_of(i, u):
+        return pl.ds(pl.multiple_of(i * chunk, chunk) + u * SUB, SUB)
+
+    def stepped(group, load, use, carry):
+        ahead = [load(u) for u in range(group)]
         for g in range(0, unroll, group):
-            if p_down is not None:
-                now = ahead
-                if g + group < unroll and (first or last):
-                    ahead = load(g + group)
-            if p_across is not None:
-                done = []
-                for u in range(g, g + group):
-                    at = pl.ds(pl.multiple_of(i_across * chunk, chunk) + u * SUB, SUB)
+            now = ahead
+            if g + group < unroll:
+                ahead = [load(u) for u in range(g + group, g + 2 * group)]
+            for k, x in enumerate(now):
+                carry = use(g + k, x, carry)
+        return carry
+
+    for p in range(PARTS):
+
+        def down(i, unused, p=p):
+            def load(u):
+                x = [k_refs[p][rows_of(i, u), lanes] for lanes in tiles]
+                return [x[q] - wide[q] if first else x[q] * wide[q] for q in range(n)]
+
+            def use(u, x, carry):
+                if first:
+                    x = [jnp.exp2(v) for v in x]
                     for q in range(n):
-                        x = k_refs[p_across][at, tiles[q]] * inverse[u]
-                        acc[q] = acc[q] + x
-                        done.append((at, tiles[q], x))
+                        k_refs[p][rows_of(i, u), tiles[q]] = x[q]
+                at = pl.ds(pl.multiple_of(p * per + i * chunk, chunk) + u * SUB, SUB)
+                y_scr[at, :] = fold(x, jnp.add)
+                return carry
+
+            stepped(4 if first else 1, load, use, None)
+            return 0
+
+        lax.fori_loop(0, per // chunk, down, 0)
+
+    ones = jnp.ones((LANES, LANES), jnp.bfloat16)
+
+    def invert(i, unused):
+        at = pl.ds(pl.multiple_of(i * 1024, 1024), 1024)
+        y = y_scr[at, :]
+        high = y.astype(jnp.bfloat16)
+        low = (y - high.astype(jnp.float32)).astype(jnp.bfloat16)
+        total = jnp.dot(high, ones, preferred_element_type=jnp.float32)
+        total = total + jnp.dot(low, ones, preferred_element_type=jnp.float32)
+        y_scr[at, :] = 1.0 / total
+        return 0
+
+    lax.fori_loop(0, PARTS * per // 1024, invert, 0)
+    acc = (jnp.zeros((SUB, LANES), jnp.float32),) * n
+    for p in range(PARTS):
+
+        def across(i, acc, p=p):
+            def load(u):
+                at = pl.ds(pl.multiple_of(p * per + i * chunk, chunk) + u * SUB, SUB)
+                inverse = y_scr[at, :]
+                return [k_refs[p][rows_of(i, u), lanes] * inverse for lanes in tiles]
+
+            def use(u, x, acc):
                 if last:
-                    for at, lanes, x in done:
-                        k_refs[p_across][at, lanes] = x
-            if p_down is not None:
-                for at, x in now:
-                    if first:
-                        x = [jnp.exp2(v) for v in x]
-                        for q in range(n):
-                            k_refs[p_down][at, tiles[q]] = x[q]
-                    c = 1.0 / jnp.sum(fold(x, jnp.add), axis=1, keepdims=True)
-                    c = jnp.broadcast_to(c, (SUB, LANES))
-                    new.append(c)
-                if g + group < unroll and not (first or last):
-                    ahead = load(g + group)
-        return tuple(new), tuple(acc)
-
-    acc = (jnp.zeros((SUB, LANES), jnp.float32),) * n
-    inverse = None
-    steps = per // chunk
-    for p in range(PARTS):
-        before = None if p == 0 else p - 1
-        inverse, acc = phases(p, 0, before, steps - 1, inverse, acc)
-
-        def step(i, carry, p=p):
-            return phases(p, i + 1, p, i, *carry)
-
-        inverse, acc = lax.fori_loop(0, steps - 1, step, (inverse, acc))
-    unused, acc = phases(None, 0, PARTS - 1, steps - 1, inverse, acc)
+                    for q in range(n):
+                        k_refs[p][rows_of(i, u), tiles[q]] = x[q]
+                return tuple(acc[q] + x[q] for q in range(n))
+
+            return stepped(2 if last else 1, load, use, acc)
+
+        acc = lax.fori_loop(0, per // chunk, across, acc)
     o_ref[0:n, :] = jnp.concatenate([jnp.sum(x, axis=0, keepdims=True) for x in acc], axis=0)
     if n_extra:
         half = LANES // 2
@@ -419,6 +429,7 @@
             out_shape=kept + outs,
             in_specs=[vmem()] * (PARTS + len(ins) + len(extra)),
             out_specs=(vmem(),) * (len(kept) + len(outs)),
+            scratch_shapes=[pltpu.VMEM((cols, LANES), f32)],
             input_output_aliases={k: k for k in range(len(kept))},
             compiler_params=grant(16),
             name="sweep_first" if first else "sweep_last" if last else "sweep",

time: 108 us -> 99.6 us (0.922)
  Pallas kernels: 60.8 us -> 52.4 us
    pallas_call x3, Pallas kernels: 35.4 us -> 27 us  [sweep(): pl.pallas_call(lambda *refs: sweep_body(first, last, len(ins), len(extra)...]
  transfers between devices with their start and end apart: 24 -> 24, of which waited for: 12 -> 12; matrix products, arithmetic and copies ran while one was open for 0% -> 0% of each run, Pallas kernels for 56% -> 53%
where the time goes in v4:
time: 99.6 us; the launch traced here: 99.4 us
  Pallas kernels  52.4 us (53%)
  starting transfers between devices  22.1 us (22%)
  waiting for transfers between devices  20.2 us (20%)
  local copies, waits for them, and re-layouts  2.35 us (2%)
  other arithmetic  1.5 us (2%)
    pallas_call x3, Pallas kernels, sweep(): pl.pallas_call(lambda *refs: sweep_body(first, last, len(ins), len(extra)...  27 us
    ppermute x24, starting transfers between devices, swap(): lax.ppermute(x, axis, [(i, i ^ bit) for i in range(lax.axis_size(axis))])  22.1 us
    ppermute x24, waiting for transfers between devices, swap(): lax.ppermute(x, axis, [(i, i ^ bit) for i in range(lax.axis_size(axis))])  20.2 us
    pallas_call x2, Pallas kernels, final(): pl.pallas_call(lambda *refs: body(len(ins), *refs), out_shape=jax.ShapeDt...  17 us
    pallas_call x1, Pallas kernels, all_crops(): pl.pallas_call(scores_body, out_shape=(k_shape,) * PARTS + (flat,), in_sp...  6.29 us
    unnamed x4, local copies, waits for them, and re-layouts  2.35 us
    pallas_call x1, Pallas kernels, all_crops(): pl.pallas_call(own_body, out_shape=(jax.ShapeDtypeStruct((half + STAT_ROW...  2.16 us
  transfers between devices with their start and end apart: 24, of which 12 were waited for; matrix products, arithmetic and copies ran while one was open for 0% of the time, Pallas kernels for 53%

profile of v4, /device:TPU:0, one launch (start us, length us, event | category | flops | bytes accessed | tf_op | source)
XLA Modules:
  0.0 99.4 jit_solution(11285892149233693936)
XLA Ops:
  0.6 0.7 bitcast_convert_fusion
  1.4 4.1 %collective-permute-start = (f32[1,64,128]{2,1,0:T(8,128)S(1)}, f32[1,64,128]{2,1,0:T(8,128)S(1)}, u32[]{:S(2)}, u32[]{:S(2)}) collective-permute-start(f32[1,64,128]{2,1,0:T(8,128)S(1)} %bitcast_convert_fusion), channel_id=1, source_target_pairs={{0,16},{4,20},{8,24},{12,28},{16,0},{20,4},{24,8},{28,12},{1,17},{... | collective-permute-start | bytes 98312 | tf_op jit(solution)/shard_map/ppermute | solution.py:92
  5.4 2.2 %collective-permute-done = f32[1,64,128]{2,1,0:T(8,128)S(1)} collective-permute-done((f32[1,64,128]{2,1,0:T(8,128)S(1)}, f32[1,64,128]{2,1,0:T(8,128)S(1)}, u32[]{:S(2)}, u32[]{:S(2)}) %collective-permute-start) | collective-permute-done | bytes 32800 | tf_op jit(solution)/shard_map/ppermute | solution.py:92
  7.7 1.6 %collective-permute-start.1 = (f32[2,64,128]{2,1,0:T(8,128)S(1)}, f32[2,64,128]{2,1,0:T(8,128)S(1)}, u32[]{:S(2)}, u32[]{:S(2)}) collective-permute-start(f32[2,64,128]{2,1,0:T(8,128)S(1)} %pad_maximum_fusion.4), channel_id=1, source_target_pairs={{0,8},{4,12},{8,0},{12,4},{16,24},{20,28},{24,16},{28,20},{1,9},{5... | collective-permute-start | bytes 196616 | tf_op jit(solution)/shard_map/ppermute | solution.py:92
  9.3 1.6 %copy-done = bf16[128,8192]{1,0:T(8,128)(2,1)S(1)} copy-done((bf16[128,8192]{1,0:T(8,128)(2,1)S(1)}, bf16[128,8192]{1,0:T(8,128)(2,1)}, u32[]{:S(2)}) %copy-start) | copy-done | bytes 2097176
  10.9 0.8 copy-done.1
  11.7 2.2 %own_stats.1 = (f32[72,128]{1,0:T(8,128)S(1)}, bf16[8192,128]{1,0:T(8,128)(2,1)S(1)}) custom-call(s32[2]{0:T(128)S(1)} %pad_add_fusion.place_ref.refs_17_.refs_15_, bf16[128,128]{1,0:T(8,128)(2,1)S(1)} %copy-done.1, bf16[128,8192]{1,0:T(8,128)(2,1)S(1)} %copy-done), custom_call_target="tpu_custom_call" | custom-call | tf_op jit(solution)/shard_map/own_stats/pallas_call | solution.py:397
  13.8 2.9 %collective-permute-start.10 = (f32[1,72,128]{2,1,0:T(8,128)S(1)}, f32[1,72,128]{2,1,0:T(8,128)S(1)}, u32[]{:S(2)}, u32[]{:S(2)}) collective-permute-start(f32[1,72,128]{2,1,0:T(8,128)S(1)} %bitcast.6), channel_id=1, source_target_pairs={{0,16},{4,20},{8,24},{12,28},{16,0},{20,4},{24,8},{28,12},{1,17},{... | collective-permute-start | bytes 110600 | tf_op jit(solution)/shard_map/ppermute | solution.py:92
  16.7 1.6 %collective-permute-start.2 = (f32[4,64,128]{2,1,0:T(8,128)S(1)}, f32[4,64,128]{2,1,0:T(8,128)S(1)}, u32[]{:S(2)}, u32[]{:S(2)}) collective-permute-start(f32[4,64,128]{2,1,0:T(8,128)S(1)} %pad_maximum_fusion.2), channel_id=1, source_target_pairs={{0,4},{4,0},{8,12},{12,8},{16,20},{20,16},{24,28},{28,24},{1,5},{5... | collective-permute-start | bytes 393224 | tf_op jit(solution)/shard_map/ppermute | solution.py:92
  18.3 0.7 collective-permute-done.10
  19.3 2.5 %collective-permute-done.2 = f32[4,64,128]{2,1,0:T(8,128)S(1)} collective-permute-done((f32[4,64,128]{2,1,0:T(8,128)S(1)}, f32[4,64,128]{2,1,0:T(8,128)S(1)}, u32[]{:S(2)}, u32[]{:S(2)}) %collective-permute-start.2) | collective-permute-done | bytes 131104 | tf_op jit(solution)/shard_map/ppermute | solution.py:92
  21.9 1.6 %collective-permute-done.11 = f32[2,72,128]{2,1,0:T(8,128)S(1)} collective-permute-done((f32[2,72,128]{2,1,0:T(8,128)S(1)}, f32[2,72,128]{2,1,0:T(8,128)S(1)}, u32[]{:S(2)}, u32[]{:S(2)}) %collective-permute-start.11) | collective-permute-done | bytes 73760 | tf_op jit(solution)/shard_map/ppermute | solution.py:92
  23.4 1.8 %collective-permute-start.12 = (f32[4,72,128]{2,1,0:T(8,128)S(1)}, f32[4,72,128]{2,1,0:T(8,128)S(1)}, u32[]{:S(2)}, u32[]{:S(2)}) collective-permute-start(f32[4,72,128]{2,1,0:T(8,128)S(1)} %pad_maximum_fusion.1.refs_8_.refs_12_), channel_id=1, source_target_pairs={{0,4},{4,0},{8,12},{12,8},{16,20},{20,16},{24,28},{28,24},{1,5},{5... | collective-permute-start | bytes 442376 | tf_op jit(solution)/shard_map/ppermute | solution.py:92
  25.2 3.4 %collective-permute-done.12.refs_9_.refs_14_ = f32[4,72,128]{2,1,0:T(8,128)S(1)} collective-permute-done((f32[4,72,128]{2,1,0:T(8,128)S(1)}, f32[4,72,128]{2,1,0:T(8,128)S(1)}, u32[]{:S(2)}, u32[]{:S(2)}) %collective-permute-start.12) | collective-permute-done | bytes 147488 | tf_op jit(solution)/shard_map/ppermute | solution.py:92
  28.7 6.3 %scores.1 = (f32[2048,1024]{1,0:T(8,128)S(1)}, f32[2048,1024]{1,0:T(8,128)S(1)}, f32[2048,1024]{1,0:T(8,128)S(1)}, f32[2048,1024]{1,0:T(8,128)S(1)}, f32[8,128]{1,0:T(8,128)S(1)}) custom-call(s32[2]{0:T(128)S(1)} %pad_add_fusion.place_ref.refs_17_.refs_15_, f32[8,64,128]{2,1,0:T(8,128)S(1)} %pad_maximum_fusion.mine_ref, ...), custom_call_target="tpu_custom_call" | custom-call | tf_op jit(solution)/shard_map/scores/pallas_call | solution.py:413
  35.5 1.7 %collective-permute-start.5 = (f32[8,128]{1,0:T(8,128)S(1)}, f32[8,128]{1,0:T(8,128)S(1)}, u32[]{:S(2)}, u32[]{:S(2)}) collective-permute-start(f32[8,128]{1,0:T(8,128)S(1)} %get-tuple-element.24.refs_4_), channel_id=1, source_target_pairs={{0,2},{1,3},{2,0},{3,1},{4,6},{5,7},{6,4},{7,5},{8,10},{9,11},{10,... | collective-permute-start | bytes 12296 | tf_op jit(solution)/shard_map/ppermute | solution.py:92
  37.3 1.9 %collective-permute-done.5.refs_6_ = f32[8,128]{1,0:T(8,128)S(1)} collective-permute-done((f32[8,128]{1,0:T(8,128)S(1)}, f32[8,128]{1,0:T(8,128)S(1)}, u32[]{:S(2)}, u32[]{:S(2)}) %collective-permute-start.5) | collective-permute-done | bytes 4128 | tf_op jit(solution)/shard_map/ppermute | solution.py:92
  39.1 1.2 %collective-permute-done.6.refs_7_ = f32[8,128]{1,0:T(8,128)S(1)} collective-permute-done((f32[8,128]{1,0:T(8,128)S(1)}, f32[8,128]{1,0:T(8,128)S(1)}, u32[]{:S(2)}, u32[]{:S(2)}) %collective-permute-start.6) | collective-permute-done | bytes 4128 | tf_op jit(solution)/shard_map/ppermute | solution.py:92
  40.3 10.7 %sweep_first.1 = (f32[2048,1024]{1,0:T(8,128)S(1)}, f32[2048,1024]{1,0:T(8,128)S(1)}, f32[2048,1024]{1,0:T(8,128)S(1)}, f32[2048,1024]{1,0:T(8,128)S(1)}, f32[8,128]{1,0:T(8,128)S(1)}) custom-call(f32[2048,1024]{1,0:T(8,128)S(1)} %get-tuple-element.20.refs_0_, ...), custom_call_target="tpu_custom_call", output_to_operand_aliasing={{0}: (0, {}), {1}: (1, {}), {2}: (2, {}), {3}: (3, {})} | custom-call | tf_op jit(solution)/shard_map/sweep_first/pallas_call | solution.py:427
  51.7 1.2 %collective-permute-start.9 = (f32[8,128]{1,0:T(8,128)S(1)}, f32[8,128]{1,0:T(8,128)S(1)}, u32[]{:S(2)}, u32[]{:S(2)}) collective-permute-start(f32[8,128]{1,0:T(8,128)S(1)} %get-tuple-element.29.refs_4_), channel_id=1, source_target_pairs={{0,3},{1,2},{2,1},{3,0},{4,7},{5,6},{6,5},{7,4},{8,11},{9,10},{10,... | collective-permute-start | bytes 12296 | tf_op jit(solution)/shard_map/ppermute | solution.py:92
  52.9 1.9 %collective-permute-done.8.refs_6_ = f32[8,128]{1,0:T(8,128)S(1)} collective-permute-done((f32[8,128]{1,0:T(8,128)S(1)}, f32[8,128]{1,0:T(8,128)S(1)}, u32[]{:S(2)}, u32[]{:S(2)}) %collective-permute-start.8) | collective-permute-done | bytes 4128 | tf_op jit(solution)/shard_map/ppermute | solution.py:92
  54.8 7.2 %sweep.1.refs_4_.refs_8_ = f32[24,128]{1,0:T(8,128)S(1)} custom-call(f32[2048,1024]{1,0:T(8,128)S(1)} %get-tuple-element.25.refs_0_, f32[2048,1024]{1,0:T(8,128)S(1)} %get-tuple-element.26.refs_1_, f32[2048,1024]{1,0:T(8,128)S(1)} %get-tuple-element.27.refs_2_, f32[2048,1024]{1,0:T(8,128)S(1)} %get-tuple-element.28.refs_3_, ...), custom_call_target="tpu_custom_call" | custom-call | tf_op jit(solution)/shard_map/sweep/pallas_call | solution.py:427
  62.2 1.4 %collective-permute-start.14 = (f32[24,128]{1,0:T(8,128)S(1)}, f32[24,128]{1,0:T(8,128)S(1)}, u32[]{:S(2)}, u32[]{:S(2)}) collective-permute-start(f32[24,128]{1,0:T(8,128)S(1)} %sweep.1.refs_4_.refs_8_), channel_id=1, source_target_pairs={{0,2},{1,3},{2,0},{3,1},{4,6},{5,7},{6,4},{7,5},{8,10},{9,11},{10,... | collective-permute-start | bytes 36872 | tf_op jit(solution)/shard_map/ppermute | solution.py:92
  63.9 1.9 %collective-permute-done.14.refs_6_.refs_10_ = f32[24,128]{1,0:T(8,128)S(1)} collective-permute-done((f32[24,128]{1,0:T(8,128)S(1)}, f32[24,128]{1,0:T(8,128)S(1)}, u32[]{:S(2)}, u32[]{:S(2)}) %collective-permute-start.14) | collective-permute-done | bytes 12320 | tf_op jit(solution)/shard_map/ppermute | solution.py:92
  65.9 0.9 collective-permute-done.15.refs_7_.refs_11_
  66.7 9.1 %sweep_last.1 = (f32[2048,1024]{1,0:T(8,128)S(1)}, f32[2048,1024]{1,0:T(8,128)S(1)}, f32[2048,1024]{1,0:T(8,128)S(1)}, f32[2048,1024]{1,0:T(8,128)S(1)}, f32[8,128]{1,0:T(8,128)S(1)}) custom-call(f32[2048,1024]{1,0:T(8,128)S(1)} %get-tuple-element.25.refs_0_, ...), custom_call_target="tpu_custom_call", output_to_operand_aliasing={{0}: (0, {}), {1}: (1, {}), {2}: (2, {}), {3}: (3, {})} | custom-call | tf_op jit(solution)/shard_map/sweep_last/pallas_call | solution.py:427
  76.0 0.7 collective-permute-start.17
  76.7 1.0 %collective-permute-start.18 = (f32[8,128]{1,0:T(8,128)S(1)}, f32[8,128]{1,0:T(8,128)S(1)}, u32[]{:S(2)}, u32[]{:S(2)}) collective-permute-start(f32[8,128]{1,0:T(8,128)S(1)} %get-tuple-element.35.refs_4_), channel_id=1, source_target_pairs={{0,3},{1,2},{2,1},{3,0},{4,7},{5,6},{6,5},{7,4},{8,11},{9,10},{10,... | collective-permute-start | bytes 12296 | tf_op jit(solution)/shard_map/ppermute | solution.py:92
  77.8 1.9 %collective-permute-done.17.refs_6_ = f32[8,128]{1,0:T(8,128)S(1)} collective-permute-done((f32[8,128]{1,0:T(8,128)S(1)}, f32[8,128]{1,0:T(8,128)S(1)}, u32[]{:S(2)}, u32[]{:S(2)}) %collective-permute-start.17) | collective-permute-done | bytes 4128 | tf_op jit(solution)/shard_map/ppermute | solution.py:92
  79.8 2.5 %own_grad.1 = f32[128,128]{1,0:T(8,128)S(1)} custom-call(f32[2048,1024]{1,0:T(8,128)S(1)} %get-tuple-element.31.refs_0_, f32[2048,1024]{1,0:T(8,128)S(1)} %get-tuple-element.32.refs_1_, f32[2048,1024]{1,0:T(8,128)S(1)} %get-tuple-element.33.refs_2_, f32[2048,1024]{1,0:T(8,128)S(1)} %get-tuple-element.34.refs_3_, f32[8,128]{1,0:T(8,128)S(1)} %get-tuple-element.35.refs_4_, ...), custom_call_target="tpu_custom_call" | custom-call | tf_op jit(solution)/shard_map/own_grad/pallas_call | solution.py:452
  82.5 1.3 %collective-permute-start.22 = (f32[128,128]{1,0:T(8,128)S(1)}, f32[128,128]{1,0:T(8,128)S(1)}, u32[]{:S(2)}, u32[]{:S(2)}) collective-permute-start(f32[128,128]{1,0:T(8,128)S(1)} %own_grad.1), channel_id=1, source_target_pairs={{0,2},{1,3},{2,0},{3,1},{4,6},{5,7},{6,4},{7,5},{8,10},{9,11},{10,... | collective-permute-start | bytes 196616 | tf_op jit(solution)/shard_map/ppermute | solution.py:92
  84.2 14.5 %proto_grad.1 = f32[16,8192]{1,0:T(8,128)} custom-call(f32[2048,1024]{1,0:T(8,128)S(1)} %get-tuple-element.31.refs_0_, f32[2048,1024]{1,0:T(8,128)S(1)} %get-tuple-element.32.refs_1_, f32[2048,1024]{1,0:T(8,128)S(1)} %get-tuple-element.33.refs_2_, f32[2048,1024]{1,0:T(8,128)S(1)} %get-tuple-element.34.refs_3_, f32[8,128]{1,0:T(8,128)S(1)} %get-tuple-element.35.refs_4_, ...), custom_call_target="tpu_custom_call" | custom-call | tf_op jit(solution)/shard_map/proto_grad/pallas_call | solution.py:452
  (35 shorter events, 3.8 us)
Async XLA Ops:
  1.4 6.3 %collective-permute-start = (f32[1,64,128]{2,1,0:T(8,128)S(1)}, f32[1,64,128]{2,1,0:T(8,128)S(1)}, u32[]{:S(2)}, u32[]{:S(2)}) collective-permute-start(f32[1,64,128]{2,1,0:T(8,128)S(1)} %bitcast_convert_fusion), channel_id=1, source_target_pairs={{0,16},{4,20},{8,24},{12,28},{16,0},{20,4},{24,8},{28,12},{1,17},{... | collective-permute-start | bytes 98312 | tf_op jit(solution)/shard_map/ppermute | solution.py:92
  7.7 9.0 %collective-permute-start.1 = (f32[2,64,128]{2,1,0:T(8,128)S(1)}, f32[2,64,128]{2,1,0:T(8,128)S(1)}, u32[]{:S(2)}, u32[]{:S(2)}) collective-permute-start(f32[2,64,128]{2,1,0:T(8,128)S(1)} %pad_maximum_fusion.4), channel_id=1, source_target_pairs={{0,8},{4,12},{8,0},{12,4},{16,24},{20,28},{24,16},{28,20},{1,9},{5... | collective-permute-start | bytes 196616 | tf_op jit(solution)/shard_map/ppermute | solution.py:92
  9.3 1.6 %copy-start = (bf16[128,8192]{1,0:T(8,128)(2,1)S(1)}, bf16[128,8192]{1,0:T(8,128)(2,1)}, u32[]{:S(2)}) copy-start(bf16[128,8192]{1,0:T(8,128)(2,1)} %w_ref.1) | copy-start | bytes 6291460
  10.9 0.8 copy-start.1
  13.8 5.2 %collective-permute-start.10 = (f32[1,72,128]{2,1,0:T(8,128)S(1)}, f32[1,72,128]{2,1,0:T(8,128)S(1)}, u32[]{:S(2)}, u32[]{:S(2)}) collective-permute-start(f32[1,72,128]{2,1,0:T(8,128)S(1)} %bitcast.6), channel_id=1, source_target_pairs={{0,16},{4,20},{8,24},{12,28},{16,0},{20,4},{24,8},{28,12},{1,17},{... | collective-permute-start | bytes 110600 | tf_op jit(solution)/shard_map/ppermute | solution.py:92
  16.7 5.0 %collective-permute-start.2 = (f32[4,64,128]{2,1,0:T(8,128)S(1)}, f32[4,64,128]{2,1,0:T(8,128)S(1)}, u32[]{:S(2)}, u32[]{:S(2)}) collective-permute-start(f32[4,64,128]{2,1,0:T(8,128)S(1)} %pad_maximum_fusion.2), channel_id=1, source_target_pairs={{0,4},{4,0},{8,12},{12,8},{16,20},{20,16},{24,28},{28,24},{1,5},{5... | collective-permute-start | bytes 393224 | tf_op jit(solution)/shard_map/ppermute | solution.py:92
  19.1 4.4 %collective-permute-start.11 = (f32[2,72,128]{2,1,0:T(8,128)S(1)}, f32[2,72,128]{2,1,0:T(8,128)S(1)}, u32[]{:S(2)}, u32[]{:S(2)}) collective-permute-start(f32[2,72,128]{2,1,0:T(8,128)S(1)} %pad_maximum_fusion.3), channel_id=1, source_target_pairs={{0,8},{4,12},{8,0},{12,4},{16,24},{20,28},{24,16},{28,20},{1,9},{5... | collective-permute-start | bytes 221192 | tf_op jit(solution)/shard_map/ppermute | solution.py:92
  21.8 6.9 %collective-permute-start.3 = (f32[8,64,128]{2,1,0:T(8,128)S(1)}, f32[8,64,128]{2,1,0:T(8,128)S(1)}, u32[]{:S(2)}, u32[]{:S(2)}) collective-permute-start(f32[8,64,128]{2,1,0:T(8,128)S(1)} %pad_maximum_fusion.mine_ref), channel_id=1, source_target_pairs={{0,1},{1,0},{2,3},{3,2},{4,5},{5,4},{6,7},{7,6},{8,9},{9,8},{10,11... | collective-permute-start | bytes 786440 | tf_op jit(solution)/shard_map/ppermute | solution.py:92
  23.4 5.2 %collective-permute-start.12 = (f32[4,72,128]{2,1,0:T(8,128)S(1)}, f32[4,72,128]{2,1,0:T(8,128)S(1)}, u32[]{:S(2)}, u32[]{:S(2)}) collective-permute-start(f32[4,72,128]{2,1,0:T(8,128)S(1)} %pad_maximum_fusion.1.refs_8_.refs_12_), channel_id=1, source_target_pairs={{0,4},{4,0},{8,12},{12,8},{16,20},{20,16},{24,28},{28,24},{1,5},{5... | collective-permute-start | bytes 442376 | tf_op jit(solution)/shard_map/ppermute | solution.py:92
  25.2 52.6 %collective-permute-start.19 = (f32[4,72,128]{2,1,0:T(8,128)S(1)}, f32[4,72,128]{2,1,0:T(8,128)S(1)}, u32[]{:S(2)}, u32[]{:S(2)}) collective-permute-start(f32[4,72,128]{2,1,0:T(8,128)S(1)} %pad_maximum_fusion.1.refs_8_.refs_12_), channel_id=1, source_target_pairs={{0,1},{1,0},{2,3},{3,2},{4,5},{5,4},{6,7},{7,6},{8,9},{9,8},{10,11... | collective-permute-start | bytes 442376 | tf_op jit(solution)/shard_map/ppermute | solution.py:92
  28.7 55.5 %collective-permute-start.20 = (f32[4,72,128]{2,1,0:T(8,128)S(1)}, f32[4,72,128]{2,1,0:T(8,128)S(1)}, u32[]{:S(2)}, u32[]{:S(2)}) collective-permute-start(f32[4,72,128]{2,1,0:T(8,128)S(1)} %collective-permute-done.12.refs_9_.refs_14_), channel_id=1, source_target_pairs={{0,1},{1,0},{2,3},{3,2},{4,5},{5,4},{6,7},{7,6},{8,9},{9,8},{10,11... | collective-permute-start | bytes 442376 | tf_op jit(solution)/shard_map/ppermute | solution.py:92
  35.0 2.3 %collective-permute-start.4 = (f32[8,128]{1,0:T(8,128)S(1)}, f32[8,128]{1,0:T(8,128)S(1)}, u32[]{:S(2)}, u32[]{:S(2)}) collective-permute-start(f32[8,128]{1,0:T(8,128)S(1)} %get-tuple-element.24.refs_4_), channel_id=1, source_target_pairs={{0,1},{1,0},{2,3},{3,2},{4,5},{5,4},{6,7},{7,6},{8,9},{9,8},{10,11... | collective-permute-start | bytes 12296 | tf_op jit(solution)/shard_map/ppermute | solution.py:92
  35.5 3.6 %collective-permute-start.5 = (f32[8,128]{1,0:T(8,128)S(1)}, f32[8,128]{1,0:T(8,128)S(1)}, u32[]{:S(2)}, u32[]{:S(2)}) collective-permute-start(f32[8,128]{1,0:T(8,128)S(1)} %get-tuple-element.24.refs_4_), channel_id=1, source_target_pairs={{0,2},{1,3},{2,0},{3,1},{4,6},{5,7},{6,4},{7,5},{8,10},{9,11},{10,... | collective-permute-start | bytes 12296 | tf_op jit(solution)/shard_map/ppermute | solution.py:92
  37.3 3.1 %collective-permute-start.6 = (f32[8,128]{1,0:T(8,128)S(1)}, f32[8,128]{1,0:T(8,128)S(1)}, u32[]{:S(2)}, u32[]{:S(2)}) collective-permute-start(f32[8,128]{1,0:T(8,128)S(1)} %get-tuple-element.24.refs_4_), channel_id=1, source_target_pairs={{0,3},{1,2},{2,1},{3,0},{4,7},{5,6},{6,5},{7,4},{8,11},{9,10},{10,... | collective-permute-start | bytes 12296 | tf_op jit(solution)/shard_map/ppermute | solution.py:92
  51.0 1.9 %collective-permute-start.7 = (f32[8,128]{1,0:T(8,128)S(1)}, f32[8,128]{1,0:T(8,128)S(1)}, u32[]{:S(2)}, u32[]{:S(2)}) collective-permute-start(f32[8,128]{1,0:T(8,128)S(1)} %get-tuple-element.29.refs_4_), channel_id=1, source_target_pairs={{0,1},{1,0},{2,3},{3,2},{4,5},{5,4},{6,7},{7,6},{8,9},{9,8},{10,11... | collective-permute-start | bytes 12296 | tf_op jit(solution)/shard_map/ppermute | solution.py:92
  51.1 3.6 %collective-permute-start.8 = (f32[8,128]{1,0:T(8,128)S(1)}, f32[8,128]{1,0:T(8,128)S(1)}, u32[]{:S(2)}, u32[]{:S(2)}) collective-permute-start(f32[8,128]{1,0:T(8,128)S(1)} %get-tuple-element.29.refs_4_), channel_id=1, source_target_pairs={{0,2},{1,3},{2,0},{3,1},{4,6},{5,7},{6,4},{7,5},{8,10},{9,11},{10,... | collective-permute-start | bytes 12296 | tf_op jit(solution)/shard_map/ppermute | solution.py:92
  51.7 3.1 %collective-permute-start.9 = (f32[8,128]{1,0:T(8,128)S(1)}, f32[8,128]{1,0:T(8,128)S(1)}, u32[]{:S(2)}, u32[]{:S(2)}) collective-permute-start(f32[8,128]{1,0:T(8,128)S(1)} %get-tuple-element.29.refs_4_), channel_id=1, source_target_pairs={{0,3},{1,2},{2,1},{3,0},{4,7},{5,6},{6,5},{7,4},{8,11},{9,10},{10,... | collective-permute-start | bytes 12296 | tf_op jit(solution)/shard_map/ppermute | solution.py:92
  62.0 1.9 %collective-permute-start.13 = (f32[24,128]{1,0:T(8,128)S(1)}, f32[24,128]{1,0:T(8,128)S(1)}, u32[]{:S(2)}, u32[]{:S(2)}) collective-permute-start(f32[24,128]{1,0:T(8,128)S(1)} %sweep.1.refs_4_.refs_8_), channel_id=1, source_target_pairs={{0,1},{1,0},{2,3},{3,2},{4,5},{5,4},{6,7},{7,6},{8,9},{9,8},{10,11... | collective-permute-start | bytes 36872 | tf_op jit(solution)/shard_map/ppermute | solution.py:92
  62.2 3.7 %collective-permute-start.14 = (f32[24,128]{1,0:T(8,128)S(1)}, f32[24,128]{1,0:T(8,128)S(1)}, u32[]{:S(2)}, u32[]{:S(2)}) collective-permute-start(f32[24,128]{1,0:T(8,128)S(1)} %sweep.1.refs_4_.refs_8_), channel_id=1, source_target_pairs={{0,2},{1,3},{2,0},{3,1},{4,6},{5,7},{6,4},{7,5},{8,10},{9,11},{10,... | collective-permute-start | bytes 36872 | tf_op jit(solution)/shard_map/ppermute | solution.py:92
  63.6 3.1 %collective-permute-start.15 = (f32[24,128]{1,0:T(8,128)S(1)}, f32[24,128]{1,0:T(8,128)S(1)}, u32[]{:S(2)}, u32[]{:S(2)}) collective-permute-start(f32[24,128]{1,0:T(8,128)S(1)} %sweep.1.refs_4_.refs_8_), channel_id=1, source_target_pairs={{0,3},{1,2},{2,1},{3,0},{4,7},{5,6},{6,5},{7,4},{8,11},{9,10},{10,... | collective-permute-start | bytes 36872 | tf_op jit(solution)/shard_map/ppermute | solution.py:92
  75.8 1.9 %collective-permute-start.16 = (f32[8,128]{1,0:T(8,128)S(1)}, f32[8,128]{1,0:T(8,128)S(1)}, u32[]{:S(2)}, u32[]{:S(2)}) collective-permute-start(f32[8,128]{1,0:T(8,128)S(1)} %get-tuple-element.35.refs_4_), channel_id=1, source_target_pairs={{0,1},{1,0},{2,3},{3,2},{4,5},{5,4},{6,7},{7,6},{8,9},{9,8},{10,11... | collective-permute-start | bytes 12296 | tf_op jit(solution)/shard_map/ppermute | solution.py:92
  76.0 3.6 %collective-permute-start.17 = (f32[8,128]{1,0:T(8,128)S(1)}, f32[8,128]{1,0:T(8,128)S(1)}, u32[]{:S(2)}, u32[]{:S(2)}) collective-permute-start(f32[8,128]{1,0:T(8,128)S(1)} %get-tuple-element.35.refs_4_), channel_id=1, source_target_pairs={{0,2},{1,3},{2,0},{3,1},{4,6},{5,7},{6,4},{7,5},{8,10},{9,11},{10,... | collective-permute-start | bytes 12296 | tf_op jit(solution)/shard_map/ppermute | solution.py:92
  76.7 3.0 %collective-permute-start.18 = (f32[8,128]{1,0:T(8,128)S(1)}, f32[8,128]{1,0:T(8,128)S(1)}, u32[]{:S(2)}, u32[]{:S(2)}) collective-permute-start(f32[8,128]{1,0:T(8,128)S(1)} %get-tuple-element.35.refs_4_), channel_id=1, source_target_pairs={{0,3},{1,2},{2,1},{3,0},{4,7},{5,6},{6,5},{7,4},{8,11},{9,10},{10,... | collective-permute-start | bytes 12296 | tf_op jit(solution)/shard_map/ppermute | solution.py:92
  82.3 16.4 %collective-permute-start.21 = (f32[128,128]{1,0:T(8,128)S(1)}, f32[128,128]{1,0:T(8,128)S(1)}, u32[]{:S(2)}, u32[]{:S(2)}) collective-permute-start(f32[128,128]{1,0:T(8,128)S(1)} %own_grad.1), channel_id=1, source_target_pairs={{0,1},{1,0},{2,3},{3,2},{4,5},{5,4},{6,7},{7,6},{8,9},{9,8},{10,11... | collective-permute-start | bytes 196616 | tf_op jit(solution)/shard_map/ppermute | solution.py:92
  82.5 16.2 %collective-permute-start.22 = (f32[128,128]{1,0:T(8,128)S(1)}, f32[128,128]{1,0:T(8,128)S(1)}, u32[]{:S(2)}, u32[]{:S(2)}) collective-permute-start(f32[128,128]{1,0:T(8,128)S(1)} %own_grad.1), channel_id=1, source_target_pairs={{0,2},{1,3},{2,0},{3,1},{4,6},{5,7},{6,4},{7,5},{8,10},{9,11},{10,... | collective-permute-start | bytes 196616 | tf_op jit(solution)/shard_map/ppermute | solution.py:92
  83.8 14.9 %collective-permute-start.23 = (f32[128,128]{1,0:T(8,128)S(1)}, f32[128,128]{1,0:T(8,128)S(1)}, u32[]{:S(2)}, u32[]{:S(2)}) collective-permute-start(f32[128,128]{1,0:T(8,128)S(1)} %own_grad.1), channel_id=1, source_target_pairs={{0,3},{1,2},{2,1},{3,0},{4,7},{5,6},{6,5},{7,4},{8,11},{9,10},{10,... | collective-permute-start | bytes 196616 | tf_op jit(solution)/shard_map/ppermute | solution.py:92

commit v5 on v4

--- a/solution.py
+++ b/solution.py
@@ -6,6 +6,7 @@
 from jax.experimental import pallas as pl
 from jax.experimental.pallas import tpu as pltpu
 from jax.sharding import PartitionSpec as P
+
 
 ITERS = 3
 
@@ -57,7 +58,7 @@
     )
     kernel = jnp.exp(teacher_scores - teacher_peak[:, None])
     row_scale = jnp.ones((teacher_feat.shape[0],), jnp.float32)
-    for sweep in range(ITERS):
+    for _ in range(ITERS):
         col_part = jnp.sum(kernel * row_scale[:, None], axis=0)
         col_scale = 1.0 / lax.psum(col_part, "dp")
         row_part = jnp.sum(kernel * col_scale[None, :], axis=1)
@@ -114,7 +115,7 @@
 def own_body(place_ref, s_ref, w_ref, out_ref, wt_ref, scores_ref):
     rows = s_ref.shape[0]
     half = rows // 2
-    count, width, unused = scores_ref.shape
+    count, width, _ = scores_ref.shape
     s = s_ref[...]
     top = None
     for j in range(count):
@@ -385,7 +386,8 @@
 
     def spread(x, bits):
         for bit in bits:
-            x = jnp.concatenate([x, swap(x, "dp", bit)], axis=0)
+            y = swap(x, "dp", bit)
+            x = jnp.concatenate([x, y], axis=0)
         return x
 
     bits = [1 << k for k in range(n_dp.bit_length() - 1)][::-1]
@@ -394,7 +396,7 @@
     other = swap(mine, "proto", 1)
 
     chunk = 1024
-    student_part, weight_t = pl.pallas_call(
+    own_stats = pl.pallas_call(
         own_body,
         out_shape=(
             jax.ShapeDtypeStruct((half + STAT_ROWS, depth), f32),
@@ -405,7 +407,8 @@
         scratch_shapes=[pltpu.VMEM((cols // chunk, chunk, own), f32)],
         compiler_params=grant(16),
         name="own_stats",
-    )(place, student_feat, proto_weight)
+    )
+    student_part, weight_t = own_stats(place, student_feat, proto_weight)
     near = spread(student_part[None], bits[:-1])
 
     k_shape = pltpu.VMEM((per, rows), f32)
@@ -436,19 +439,24 @@
         )(*kernel, *ins, *extra)
         return (result[:PARTS] if kept else kernel), result[-1]
 
+    local_peak, near = lax.optimization_barrier((local_peak, near))
     ins = everyone(local_peak)
     far = swap(near, "dp", bits[-1])
     near_other = swap(near, "proto", 1)
-    far_other = swap(far, "proto", 1)
     stats = None
     for it in range(ITERS):
         extra = (near, far) if it == ITERS - 2 else ()
         kernel, row_part = sweep(kernel, ins, extra, it)
+        if it == 0:
+            row_part, far = lax.optimization_barrier((row_part, far))
+            far_other = swap(far, "proto", 1)
+        elif it == 1:
+            row_part, far_other = lax.optimization_barrier((row_part, far_other))
         ins = everyone(row_part)
         if extra:
             stats = ins
 
-    def final(body, operands, shape, scratch, mib, name):
+    def final(body, operands, shape, scratch):
         return pl.pallas_call(
             lambda *refs: body(len(ins), *refs),
             out_shape=jax.ShapeDtypeStruct(shape, f32),
@@ -456,7 +464,6 @@
             out_specs=vmem(),
             scratch_shapes=scratch,
             compiler_params=grant(16),
-            name=name,
         )(*kernel, *ins, *stats, *operands, place)
 
     pair = [pltpu.VMEM((1024, LANES), f32), pltpu.VMEM((1024, LANES), bf16)]
@@ -465,8 +472,6 @@
         (near, near_other, weight_t),
         (own, depth),
         [pltpu.VMEM((own, depth), bf16)] + pair * 2,
-        4,
-        "own_grad",
     )
     parts = everyone(own_part)
     pair = [pltpu.VMEM((512, rows), f32), pltpu.VMEM((512, rows), bf16)]
@@ -475,8 +480,6 @@
         (near, near_other, far, far_other, weight_t),
         (depth // n_dp, cols),
         [pltpu.VMEM((rows, depth), bf16)] + pair * 2,
-        10,
-        "proto_grad",
     )
     feature_grad = fold(parts, jnp.add)
     return (proto_grad, feature_grad)

time: 99.6 us -> 99 us (level)
  transfers between devices with their start and end apart: 24 -> 24, of which waited for: 12 -> 12; matrix products, arithmetic and copies ran while one was open for 0% -> 0% of each run, Pallas kernels for 53% -> 44%
where the time goes in v5:
time: 99 us; the launch traced here: 98.8 us
  Pallas kernels  52.4 us (53%)
  starting transfers between devices  21.7 us (22%)
  waiting for transfers between devices  20 us (20%)
  local copies, waits for them, and re-layouts  2.35 us (2%)
  other arithmetic  1.5 us (2%)
    pallas_call x3, Pallas kernels, sweep(): pl.pallas_call(lambda *refs: sweep_body(first, last, len(ins), len(extra)...  27 us
    ppermute x24, starting transfers between devices, swap(): lax.ppermute(x, axis, [(i, i ^ bit) for i in range(lax.axis_size(axis))])  21.7 us
    ppermute x24, waiting for transfers between devices, swap(): lax.ppermute(x, axis, [(i, i ^ bit) for i in range(lax.axis_size(axis))])  20 us
    pallas_call x2, Pallas kernels, final(): pl.pallas_call(lambda *refs: body(len(ins), *refs), out_shape=jax.ShapeDt...  17 us
    pallas_call x1, Pallas kernels, all_crops(): pl.pallas_call(scores_body, out_shape=(k_shape,) * PARTS + (flat,), in_sp...  6.33 us
    unnamed x4, local copies, waits for them, and re-layouts  2.35 us
    pallas_call x1, Pallas kernels, all_crops(): student_part, weight_t = own_stats(place, student_feat, proto_weight)  2.16 us
  transfers between devices with their start and end apart: 24, of which 12 were waited for; matrix products, arithmetic and copies ran while one was open for 0% of the time, Pallas kernels for 44%

profile of v5, /device:TPU:0, one launch (start us, length us, event | category | flops | bytes accessed | tf_op | source)
XLA Modules:
  0.0 98.8 jit_solution(5344307004598558009)
XLA Ops:
  0.6 0.7 bitcast_convert_fusion
  1.4 4.1 %collective-permute-start = (f32[1,64,128]{2,1,0:T(8,128)S(1)}, f32[1,64,128]{2,1,0:T(8,128)S(1)}, u32[]{:S(2)}, u32[]{:S(2)}) collective-permute-start(f32[1,64,128]{2,1,0:T(8,128)S(1)} %bitcast_convert_fusion), channel_id=1, source_target_pairs={{0,16},{4,20},{8,24},{12,28},{16,0},{20,4},{24,8},{28,12},{1,17},{... | collective-permute-start | bytes 98312 | tf_op jit(solution)/shard_map/ppermute | solution.py:93
  5.4 2.2 %collective-permute-done = f32[1,64,128]{2,1,0:T(8,128)S(1)} collective-permute-done((f32[1,64,128]{2,1,0:T(8,128)S(1)}, f32[1,64,128]{2,1,0:T(8,128)S(1)}, u32[]{:S(2)}, u32[]{:S(2)}) %collective-permute-start) | collective-permute-done | bytes 32800 | tf_op jit(solution)/shard_map/ppermute | solution.py:93
  7.7 1.6 %collective-permute-start.1 = (f32[2,64,128]{2,1,0:T(8,128)S(1)}, f32[2,64,128]{2,1,0:T(8,128)S(1)}, u32[]{:S(2)}, u32[]{:S(2)}) collective-permute-start(f32[2,64,128]{2,1,0:T(8,128)S(1)} %pad_maximum_fusion.4), channel_id=1, source_target_pairs={{0,8},{4,12},{8,0},{12,4},{16,24},{20,28},{24,16},{28,20},{1,9},{5... | collective-permute-start | bytes 196616 | tf_op jit(solution)/shard_map/ppermute | solution.py:93
  9.2 2.7 %collective-permute-done.1 = f32[2,64,128]{2,1,0:T(8,128)S(1)} collective-permute-done((f32[2,64,128]{2,1,0:T(8,128)S(1)}, f32[2,64,128]{2,1,0:T(8,128)S(1)}, u32[]{:S(2)}, u32[]{:S(2)}) %collective-permute-start.1) | collective-permute-done | bytes 65568 | tf_op jit(solution)/shard_map/ppermute | solution.py:93
  12.0 1.8 %collective-permute-start.2 = (f32[4,64,128]{2,1,0:T(8,128)S(1)}, f32[4,64,128]{2,1,0:T(8,128)S(1)}, u32[]{:S(2)}, u32[]{:S(2)}) collective-permute-start(f32[4,64,128]{2,1,0:T(8,128)S(1)} %pad_maximum_fusion.2), channel_id=1, source_target_pairs={{0,4},{4,0},{8,12},{12,8},{16,20},{20,16},{24,28},{28,24},{1,5},{5... | collective-permute-start | bytes 393224 | tf_op jit(solution)/shard_map/ppermute | solution.py:93
  13.8 1.6 %copy-done = bf16[128,8192]{1,0:T(8,128)(2,1)S(1)} copy-done((bf16[128,8192]{1,0:T(8,128)(2,1)S(1)}, bf16[128,8192]{1,0:T(8,128)(2,1)}, u32[]{:S(2)}) %copy-start) | copy-done | bytes 2097176
  15.4 0.8 copy-done.1
  16.2 2.2 %own_stats.1 = (f32[72,128]{1,0:T(8,128)S(1)}, bf16[8192,128]{1,0:T(8,128)(2,1)S(1)}) custom-call(s32[2]{0:T(128)S(1)} %pad_add_fusion.place_ref.refs_17_.refs_15_, bf16[128,128]{1,0:T(8,128)(2,1)S(1)} %copy-done.1, bf16[128,8192]{1,0:T(8,128)(2,1)S(1)} %copy-done), custom_call_target="tpu_custom_call" | custom-call | tf_op jit(solution)/shard_map/own_stats/pallas_call | solution.py:411
  18.4 2.4 %collective-permute-start.4 = (f32[1,72,128]{2,1,0:T(8,128)S(1)}, f32[1,72,128]{2,1,0:T(8,128)S(1)}, u32[]{:S(2)}, u32[]{:S(2)}) collective-permute-start(f32[1,72,128]{2,1,0:T(8,128)S(1)} %bitcast.6), channel_id=1, source_target_pairs={{0,16},{4,20},{8,24},{12,28},{16,0},{20,4},{24,8},{28,12},{1,17},{... | collective-permute-start | bytes 110600 | tf_op jit(solution)/shard_map/ppermute | solution.py:93
  20.9 2.4 %collective-permute-done.4 = f32[1,72,128]{2,1,0:T(8,128)S(1)} collective-permute-done((f32[1,72,128]{2,1,0:T(8,128)S(1)}, f32[1,72,128]{2,1,0:T(8,128)S(1)}, u32[]{:S(2)}, u32[]{:S(2)}) %collective-permute-start.4) | collective-permute-done | bytes 36896 | tf_op jit(solution)/shard_map/ppermute | solution.py:93
  23.3 1.4 %collective-permute-start.5 = (f32[2,72,128]{2,1,0:T(8,128)S(1)}, f32[2,72,128]{2,1,0:T(8,128)S(1)}, u32[]{:S(2)}, u32[]{:S(2)}) collective-permute-start(f32[2,72,128]{2,1,0:T(8,128)S(1)} %pad_maximum_fusion.3), channel_id=1, source_target_pairs={{0,8},{4,12},{8,0},{12,4},{16,24},{20,28},{24,16},{28,20},{1,9},{5... | collective-permute-start | bytes 221192 | tf_op jit(solution)/shard_map/ppermute | solution.py:93
  24.6 3.0 %collective-permute-done.5 = f32[2,72,128]{2,1,0:T(8,128)S(1)} collective-permute-done((f32[2,72,128]{2,1,0:T(8,128)S(1)}, f32[2,72,128]{2,1,0:T(8,128)S(1)}, u32[]{:S(2)}, u32[]{:S(2)}) %collective-permute-start.5) | collective-permute-done | bytes 73760 | tf_op jit(solution)/shard_map/ppermute | solution.py:93
  27.7 6.3 %scores.1 = (f32[2048,1024]{1,0:T(8,128)S(1)}, f32[2048,1024]{1,0:T(8,128)S(1)}, f32[2048,1024]{1,0:T(8,128)S(1)}, f32[2048,1024]{1,0:T(8,128)S(1)}, f32[8,128]{1,0:T(8,128)S(1)}) custom-call(s32[2]{0:T(128)S(1)} %pad_add_fusion.place_ref.refs_17_.refs_15_, f32[8,64,128]{2,1,0:T(8,128)S(1)} %pad_maximum_fusion.mine_ref, ...), custom_call_target="tpu_custom_call" | custom-call | tf_op jit(solution)/shard_map/scores/pallas_call | solution.py:416
  34.4 1.7 %collective-permute-start.7 = (f32[8,128]{1,0:T(8,128)S(1)}, f32[8,128]{1,0:T(8,128)S(1)}, u32[]{:S(2)}, u32[]{:S(2)}) collective-permute-start(f32[8,128]{1,0:T(8,128)S(1)} %get-tuple-element.32.refs_4_), channel_id=1, source_target_pairs={{0,2},{1,3},{2,0},{3,1},{4,6},{5,7},{6,4},{7,5},{8,10},{9,11},{10,... | collective-permute-start | bytes 12296 | tf_op jit(solution)/shard_map/ppermute | solution.py:93
  36.2 1.7 %collective-permute-done.7.refs_6_ = f32[8,128]{1,0:T(8,128)S(1)} collective-permute-done((f32[8,128]{1,0:T(8,128)S(1)}, f32[8,128]{1,0:T(8,128)S(1)}, u32[]{:S(2)}, u32[]{:S(2)}) %collective-permute-start.7) | collective-permute-done | bytes 4128 | tf_op jit(solution)/shard_map/ppermute | solution.py:93
  38.0 1.1 %collective-permute-done.8.refs_7_ = f32[8,128]{1,0:T(8,128)S(1)} collective-permute-done((f32[8,128]{1,0:T(8,128)S(1)}, f32[8,128]{1,0:T(8,128)S(1)}, u32[]{:S(2)}, u32[]{:S(2)}) %collective-permute-start.8) | collective-permute-done | bytes 4128 | tf_op jit(solution)/shard_map/ppermute | solution.py:93
  39.1 10.7 %sweep_first.1 = (f32[2048,1024]{1,0:T(8,128)S(1)}, f32[2048,1024]{1,0:T(8,128)S(1)}, f32[2048,1024]{1,0:T(8,128)S(1)}, f32[2048,1024]{1,0:T(8,128)S(1)}, f32[8,128]{1,0:T(8,128)S(1)}) custom-call(f32[2048,1024]{1,0:T(8,128)S(1)} %get-tuple-element.26.refs_0_, ...), custom_call_target="tpu_custom_call", output_to_operand_aliasing={{0}: (0, {}), {1}: (1, {}), {2}: (2, {}), {3}: (3, {})} | custom-call | tf_op jit(solution)/shard_map/sweep_first/pallas_call | solution.py:430
  51.2 1.0 collective-permute-start.12
  52.2 2.0 %collective-permute-done.11.refs_6_ = f32[8,128]{1,0:T(8,128)S(1)} collective-permute-done((f32[8,128]{1,0:T(8,128)S(1)}, f32[8,128]{1,0:T(8,128)S(1)}, u32[]{:S(2)}, u32[]{:S(2)}) %collective-permute-start.11) | collective-permute-done | bytes 4128 | tf_op jit(solution)/shard_map/ppermute | solution.py:93
  54.3 7.2 %sweep.1.refs_4_.refs_8_ = f32[24,128]{1,0:T(8,128)S(1)} custom-call(f32[2048,1024]{1,0:T(8,128)S(1)} %get-tuple-element.33.refs_0_, f32[2048,1024]{1,0:T(8,128)S(1)} %get-tuple-element.34.refs_1_, f32[2048,1024]{1,0:T(8,128)S(1)} %get-tuple-element.35.refs_2_, f32[2048,1024]{1,0:T(8,128)S(1)} %get-tuple-element.36.refs_3_, ...), custom_call_target="tpu_custom_call" | custom-call | tf_op jit(solution)/shard_map/sweep/pallas_call | solution.py:430
  61.6 1.4 %collective-permute-start.15 = (f32[24,128]{1,0:T(8,128)S(1)}, f32[24,128]{1,0:T(8,128)S(1)}, u32[]{:S(2)}, u32[]{:S(2)}) collective-permute-start(f32[24,128]{1,0:T(8,128)S(1)} %sweep.1.refs_4_.refs_8_), channel_id=1, source_target_pairs={{0,2},{1,3},{2,0},{3,1},{4,6},{5,7},{6,4},{7,5},{8,10},{9,11},{10,... | collective-permute-start | bytes 36872 | tf_op jit(solution)/shard_map/ppermute | solution.py:93
  63.4 1.9 %collective-permute-done.15.refs_6_.refs_10_ = f32[24,128]{1,0:T(8,128)S(1)} collective-permute-done((f32[24,128]{1,0:T(8,128)S(1)}, f32[24,128]{1,0:T(8,128)S(1)}, u32[]{:S(2)}, u32[]{:S(2)}) %collective-permute-start.15) | collective-permute-done | bytes 12320 | tf_op jit(solution)/shard_map/ppermute | solution.py:93
  65.3 0.8 collective-permute-done.16.refs_7_.refs_11_
  66.2 9.1 %sweep_last.1 = (f32[2048,1024]{1,0:T(8,128)S(1)}, f32[2048,1024]{1,0:T(8,128)S(1)}, f32[2048,1024]{1,0:T(8,128)S(1)}, f32[2048,1024]{1,0:T(8,128)S(1)}, f32[8,128]{1,0:T(8,128)S(1)}) custom-call(f32[2048,1024]{1,0:T(8,128)S(1)} %get-tuple-element.33.refs_0_, ...), custom_call_target="tpu_custom_call", output_to_operand_aliasing={{0}: (0, {}), {1}: (1, {}), {2}: (2, {}), {3}: (3, {})} | custom-call | tf_op jit(solution)/shard_map/sweep_last/pallas_call | solution.py:430
  75.4 0.7 collective-permute-start.18
  76.2 1.0 %collective-permute-start.19 = (f32[8,128]{1,0:T(8,128)S(1)}, f32[8,128]{1,0:T(8,128)S(1)}, u32[]{:S(2)}, u32[]{:S(2)}) collective-permute-start(f32[8,128]{1,0:T(8,128)S(1)} %get-tuple-element.46.refs_4_), channel_id=1, source_target_pairs={{0,3},{1,2},{2,1},{3,0},{4,7},{5,6},{6,5},{7,4},{8,11},{9,10},{10,... | collective-permute-start | bytes 12296 | tf_op jit(solution)/shard_map/ppermute | solution.py:93
  77.2 1.9 %collective-permute-done.18.refs_6_ = f32[8,128]{1,0:T(8,128)S(1)} collective-permute-done((f32[8,128]{1,0:T(8,128)S(1)}, f32[8,128]{1,0:T(8,128)S(1)}, u32[]{:S(2)}, u32[]{:S(2)}) %collective-permute-start.18) | collective-permute-done | bytes 4128 | tf_op jit(solution)/shard_map/ppermute | solution.py:93
  79.2 2.5 %shard_map.51 = f32[128,128]{1,0:T(8,128)S(1)} custom-call(f32[2048,1024]{1,0:T(8,128)S(1)} %get-tuple-element.42.refs_0_, f32[2048,1024]{1,0:T(8,128)S(1)} %get-tuple-element.43.refs_1_, f32[2048,1024]{1,0:T(8,128)S(1)} %get-tuple-element.44.refs_2_, f32[2048,1024]{1,0:T(8,128)S(1)} %get-tuple-element.45.refs_3_, f32[8,128]{1,0:T(8,128)S(1)} %get-tuple-element.46.refs_4_, ...), custom_call_target="tpu_custom_call" | custom-call | tf_op jit(solution)/shard_map/pallas_call | solution.py:460
  81.9 1.3 %collective-permute-start.22 = (f32[128,128]{1,0:T(8,128)S(1)}, f32[128,128]{1,0:T(8,128)S(1)}, u32[]{:S(2)}, u32[]{:S(2)}) collective-permute-start(f32[128,128]{1,0:T(8,128)S(1)} %shard_map.51), channel_id=1, source_target_pairs={{0,2},{1,3},{2,0},{3,1},{4,6},{5,7},{6,4},{7,5},{8,10},{9,11},{10,... | collective-permute-start | bytes 196616 | tf_op jit(solution)/shard_map/ppermute | solution.py:93
  83.6 14.5 %shard_map.50 = f32[16,8192]{1,0:T(8,128)} custom-call(f32[2048,1024]{1,0:T(8,128)S(1)} %get-tuple-element.42.refs_0_, f32[2048,1024]{1,0:T(8,128)S(1)} %get-tuple-element.43.refs_1_, f32[2048,1024]{1,0:T(8,128)S(1)} %get-tuple-element.44.refs_2_, f32[2048,1024]{1,0:T(8,128)S(1)} %get-tuple-element.45.refs_3_, f32[8,128]{1,0:T(8,128)S(1)} %get-tuple-element.46.refs_4_, ...), custom_call_target="tpu_custom_call" | custom-call | tf_op jit(solution)/shard_map/pallas_call | solution.py:460
  98.1 0.6 add_add_fusion
  (35 shorter events, 3.8 us)
Async XLA Ops:
  1.4 6.3 %collective-permute-start = (f32[1,64,128]{2,1,0:T(8,128)S(1)}, f32[1,64,128]{2,1,0:T(8,128)S(1)}, u32[]{:S(2)}, u32[]{:S(2)}) collective-permute-start(f32[1,64,128]{2,1,0:T(8,128)S(1)} %bitcast_convert_fusion), channel_id=1, source_target_pairs={{0,16},{4,20},{8,24},{12,28},{16,0},{20,4},{24,8},{28,12},{1,17},{... | collective-permute-start | bytes 98312 | tf_op jit(solution)/shard_map/ppermute | solution.py:93
  7.7 4.3 %collective-permute-start.1 = (f32[2,64,128]{2,1,0:T(8,128)S(1)}, f32[2,64,128]{2,1,0:T(8,128)S(1)}, u32[]{:S(2)}, u32[]{:S(2)}) collective-permute-start(f32[2,64,128]{2,1,0:T(8,128)S(1)} %pad_maximum_fusion.4), channel_id=1, source_target_pairs={{0,8},{4,12},{8,0},{12,4},{16,24},{20,28},{24,16},{28,20},{1,9},{5... | collective-permute-start | bytes 196616 | tf_op jit(solution)/shard_map/ppermute | solution.py:93
  12.0 8.8 %collective-permute-start.2 = (f32[4,64,128]{2,1,0:T(8,128)S(1)}, f32[4,64,128]{2,1,0:T(8,128)S(1)}, u32[]{:S(2)}, u32[]{:S(2)}) collective-permute-start(f32[4,64,128]{2,1,0:T(8,128)S(1)} %pad_maximum_fusion.2), channel_id=1, source_target_pairs={{0,4},{4,0},{8,12},{12,8},{16,20},{20,16},{24,28},{28,24},{1,5},{5... | collective-permute-start | bytes 393224 | tf_op jit(solution)/shard_map/ppermute | solution.py:93
  13.8 1.6 %copy-start = (bf16[128,8192]{1,0:T(8,128)(2,1)S(1)}, bf16[128,8192]{1,0:T(8,128)(2,1)}, u32[]{:S(2)}) copy-start(bf16[128,8192]{1,0:T(8,128)(2,1)} %w_ref.1) | copy-start | bytes 6291460
  15.4 0.8 copy-start.1
  18.4 4.9 %collective-permute-start.4 = (f32[1,72,128]{2,1,0:T(8,128)S(1)}, f32[1,72,128]{2,1,0:T(8,128)S(1)}, u32[]{:S(2)}, u32[]{:S(2)}) collective-permute-start(f32[1,72,128]{2,1,0:T(8,128)S(1)} %bitcast.6), channel_id=1, source_target_pairs={{0,16},{4,20},{8,24},{12,28},{16,0},{20,4},{24,8},{28,12},{1,17},{... | collective-permute-start | bytes 110600 | tf_op jit(solution)/shard_map/ppermute | solution.py:93
  20.8 6.8 %collective-permute-start.3 = (f32[8,64,128]{2,1,0:T(8,128)S(1)}, f32[8,64,128]{2,1,0:T(8,128)S(1)}, u32[]{:S(2)}, u32[]{:S(2)}) collective-permute-start(f32[8,64,128]{2,1,0:T(8,128)S(1)} %pad_maximum_fusion.mine_ref), channel_id=1, source_target_pairs={{0,1},{1,0},{2,3},{3,2},{4,5},{5,4},{6,7},{7,6},{8,9},{9,8},{10,11... | collective-permute-start | bytes 786440 | tf_op jit(solution)/shard_map/ppermute | solution.py:93
  23.3 4.4 %collective-permute-start.5 = (f32[2,72,128]{2,1,0:T(8,128)S(1)}, f32[2,72,128]{2,1,0:T(8,128)S(1)}, u32[]{:S(2)}, u32[]{:S(2)}) collective-permute-start(f32[2,72,128]{2,1,0:T(8,128)S(1)} %pad_maximum_fusion.3), channel_id=1, source_target_pairs={{0,8},{4,12},{8,0},{12,4},{16,24},{20,28},{24,16},{28,20},{1,9},{5... | collective-permute-start | bytes 221192 | tf_op jit(solution)/shard_map/ppermute | solution.py:93
  34.0 15.7 %collective-permute-start.9 = (f32[4,72,128]{2,1,0:T(8,128)S(1)}, f32[4,72,128]{2,1,0:T(8,128)S(1)}, u32[]{:S(2)}, u32[]{:S(2)}) collective-permute-start(f32[4,72,128]{2,1,0:T(8,128)S(1)} %pad_maximum_fusion.1.refs_8_.refs_12_), channel_id=1, source_target_pairs={{0,4},{4,0},{8,12},{12,8},{16,20},{20,16},{24,28},{28,24},{1,5},{5... | collective-permute-start | bytes 442376 | tf_op jit(solution)/shard_map/ppermute | solution.py:93
  34.4 1.9 %collective-permute-start.6 = (f32[8,128]{1,0:T(8,128)S(1)}, f32[8,128]{1,0:T(8,128)S(1)}, u32[]{:S(2)}, u32[]{:S(2)}) collective-permute-start(f32[8,128]{1,0:T(8,128)S(1)} %get-tuple-element.32.refs_4_), channel_id=1, source_target_pairs={{0,1},{1,0},{2,3},{3,2},{4,5},{5,4},{6,7},{7,6},{8,9},{9,8},{10,11... | collective-permute-start | bytes 12296 | tf_op jit(solution)/shard_map/ppermute | solution.py:93
  34.4 3.6 %collective-permute-start.7 = (f32[8,128]{1,0:T(8,128)S(1)}, f32[8,128]{1,0:T(8,128)S(1)}, u32[]{:S(2)}, u32[]{:S(2)}) collective-permute-start(f32[8,128]{1,0:T(8,128)S(1)} %get-tuple-element.32.refs_4_), channel_id=1, source_target_pairs={{0,2},{1,3},{2,0},{3,1},{4,6},{5,7},{6,4},{7,5},{8,10},{9,11},{10,... | collective-permute-start | bytes 12296 | tf_op jit(solution)/shard_map/ppermute | solution.py:93
  36.0 3.0 %collective-permute-start.8 = (f32[8,128]{1,0:T(8,128)S(1)}, f32[8,128]{1,0:T(8,128)S(1)}, u32[]{:S(2)}, u32[]{:S(2)}) collective-permute-start(f32[8,128]{1,0:T(8,128)S(1)} %get-tuple-element.32.refs_4_), channel_id=1, source_target_pairs={{0,3},{1,2},{2,1},{3,0},{4,7},{5,6},{6,5},{7,4},{8,11},{9,10},{10,... | collective-permute-start | bytes 12296 | tf_op jit(solution)/shard_map/ppermute | solution.py:93
  49.7 11.7 %collective-permute-start.13 = (f32[4,72,128]{2,1,0:T(8,128)S(1)}, f32[4,72,128]{2,1,0:T(8,128)S(1)}, u32[]{:S(2)}, u32[]{:S(2)}) collective-permute-start(f32[4,72,128]{2,1,0:T(8,128)S(1)} %collective-permute-done.9.refs_9_.refs_14_), channel_id=1, source_target_pairs={{0,1},{1,0},{2,3},{3,2},{4,5},{5,4},{6,7},{7,6},{8,9},{9,8},{10,11... | collective-permute-start | bytes 442376 | tf_op jit(solution)/shard_map/ppermute | solution.py:93
  50.1 27.1 %collective-permute-start.20 = (f32[4,72,128]{2,1,0:T(8,128)S(1)}, f32[4,72,128]{2,1,0:T(8,128)S(1)}, u32[]{:S(2)}, u32[]{:S(2)}) collective-permute-start(f32[4,72,128]{2,1,0:T(8,128)S(1)} %pad_maximum_fusion.1.refs_8_.refs_12_), channel_id=1, source_target_pairs={{0,1},{1,0},{2,3},{3,2},{4,5},{5,4},{6,7},{7,6},{8,9},{9,8},{10,11... | collective-permute-start | bytes 442376 | tf_op jit(solution)/shard_map/ppermute | solution.py:93
  50.3 1.9 %collective-permute-start.10 = (f32[8,128]{1,0:T(8,128)S(1)}, f32[8,128]{1,0:T(8,128)S(1)}, u32[]{:S(2)}, u32[]{:S(2)}) collective-permute-start(f32[8,128]{1,0:T(8,128)S(1)} %get-tuple-element.39.refs_4_), channel_id=1, source_target_pairs={{0,1},{1,0},{2,3},{3,2},{4,5},{5,4},{6,7},{7,6},{8,9},{9,8},{10,11... | collective-permute-start | bytes 12296 | tf_op jit(solution)/shard_map/ppermute | solution.py:93
  50.6 3.6 %collective-permute-start.11 = (f32[8,128]{1,0:T(8,128)S(1)}, f32[8,128]{1,0:T(8,128)S(1)}, u32[]{:S(2)}, u32[]{:S(2)}) collective-permute-start(f32[8,128]{1,0:T(8,128)S(1)} %get-tuple-element.39.refs_4_), channel_id=1, source_target_pairs={{0,2},{1,3},{2,0},{3,1},{4,6},{5,7},{6,4},{7,5},{8,10},{9,11},{10,... | collective-permute-start | bytes 12296 | tf_op jit(solution)/shard_map/ppermute | solution.py:93
  51.2 3.0 %collective-permute-start.12 = (f32[8,128]{1,0:T(8,128)S(1)}, f32[8,128]{1,0:T(8,128)S(1)}, u32[]{:S(2)}, u32[]{:S(2)}) collective-permute-start(f32[8,128]{1,0:T(8,128)S(1)} %get-tuple-element.39.refs_4_), channel_id=1, source_target_pairs={{0,3},{1,2},{2,1},{3,0},{4,7},{5,6},{6,5},{7,4},{8,11},{9,10},{10,... | collective-permute-start | bytes 12296 | tf_op jit(solution)/shard_map/ppermute | solution.py:93
  61.5 1.9 %collective-permute-start.14 = (f32[24,128]{1,0:T(8,128)S(1)}, f32[24,128]{1,0:T(8,128)S(1)}, u32[]{:S(2)}, u32[]{:S(2)}) collective-permute-start(f32[24,128]{1,0:T(8,128)S(1)} %sweep.1.refs_4_.refs_8_), channel_id=1, source_target_pairs={{0,1},{1,0},{2,3},{3,2},{4,5},{5,4},{6,7},{7,6},{8,9},{9,8},{10,11... | collective-permute-start | bytes 36872 | tf_op jit(solution)/shard_map/ppermute | solution.py:93
  61.6 3.7 %collective-permute-start.15 = (f32[24,128]{1,0:T(8,128)S(1)}, f32[24,128]{1,0:T(8,128)S(1)}, u32[]{:S(2)}, u32[]{:S(2)}) collective-permute-start(f32[24,128]{1,0:T(8,128)S(1)} %sweep.1.refs_4_.refs_8_), channel_id=1, source_target_pairs={{0,2},{1,3},{2,0},{3,1},{4,6},{5,7},{6,4},{7,5},{8,10},{9,11},{10,... | collective-permute-start | bytes 36872 | tf_op jit(solution)/shard_map/ppermute | solution.py:93
  63.0 3.1 %collective-permute-start.16 = (f32[24,128]{1,0:T(8,128)S(1)}, f32[24,128]{1,0:T(8,128)S(1)}, u32[]{:S(2)}, u32[]{:S(2)}) collective-permute-start(f32[24,128]{1,0:T(8,128)S(1)} %sweep.1.refs_4_.refs_8_), channel_id=1, source_target_pairs={{0,3},{1,2},{2,1},{3,0},{4,7},{5,6},{6,5},{7,4},{8,11},{9,10},{10,... | collective-permute-start | bytes 36872 | tf_op jit(solution)/shard_map/ppermute | solution.py:93
  75.3 1.9 %collective-permute-start.17 = (f32[8,128]{1,0:T(8,128)S(1)}, f32[8,128]{1,0:T(8,128)S(1)}, u32[]{:S(2)}, u32[]{:S(2)}) collective-permute-start(f32[8,128]{1,0:T(8,128)S(1)} %get-tuple-element.46.refs_4_), channel_id=1, source_target_pairs={{0,1},{1,0},{2,3},{3,2},{4,5},{5,4},{6,7},{7,6},{8,9},{9,8},{10,11... | collective-permute-start | bytes 12296 | tf_op jit(solution)/shard_map/ppermute | solution.py:93
  75.4 3.6 %collective-permute-start.18 = (f32[8,128]{1,0:T(8,128)S(1)}, f32[8,128]{1,0:T(8,128)S(1)}, u32[]{:S(2)}, u32[]{:S(2)}) collective-permute-start(f32[8,128]{1,0:T(8,128)S(1)} %get-tuple-element.46.refs_4_), channel_id=1, source_target_pairs={{0,2},{1,3},{2,0},{3,1},{4,6},{5,7},{6,4},{7,5},{8,10},{9,11},{10,... | collective-permute-start | bytes 12296 | tf_op jit(solution)/shard_map/ppermute | solution.py:93
  76.2 3.0 %collective-permute-start.19 = (f32[8,128]{1,0:T(8,128)S(1)}, f32[8,128]{1,0:T(8,128)S(1)}, u32[]{:S(2)}, u32[]{:S(2)}) collective-permute-start(f32[8,128]{1,0:T(8,128)S(1)} %get-tuple-element.46.refs_4_), channel_id=1, source_target_pairs={{0,3},{1,2},{2,1},{3,0},{4,7},{5,6},{6,5},{7,4},{8,11},{9,10},{10,... | collective-permute-start | bytes 12296 | tf_op jit(solution)/shard_map/ppermute | solution.py:93
  81.7 16.4 %collective-permute-start.21 = (f32[128,128]{1,0:T(8,128)S(1)}, f32[128,128]{1,0:T(8,128)S(1)}, u32[]{:S(2)}, u32[]{:S(2)}) collective-permute-start(f32[128,128]{1,0:T(8,128)S(1)} %shard_map.51), channel_id=1, source_target_pairs={{0,1},{1,0},{2,3},{3,2},{4,5},{5,4},{6,7},{7,6},{8,9},{9,8},{10,11... | collective-permute-start | bytes 196616 | tf_op jit(solution)/shard_map/ppermute | solution.py:93
  81.9 16.2 %collective-permute-start.22 = (f32[128,128]{1,0:T(8,128)S(1)}, f32[128,128]{1,0:T(8,128)S(1)}, u32[]{:S(2)}, u32[]{:S(2)}) collective-permute-start(f32[128,128]{1,0:T(8,128)S(1)} %shard_map.51), channel_id=1, source_target_pairs={{0,2},{1,3},{2,0},{3,1},{4,6},{5,7},{6,4},{7,5},{8,10},{9,11},{10,... | collective-permute-start | bytes 196616 | tf_op jit(solution)/shard_map/ppermute | solution.py:93
  83.2 14.9 %collective-permute-start.23 = (f32[128,128]{1,0:T(8,128)S(1)}, f32[128,128]{1,0:T(8,128)S(1)}, u32[]{:S(2)}, u32[]{:S(2)}) collective-permute-start(f32[128,128]{1,0:T(8,128)S(1)} %shard_map.51), channel_id=1, source_target_pairs={{0,3},{1,2},{2,1},{3,0},{4,7},{5,6},{6,5},{7,4},{8,11},{9,10},{10,... | collective-permute-start | bytes 196616 | tf_op jit(solution)/shard_map/ppermute | solution.py:93

commit v6 on v5

--- a/solution.py
+++ b/solution.py
@@ -230,7 +230,7 @@
     ones = jnp.ones((LANES, LANES), jnp.bfloat16)
 
     def invert(i, unused):
-        at = pl.ds(pl.multiple_of(i * 1024, 1024), 1024)
+        at = pl.ds(pl.multiple_of(i * per, per), per)
         y = y_scr[at, :]
         high = y.astype(jnp.bfloat16)
         low = (y - high.astype(jnp.float32)).astype(jnp.bfloat16)
@@ -239,7 +239,7 @@
         y_scr[at, :] = 1.0 / total
         return 0
 
-    lax.fori_loop(0, PARTS * per // 1024, invert, 0)
+    lax.fori_loop(0, PARTS, invert, 0)
     acc = (jnp.zeros((SUB, LANES), jnp.float32),) * n
     for p in range(PARTS):
 
@@ -474,7 +474,7 @@
         [pltpu.VMEM((own, depth), bf16)] + pair * 2,
     )
     parts = everyone(own_part)
-    pair = [pltpu.VMEM((512, rows), f32), pltpu.VMEM((512, rows), bf16)]
+    pair = [pltpu.VMEM((1024, rows), f32), pltpu.VMEM((1024, rows), bf16)]
     proto_grad = final(
         proto_grad_body,
         (near, near_other, far, far_other, weight_t),
@@ -496,7 +496,7 @@
             own * n_dp * cols * 4 <= KERNEL_BYTES
             and own == LANES
             and depth == LANES
-            and cols % (PARTS * 1024) == 0
+            and cols % (PARTS * 2048) == 0
             and n_dp & (n_dp - 1) == 0
             and n_proto & (n_proto - 1) == 0
             and 2 <= n_proto <= 8

time: 99 us -> 95.5 us (0.965)
  Pallas kernels: 52.4 us -> 48.9 us
    pallas_call x3, Pallas kernels: 27 us -> 25.1 us  [sweep(): pl.pallas_call(lambda *refs: sweep_body(first, last, len(ins), len(extra)...]
    pallas_call x2, Pallas kernels: 17 us -> 15.2 us  [final(): pl.pallas_call(lambda *refs: body(len(ins), *refs), out_shape=jax.ShapeDt...]
  transfers between devices with their start and end apart: 24 -> 24, of which waited for: 12 -> 12; matrix products, arithmetic and copies ran while one was open for 0% -> 0% of each run, Pallas kernels for 44% -> 42%
where the time goes in v6:
time: 95.5 us; the launch traced here: 95.2 us
  Pallas kernels  48.9 us (51%)
  starting transfers between devices  21.7 us (23%)
  waiting for transfers between devices  20 us (21%)
  local copies, waits for them, and re-layouts  2.35 us (2%)
  other arithmetic  1.5 us (2%)
    pallas_call x3, Pallas kernels, sweep(): pl.pallas_call(lambda *refs: sweep_body(first, last, len(ins), len(extra)...  25.1 us
    ppermute x24, starting transfers between devices, swap(): lax.ppermute(x, axis, [(i, i ^ bit) for i in range(lax.axis_size(axis))])  21.7 us
    ppermute x24, waiting for transfers between devices, swap(): lax.ppermute(x, axis, [(i, i ^ bit) for i in range(lax.axis_size(axis))])  20 us
    pallas_call x2, Pallas kernels, final(): pl.pallas_call(lambda *refs: body(len(ins), *refs), out_shape=jax.ShapeDt...  15.2 us
    pallas_call x1, Pallas kernels, all_crops(): pl.pallas_call(scores_body, out_shape=(k_shape,) * PARTS + (flat,), in_sp...  6.33 us
    unnamed x4, local copies, waits for them, and re-layouts  2.35 us
    pallas_call x1, Pallas kernels, all_crops(): student_part, weight_t = own_stats(place, student_feat, proto_weight)  2.16 us
  transfers between devices with their start and end apart: 24, of which 12 were waited for; matrix products, arithmetic and copies ran while one was open for 0% of the time, Pallas kernels for 42%

profile of v6, /device:TPU:0, one launch (start us, length us, event | category | flops | bytes accessed | tf_op | source)
XLA Modules:
  0.0 95.2 jit_solution(328447963267593286)
XLA Ops:
  0.6 0.7 bitcast_convert_fusion
  1.4 4.1 %collective-permute-start = (f32[1,64,128]{2,1,0:T(8,128)S(1)}, f32[1,64,128]{2,1,0:T(8,128)S(1)}, u32[]{:S(2)}, u32[]{:S(2)}) collective-permute-start(f32[1,64,128]{2,1,0:T(8,128)S(1)} %bitcast_convert_fusion), channel_id=1, source_target_pairs={{0,16},{4,20},{8,24},{12,28},{16,0},{20,4},{24,8},{28,12},{1,17},{... | collective-permute-start | bytes 98312 | tf_op jit(solution)/shard_map/ppermute | solution.py:93
  5.4 2.2 %collective-permute-done = f32[1,64,128]{2,1,0:T(8,128)S(1)} collective-permute-done((f32[1,64,128]{2,1,0:T(8,128)S(1)}, f32[1,64,128]{2,1,0:T(8,128)S(1)}, u32[]{:S(2)}, u32[]{:S(2)}) %collective-permute-start) | collective-permute-done | bytes 32800 | tf_op jit(solution)/shard_map/ppermute | solution.py:93
  7.7 1.6 %collective-permute-start.1 = (f32[2,64,128]{2,1,0:T(8,128)S(1)}, f32[2,64,128]{2,1,0:T(8,128)S(1)}, u32[]{:S(2)}, u32[]{:S(2)}) collective-permute-start(f32[2,64,128]{2,1,0:T(8,128)S(1)} %pad_maximum_fusion.4), channel_id=1, source_target_pairs={{0,8},{4,12},{8,0},{12,4},{16,24},{20,28},{24,16},{28,20},{1,9},{5... | collective-permute-start | bytes 196616 | tf_op jit(solution)/shard_map/ppermute | solution.py:93
  9.2 2.7 %collective-permute-done.1 = f32[2,64,128]{2,1,0:T(8,128)S(1)} collective-permute-done((f32[2,64,128]{2,1,0:T(8,128)S(1)}, f32[2,64,128]{2,1,0:T(8,128)S(1)}, u32[]{:S(2)}, u32[]{:S(2)}) %collective-permute-start.1) | collective-permute-done | bytes 65568 | tf_op jit(solution)/shard_map/ppermute | solution.py:93
  12.0 1.8 %collective-permute-start.2 = (f32[4,64,128]{2,1,0:T(8,128)S(1)}, f32[4,64,128]{2,1,0:T(8,128)S(1)}, u32[]{:S(2)}, u32[]{:S(2)}) collective-permute-start(f32[4,64,128]{2,1,0:T(8,128)S(1)} %pad_maximum_fusion.2), channel_id=1, source_target_pairs={{0,4},{4,0},{8,12},{12,8},{16,20},{20,16},{24,28},{28,24},{1,5},{5... | collective-permute-start | bytes 393224 | tf_op jit(solution)/shard_map/ppermute | solution.py:93
  13.8 1.6 %copy-done = bf16[128,8192]{1,0:T(8,128)(2,1)S(1)} copy-done((bf16[128,8192]{1,0:T(8,128)(2,1)S(1)}, bf16[128,8192]{1,0:T(8,128)(2,1)}, u32[]{:S(2)}) %copy-start) | copy-done | bytes 2097176
  15.4 0.8 copy-done.1
  16.2 2.2 %own_stats.1 = (f32[72,128]{1,0:T(8,128)S(1)}, bf16[8192,128]{1,0:T(8,128)(2,1)S(1)}) custom-call(s32[2]{0:T(128)S(1)} %pad_add_fusion.place_ref.refs_17_.refs_15_, bf16[128,128]{1,0:T(8,128)(2,1)S(1)} %copy-done.1, bf16[128,8192]{1,0:T(8,128)(2,1)S(1)} %copy-done), custom_call_target="tpu_custom_call" | custom-call | tf_op jit(solution)/shard_map/own_stats/pallas_call | solution.py:411
  18.4 2.4 %collective-permute-start.4 = (f32[1,72,128]{2,1,0:T(8,128)S(1)}, f32[1,72,128]{2,1,0:T(8,128)S(1)}, u32[]{:S(2)}, u32[]{:S(2)}) collective-permute-start(f32[1,72,128]{2,1,0:T(8,128)S(1)} %bitcast.6), channel_id=1, source_target_pairs={{0,16},{4,20},{8,24},{12,28},{16,0},{20,4},{24,8},{28,12},{1,17},{... | collective-permute-start | bytes 110600 | tf_op jit(solution)/shard_map/ppermute | solution.py:93
  20.9 2.4 %collective-permute-done.4 = f32[1,72,128]{2,1,0:T(8,128)S(1)} collective-permute-done((f32[1,72,128]{2,1,0:T(8,128)S(1)}, f32[1,72,128]{2,1,0:T(8,128)S(1)}, u32[]{:S(2)}, u32[]{:S(2)}) %collective-permute-start.4) | collective-permute-done | bytes 36896 | tf_op jit(solution)/shard_map/ppermute | solution.py:93
  23.3 1.4 %collective-permute-start.5 = (f32[2,72,128]{2,1,0:T(8,128)S(1)}, f32[2,72,128]{2,1,0:T(8,128)S(1)}, u32[]{:S(2)}, u32[]{:S(2)}) collective-permute-start(f32[2,72,128]{2,1,0:T(8,128)S(1)} %pad_maximum_fusion.3), channel_id=1, source_target_pairs={{0,8},{4,12},{8,0},{12,4},{16,24},{20,28},{24,16},{28,20},{1,9},{5... | collective-permute-start | bytes 221192 | tf_op jit(solution)/shard_map/ppermute | solution.py:93
  24.6 3.0 %collective-permute-done.5 = f32[2,72,128]{2,1,0:T(8,128)S(1)} collective-permute-done((f32[2,72,128]{2,1,0:T(8,128)S(1)}, f32[2,72,128]{2,1,0:T(8,128)S(1)}, u32[]{:S(2)}, u32[]{:S(2)}) %collective-permute-start.5) | collective-permute-done | bytes 73760 | tf_op jit(solution)/shard_map/ppermute | solution.py:93
  27.7 6.3 %scores.1 = (f32[2048,1024]{1,0:T(8,128)S(1)}, f32[2048,1024]{1,0:T(8,128)S(1)}, f32[2048,1024]{1,0:T(8,128)S(1)}, f32[2048,1024]{1,0:T(8,128)S(1)}, f32[8,128]{1,0:T(8,128)S(1)}) custom-call(s32[2]{0:T(128)S(1)} %pad_add_fusion.place_ref.refs_17_.refs_15_, f32[8,64,128]{2,1,0:T(8,128)S(1)} %pad_maximum_fusion.mine_ref, ...), custom_call_target="tpu_custom_call" | custom-call | tf_op jit(solution)/shard_map/scores/pallas_call | solution.py:416
  34.4 1.7 %collective-permute-start.7 = (f32[8,128]{1,0:T(8,128)S(1)}, f32[8,128]{1,0:T(8,128)S(1)}, u32[]{:S(2)}, u32[]{:S(2)}) collective-permute-start(f32[8,128]{1,0:T(8,128)S(1)} %get-tuple-element.32.refs_4_), channel_id=1, source_target_pairs={{0,2},{1,3},{2,0},{3,1},{4,6},{5,7},{6,4},{7,5},{8,10},{9,11},{10,... | collective-permute-start | bytes 12296 | tf_op jit(solution)/shard_map/ppermute | solution.py:93
  36.2 1.7 %collective-permute-done.7.refs_6_ = f32[8,128]{1,0:T(8,128)S(1)} collective-permute-done((f32[8,128]{1,0:T(8,128)S(1)}, f32[8,128]{1,0:T(8,128)S(1)}, u32[]{:S(2)}, u32[]{:S(2)}) %collective-permute-start.7) | collective-permute-done | bytes 4128 | tf_op jit(solution)/shard_map/ppermute | solution.py:93
  38.0 1.1 %collective-permute-done.8.refs_7_ = f32[8,128]{1,0:T(8,128)S(1)} collective-permute-done((f32[8,128]{1,0:T(8,128)S(1)}, f32[8,128]{1,0:T(8,128)S(1)}, u32[]{:S(2)}, u32[]{:S(2)}) %collective-permute-start.8) | collective-permute-done | bytes 4128 | tf_op jit(solution)/shard_map/ppermute | solution.py:93
  39.1 10.0 %sweep_first.1 = (f32[2048,1024]{1,0:T(8,128)S(1)}, f32[2048,1024]{1,0:T(8,128)S(1)}, f32[2048,1024]{1,0:T(8,128)S(1)}, f32[2048,1024]{1,0:T(8,128)S(1)}, f32[8,128]{1,0:T(8,128)S(1)}) custom-call(f32[2048,1024]{1,0:T(8,128)S(1)} %get-tuple-element.26.refs_0_, ...), custom_call_target="tpu_custom_call", output_to_operand_aliasing={{0}: (0, {}), {1}: (1, {}), {2}: (2, {}), {3}: (3, {})} | custom-call | tf_op jit(solution)/shard_map/sweep_first/pallas_call | solution.py:430
  50.6 1.0 %collective-permute-start.12 = (f32[8,128]{1,0:T(8,128)S(1)}, f32[8,128]{1,0:T(8,128)S(1)}, u32[]{:S(2)}, u32[]{:S(2)}) collective-permute-start(f32[8,128]{1,0:T(8,128)S(1)} %get-tuple-element.39.refs_4_), channel_id=1, source_target_pairs={{0,3},{1,2},{2,1},{3,0},{4,7},{5,6},{6,5},{7,4},{8,11},{9,10},{10,... | collective-permute-start | bytes 12296 | tf_op jit(solution)/shard_map/ppermute | solution.py:93
  51.5 2.0 %collective-permute-done.11.refs_6_ = f32[8,128]{1,0:T(8,128)S(1)} collective-permute-done((f32[8,128]{1,0:T(8,128)S(1)}, f32[8,128]{1,0:T(8,128)S(1)}, u32[]{:S(2)}, u32[]{:S(2)}) %collective-permute-start.11) | collective-permute-done | bytes 4128 | tf_op jit(solution)/shard_map/ppermute | solution.py:93
  53.6 6.5 %sweep.1.refs_4_.refs_8_ = f32[24,128]{1,0:T(8,128)S(1)} custom-call(f32[2048,1024]{1,0:T(8,128)S(1)} %get-tuple-element.33.refs_0_, f32[2048,1024]{1,0:T(8,128)S(1)} %get-tuple-element.34.refs_1_, f32[2048,1024]{1,0:T(8,128)S(1)} %get-tuple-element.35.refs_2_, f32[2048,1024]{1,0:T(8,128)S(1)} %get-tuple-element.36.refs_3_, ...), custom_call_target="tpu_custom_call" | custom-call | tf_op jit(solution)/shard_map/sweep/pallas_call | solution.py:430
  60.3 1.4 %collective-permute-start.15 = (f32[24,128]{1,0:T(8,128)S(1)}, f32[24,128]{1,0:T(8,128)S(1)}, u32[]{:S(2)}, u32[]{:S(2)}) collective-permute-start(f32[24,128]{1,0:T(8,128)S(1)} %sweep.1.refs_4_.refs_8_), channel_id=1, source_target_pairs={{0,2},{1,3},{2,0},{3,1},{4,6},{5,7},{6,4},{7,5},{8,10},{9,11},{10,... | collective-permute-start | bytes 36872 | tf_op jit(solution)/shard_map/ppermute | solution.py:93
  62.1 1.9 %collective-permute-done.15.refs_6_.refs_10_ = f32[24,128]{1,0:T(8,128)S(1)} collective-permute-done((f32[24,128]{1,0:T(8,128)S(1)}, f32[24,128]{1,0:T(8,128)S(1)}, u32[]{:S(2)}, u32[]{:S(2)}) %collective-permute-start.15) | collective-permute-done | bytes 12320 | tf_op jit(solution)/shard_map/ppermute | solution.py:93
  64.0 0.8 collective-permute-done.16.refs_7_.refs_11_
  64.8 8.6 %sweep_last.1 = (f32[2048,1024]{1,0:T(8,128)S(1)}, f32[2048,1024]{1,0:T(8,128)S(1)}, f32[2048,1024]{1,0:T(8,128)S(1)}, f32[2048,1024]{1,0:T(8,128)S(1)}, f32[8,128]{1,0:T(8,128)S(1)}) custom-call(f32[2048,1024]{1,0:T(8,128)S(1)} %get-tuple-element.33.refs_0_, ...), custom_call_target="tpu_custom_call", output_to_operand_aliasing={{0}: (0, {}), {1}: (1, {}), {2}: (2, {}), {3}: (3, {})} | custom-call | tf_op jit(solution)/shard_map/sweep_last/pallas_call | solution.py:430
  73.6 0.7 collective-permute-start.18
  74.3 1.0 %collective-permute-start.19 = (f32[8,128]{1,0:T(8,128)S(1)}, f32[8,128]{1,0:T(8,128)S(1)}, u32[]{:S(2)}, u32[]{:S(2)}) collective-permute-start(f32[8,128]{1,0:T(8,128)S(1)} %get-tuple-element.46.refs_4_), channel_id=1, source_target_pairs={{0,3},{1,2},{2,1},{3,0},{4,7},{5,6},{6,5},{7,4},{8,11},{9,10},{10,... | collective-permute-start | bytes 12296 | tf_op jit(solution)/shard_map/ppermute | solution.py:93
  75.4 1.9 %collective-permute-done.18.refs_6_ = f32[8,128]{1,0:T(8,128)S(1)} collective-permute-done((f32[8,128]{1,0:T(8,128)S(1)}, f32[8,128]{1,0:T(8,128)S(1)}, u32[]{:S(2)}, u32[]{:S(2)}) %collective-permute-start.18) | collective-permute-done | bytes 4128 | tf_op jit(solution)/shard_map/ppermute | solution.py:93
  77.4 2.5 %shard_map.51 = f32[128,128]{1,0:T(8,128)S(1)} custom-call(f32[2048,1024]{1,0:T(8,128)S(1)} %get-tuple-element.42.refs_0_, f32[2048,1024]{1,0:T(8,128)S(1)} %get-tuple-element.43.refs_1_, f32[2048,1024]{1,0:T(8,128)S(1)} %get-tuple-element.44.refs_2_, f32[2048,1024]{1,0:T(8,128)S(1)} %get-tuple-element.45.refs_3_, f32[8,128]{1,0:T(8,128)S(1)} %get-tuple-element.46.refs_4_, ...), custom_call_target="tpu_custom_call" | custom-call | tf_op jit(solution)/shard_map/pallas_call | solution.py:460
  80.0 1.3 %collective-permute-start.22 = (f32[128,128]{1,0:T(8,128)S(1)}, f32[128,128]{1,0:T(8,128)S(1)}, u32[]{:S(2)}, u32[]{:S(2)}) collective-permute-start(f32[128,128]{1,0:T(8,128)S(1)} %shard_map.51), channel_id=1, source_target_pairs={{0,2},{1,3},{2,0},{3,1},{4,6},{5,7},{6,4},{7,5},{8,10},{9,11},{10,... | collective-permute-start | bytes 196616 | tf_op jit(solution)/shard_map/ppermute | solution.py:93
  81.8 12.8 %shard_map.50 = f32[16,8192]{1,0:T(8,128)} custom-call(f32[2048,1024]{1,0:T(8,128)S(1)} %get-tuple-element.42.refs_0_, f32[2048,1024]{1,0:T(8,128)S(1)} %get-tuple-element.43.refs_1_, f32[2048,1024]{1,0:T(8,128)S(1)} %get-tuple-element.44.refs_2_, f32[2048,1024]{1,0:T(8,128)S(1)} %get-tuple-element.45.refs_3_, f32[8,128]{1,0:T(8,128)S(1)} %get-tuple-element.46.refs_4_, ...), custom_call_target="tpu_custom_call" | custom-call | tf_op jit(solution)/shard_map/pallas_call | solution.py:460
  94.6 0.6 add_add_fusion
  (35 shorter events, 3.8 us)
Async XLA Ops:
  1.4 6.3 %collective-permute-start = (f32[1,64,128]{2,1,0:T(8,128)S(1)}, f32[1,64,128]{2,1,0:T(8,128)S(1)}, u32[]{:S(2)}, u32[]{:S(2)}) collective-permute-start(f32[1,64,128]{2,1,0:T(8,128)S(1)} %bitcast_convert_fusion), channel_id=1, source_target_pairs={{0,16},{4,20},{8,24},{12,28},{16,0},{20,4},{24,8},{28,12},{1,17},{... | collective-permute-start | bytes 98312 | tf_op jit(solution)/shard_map/ppermute | solution.py:93
  7.7 4.3 %collective-permute-start.1 = (f32[2,64,128]{2,1,0:T(8,128)S(1)}, f32[2,64,128]{2,1,0:T(8,128)S(1)}, u32[]{:S(2)}, u32[]{:S(2)}) collective-permute-start(f32[2,64,128]{2,1,0:T(8,128)S(1)} %pad_maximum_fusion.4), channel_id=1, source_target_pairs={{0,8},{4,12},{8,0},{12,4},{16,24},{20,28},{24,16},{28,20},{1,9},{5... | collective-permute-start | bytes 196616 | tf_op jit(solution)/shard_map/ppermute | solution.py:93
  12.0 8.8 %collective-permute-start.2 = (f32[4,64,128]{2,1,0:T(8,128)S(1)}, f32[4,64,128]{2,1,0:T(8,128)S(1)}, u32[]{:S(2)}, u32[]{:S(2)}) collective-permute-start(f32[4,64,128]{2,1,0:T(8,128)S(1)} %pad_maximum_fusion.2), channel_id=1, source_target_pairs={{0,4},{4,0},{8,12},{12,8},{16,20},{20,16},{24,28},{28,24},{1,5},{5... | collective-permute-start | bytes 393224 | tf_op jit(solution)/shard_map/ppermute | solution.py:93
  13.8 1.6 %copy-start = (bf16[128,8192]{1,0:T(8,128)(2,1)S(1)}, bf16[128,8192]{1,0:T(8,128)(2,1)}, u32[]{:S(2)}) copy-start(bf16[128,8192]{1,0:T(8,128)(2,1)} %w_ref.1) | copy-start | bytes 6291460
  15.4 0.8 copy-start.1
  18.4 4.9 %collective-permute-start.4 = (f32[1,72,128]{2,1,0:T(8,128)S(1)}, f32[1,72,128]{2,1,0:T(8,128)S(1)}, u32[]{:S(2)}, u32[]{:S(2)}) collective-permute-start(f32[1,72,128]{2,1,0:T(8,128)S(1)} %bitcast.6), channel_id=1, source_target_pairs={{0,16},{4,20},{8,24},{12,28},{16,0},{20,4},{24,8},{28,12},{1,17},{... | collective-permute-start | bytes 110600 | tf_op jit(solution)/shard_map/ppermute | solution.py:93
  20.8 6.8 %collective-permute-start.3 = (f32[8,64,128]{2,1,0:T(8,128)S(1)}, f32[8,64,128]{2,1,0:T(8,128)S(1)}, u32[]{:S(2)}, u32[]{:S(2)}) collective-permute-start(f32[8,64,128]{2,1,0:T(8,128)S(1)} %pad_maximum_fusion.mine_ref), channel_id=1, source_target_pairs={{0,1},{1,0},{2,3},{3,2},{4,5},{5,4},{6,7},{7,6},{8,9},{9,8},{10,11... | collective-permute-start | bytes 786440 | tf_op jit(solution)/shard_map/ppermute | solution.py:93
  23.3 4.4 %collective-permute-start.5 = (f32[2,72,128]{2,1,0:T(8,128)S(1)}, f32[2,72,128]{2,1,0:T(8,128)S(1)}, u32[]{:S(2)}, u32[]{:S(2)}) collective-permute-start(f32[2,72,128]{2,1,0:T(8,128)S(1)} %pad_maximum_fusion.3), channel_id=1, source_target_pairs={{0,8},{4,12},{8,0},{12,4},{16,24},{20,28},{24,16},{28,20},{1,9},{5... | collective-permute-start | bytes 221192 | tf_op jit(solution)/shard_map/ppermute | solution.py:93
  34.0 15.1 %collective-permute-start.9 = (f32[4,72,128]{2,1,0:T(8,128)S(1)}, f32[4,72,128]{2,1,0:T(8,128)S(1)}, u32[]{:S(2)}, u32[]{:S(2)}) collective-permute-start(f32[4,72,128]{2,1,0:T(8,128)S(1)} %pad_maximum_fusion.1.refs_8_.refs_12_), channel_id=1, source_target_pairs={{0,4},{4,0},{8,12},{12,8},{16,20},{20,16},{24,28},{28,24},{1,5},{5... | collective-permute-start | bytes 442376 | tf_op jit(solution)/shard_map/ppermute | solution.py:93
  34.4 1.9 %collective-permute-start.6 = (f32[8,128]{1,0:T(8,128)S(1)}, f32[8,128]{1,0:T(8,128)S(1)}, u32[]{:S(2)}, u32[]{:S(2)}) collective-permute-start(f32[8,128]{1,0:T(8,128)S(1)} %get-tuple-element.32.refs_4_), channel_id=1, source_target_pairs={{0,1},{1,0},{2,3},{3,2},{4,5},{5,4},{6,7},{7,6},{8,9},{9,8},{10,11... | collective-permute-start | bytes 12296 | tf_op jit(solution)/shard_map/ppermute | solution.py:93
  34.4 3.6 %collective-permute-start.7 = (f32[8,128]{1,0:T(8,128)S(1)}, f32[8,128]{1,0:T(8,128)S(1)}, u32[]{:S(2)}, u32[]{:S(2)}) collective-permute-start(f32[8,128]{1,0:T(8,128)S(1)} %get-tuple-element.32.refs_4_), channel_id=1, source_target_pairs={{0,2},{1,3},{2,0},{3,1},{4,6},{5,7},{6,4},{7,5},{8,10},{9,11},{10,... | collective-permute-start | bytes 12296 | tf_op jit(solution)/shard_map/ppermute | solution.py:93
  36.0 3.0 %collective-permute-start.8 = (f32[8,128]{1,0:T(8,128)S(1)}, f32[8,128]{1,0:T(8,128)S(1)}, u32[]{:S(2)}, u32[]{:S(2)}) collective-permute-start(f32[8,128]{1,0:T(8,128)S(1)} %get-tuple-element.32.refs_4_), channel_id=1, source_target_pairs={{0,3},{1,2},{2,1},{3,0},{4,7},{5,6},{6,5},{7,4},{8,11},{9,10},{10,... | collective-permute-start | bytes 12296 | tf_op jit(solution)/shard_map/ppermute | solution.py:93
  49.1 11.0 %collective-permute-start.13 = (f32[4,72,128]{2,1,0:T(8,128)S(1)}, f32[4,72,128]{2,1,0:T(8,128)S(1)}, u32[]{:S(2)}, u32[]{:S(2)}) collective-permute-start(f32[4,72,128]{2,1,0:T(8,128)S(1)} %collective-permute-done.9.refs_9_.refs_14_), channel_id=1, source_target_pairs={{0,1},{1,0},{2,3},{3,2},{4,5},{5,4},{6,7},{7,6},{8,9},{9,8},{10,11... | collective-permute-start | bytes 442376 | tf_op jit(solution)/shard_map/ppermute | solution.py:93
  49.4 25.9 %collective-permute-start.20 = (f32[4,72,128]{2,1,0:T(8,128)S(1)}, f32[4,72,128]{2,1,0:T(8,128)S(1)}, u32[]{:S(2)}, u32[]{:S(2)}) collective-permute-start(f32[4,72,128]{2,1,0:T(8,128)S(1)} %pad_maximum_fusion.1.refs_8_.refs_12_), channel_id=1, source_target_pairs={{0,1},{1,0},{2,3},{3,2},{4,5},{5,4},{6,7},{7,6},{8,9},{9,8},{10,11... | collective-permute-start | bytes 442376 | tf_op jit(solution)/shard_map/ppermute | solution.py:93
  49.7 1.9 %collective-permute-start.10 = (f32[8,128]{1,0:T(8,128)S(1)}, f32[8,128]{1,0:T(8,128)S(1)}, u32[]{:S(2)}, u32[]{:S(2)}) collective-permute-start(f32[8,128]{1,0:T(8,128)S(1)} %get-tuple-element.39.refs_4_), channel_id=1, source_target_pairs={{0,1},{1,0},{2,3},{3,2},{4,5},{5,4},{6,7},{7,6},{8,9},{9,8},{10,11... | collective-permute-start | bytes 12296 | tf_op jit(solution)/shard_map/ppermute | solution.py:93
  49.9 3.6 %collective-permute-start.11 = (f32[8,128]{1,0:T(8,128)S(1)}, f32[8,128]{1,0:T(8,128)S(1)}, u32[]{:S(2)}, u32[]{:S(2)}) collective-permute-start(f32[8,128]{1,0:T(8,128)S(1)} %get-tuple-element.39.refs_4_), channel_id=1, source_target_pairs={{0,2},{1,3},{2,0},{3,1},{4,6},{5,7},{6,4},{7,5},{8,10},{9,11},{10,... | collective-permute-start | bytes 12296 | tf_op jit(solution)/shard_map/ppermute | solution.py:93
  50.6 3.0 %collective-permute-start.12 = (f32[8,128]{1,0:T(8,128)S(1)}, f32[8,128]{1,0:T(8,128)S(1)}, u32[]{:S(2)}, u32[]{:S(2)}) collective-permute-start(f32[8,128]{1,0:T(8,128)S(1)} %get-tuple-element.39.refs_4_), channel_id=1, source_target_pairs={{0,3},{1,2},{2,1},{3,0},{4,7},{5,6},{6,5},{7,4},{8,11},{9,10},{10,... | collective-permute-start | bytes 12296 | tf_op jit(solution)/shard_map/ppermute | solution.py:93
  60.1 1.9 %collective-permute-start.14 = (f32[24,128]{1,0:T(8,128)S(1)}, f32[24,128]{1,0:T(8,128)S(1)}, u32[]{:S(2)}, u32[]{:S(2)}) collective-permute-start(f32[24,128]{1,0:T(8,128)S(1)} %sweep.1.refs_4_.refs_8_), channel_id=1, source_target_pairs={{0,1},{1,0},{2,3},{3,2},{4,5},{5,4},{6,7},{7,6},{8,9},{9,8},{10,11... | collective-permute-start | bytes 36872 | tf_op jit(solution)/shard_map/ppermute | solution.py:93
  60.3 3.7 %collective-permute-start.15 = (f32[24,128]{1,0:T(8,128)S(1)}, f32[24,128]{1,0:T(8,128)S(1)}, u32[]{:S(2)}, u32[]{:S(2)}) collective-permute-start(f32[24,128]{1,0:T(8,128)S(1)} %sweep.1.refs_4_.refs_8_), channel_id=1, source_target_pairs={{0,2},{1,3},{2,0},{3,1},{4,6},{5,7},{6,4},{7,5},{8,10},{9,11},{10,... | collective-permute-start | bytes 36872 | tf_op jit(solution)/shard_map/ppermute | solution.py:93
  61.7 3.1 %collective-permute-start.16 = (f32[24,128]{1,0:T(8,128)S(1)}, f32[24,128]{1,0:T(8,128)S(1)}, u32[]{:S(2)}, u32[]{:S(2)}) collective-permute-start(f32[24,128]{1,0:T(8,128)S(1)} %sweep.1.refs_4_.refs_8_), channel_id=1, source_target_pairs={{0,3},{1,2},{2,1},{3,0},{4,7},{5,6},{6,5},{7,4},{8,11},{9,10},{10,... | collective-permute-start | bytes 36872 | tf_op jit(solution)/shard_map/ppermute | solution.py:93
  73.4 1.9 %collective-permute-start.17 = (f32[8,128]{1,0:T(8,128)S(1)}, f32[8,128]{1,0:T(8,128)S(1)}, u32[]{:S(2)}, u32[]{:S(2)}) collective-permute-start(f32[8,128]{1,0:T(8,128)S(1)} %get-tuple-element.46.refs_4_), channel_id=1, source_target_pairs={{0,1},{1,0},{2,3},{3,2},{4,5},{5,4},{6,7},{7,6},{8,9},{9,8},{10,11... | collective-permute-start | bytes 12296 | tf_op jit(solution)/shard_map/ppermute | solution.py:93
  73.6 3.6 %collective-permute-start.18 = (f32[8,128]{1,0:T(8,128)S(1)}, f32[8,128]{1,0:T(8,128)S(1)}, u32[]{:S(2)}, u32[]{:S(2)}) collective-permute-start(f32[8,128]{1,0:T(8,128)S(1)} %get-tuple-element.46.refs_4_), channel_id=1, source_target_pairs={{0,2},{1,3},{2,0},{3,1},{4,6},{5,7},{6,4},{7,5},{8,10},{9,11},{10,... | collective-permute-start | bytes 12296 | tf_op jit(solution)/shard_map/ppermute | solution.py:93
  74.3 3.0 %collective-permute-start.19 = (f32[8,128]{1,0:T(8,128)S(1)}, f32[8,128]{1,0:T(8,128)S(1)}, u32[]{:S(2)}, u32[]{:S(2)}) collective-permute-start(f32[8,128]{1,0:T(8,128)S(1)} %get-tuple-element.46.refs_4_), channel_id=1, source_target_pairs={{0,3},{1,2},{2,1},{3,0},{4,7},{5,6},{6,5},{7,4},{8,11},{9,10},{10,... | collective-permute-start | bytes 12296 | tf_op jit(solution)/shard_map/ppermute | solution.py:93
  79.9 14.7 %collective-permute-start.21 = (f32[128,128]{1,0:T(8,128)S(1)}, f32[128,128]{1,0:T(8,128)S(1)}, u32[]{:S(2)}, u32[]{:S(2)}) collective-permute-start(f32[128,128]{1,0:T(8,128)S(1)} %shard_map.51), channel_id=1, source_target_pairs={{0,1},{1,0},{2,3},{3,2},{4,5},{5,4},{6,7},{7,6},{8,9},{9,8},{10,11... | collective-permute-start | bytes 196616 | tf_op jit(solution)/shard_map/ppermute | solution.py:93
  80.0 14.5 %collective-permute-start.22 = (f32[128,128]{1,0:T(8,128)S(1)}, f32[128,128]{1,0:T(8,128)S(1)}, u32[]{:S(2)}, u32[]{:S(2)}) collective-permute-start(f32[128,128]{1,0:T(8,128)S(1)} %shard_map.51), channel_id=1, source_target_pairs={{0,2},{1,3},{2,0},{3,1},{4,6},{5,7},{6,4},{7,5},{8,10},{9,11},{10,... | collective-permute-start | bytes 196616 | tf_op jit(solution)/shard_map/ppermute | solution.py:93
  81.4 13.2 %collective-permute-start.23 = (f32[128,128]{1,0:T(8,128)S(1)}, f32[128,128]{1,0:T(8,128)S(1)}, u32[]{:S(2)}, u32[]{:S(2)}) collective-permute-start(f32[128,128]{1,0:T(8,128)S(1)} %shard_map.51), channel_id=1, source_target_pairs={{0,3},{1,2},{2,1},{3,0},{4,7},{5,6},{6,5},{7,4},{8,11},{9,10},{10,... | collective-permute-start | bytes 196616 | tf_op jit(solution)/shard_map/ppermute | solution.py:93
